TPU v7x, 32 devices: a whole 2x2x4 slice. The times are simulated.
32 devices in a mesh: gx: 8 (over y, x, core), gy: 4 (over z).
Axes of the slice: x: 2, y: 2, z: 4, core: 2. Of those that a mesh axis runs over, the one named last changes fastest.
Arguments:
- pressure_now: float32 [64, 384, 768], P('gx', 'gy'), may hold values from -6 to 6
- pressure_prev: float32 [64, 384, 768], P('gx', 'gy'), may hold values from -6 to 6
- wave_speed: bfloat16 [64, 384, 768], P('gx', 'gy'), may hold values from 0.099609375 to 0.328125
- node_cell: int32 [8, 4, 2048], P('gx', 'gy'), may hold values from 0 to 589823, as said below
- node_material: int32 [8, 4, 2048], P('gx', 'gy'), may hold values from 0 to 7
- filter_state: float32 [8, 4, 2048], P('gx', 'gy'), may hold values from -6 to 6
- material_pole: float32 [8], replicated, may hold values from 0.3 to 0.95
- material_loss: float32 [8], replicated, may hold values from 0.1 to 0.6
- sphere_anchor: int32 [128, 3], replicated, may hold values from 0 to 720, as said below
Outputs:
- pressure: float32 [64, 384, 768], P('gx', 'gy')
- pressure_before: float32 [64, 384, 768], P('gx', 'gy')
- filter_out: float32 [8, 4, 2048], P('gx', 'gy')
- coefficients: float32 [128, 256], P('gy')
Inputs may be any that keep to these rules, and one draw needn't show every extreme that they name: `node_cell`: within one device the node cells are distinct, and none lies in the outermost layer of cells of the device's block along the first or the second dimension. `sphere_anchor`: sphere s lies in the block row s // 32 along the second dimension: its y start is that row's first cell plus a multiple of 48; its z start is a multiple of 48; its x start is at most 16; spheres are placed unevenly along x and may intersect.
All inputs are finite; a program needn't handle non-finite values.
Results may differ from a plain program's by a relative error of at most 0.0019.
Values may be sent and summed in bfloat16 or wider, within the bound.
No kernel may reach another device: no remote copies, remote signals or barrier semaphores. Data moves between devices by JAX's collectives and lax.ppermute only.
A program may use at most 192 MiB of HBM per device.

v0:
```python
import math

import jax
import jax.numpy as jnp
import numpy as np
from jax import lax
from jax.sharding import PartitionSpec as P

NS = 128
CUBE = 48
COEFS = 256
STEPS = 2


def padded_2(value, sides, width):
    for axis, dim in sides:
        count, length = (lax.axis_size(axis), value.shape[dim])
        up = [(i, (i + 1) % count) for i in range(count - 1)]
        down = [(j, i) for i, j in up]
        last = lax.slice_in_dim(value, length - width, length, axis=dim)
        initial = lax.slice_in_dim(value, 0, width, axis=dim)
        before = lax.ppermute(last, axis, up)
        after = lax.ppermute(initial, axis, down)
        value = jnp.concatenate([before, value, after], axis=dim)
    return value


def harmonic_table():
    half_side = CUBE / 2.0
    coords = (np.arange(CUBE) + 0.5 - half_side) / half_side
    x_pos, y_pos, z_pos = np.meshgrid(coords, coords, coords, indexing="ij")
    x_pos = x_pos.reshape(-1)
    y_pos = y_pos.reshape(-1)
    z_pos = z_pos.reshape(-1)
    radius_sq = x_pos * x_pos + y_pos * y_pos + z_pos * z_pos
    inside = np.where(radius_sq <= 1.0, 1.0, 0.0)
    degree_top = math.isqrt(COEFS) - 1
    zero_field = x_pos * 0.0
    real_part = {(0, 0): zero_field + 1.0}
    imag_part = {(0, 0): zero_field}
    for azimuth in range(1, degree_top + 1):
        last_real = real_part[azimuth - 1, azimuth - 1]
        last_imag = imag_part[azimuth - 1, azimuth - 1]
        real_part[azimuth, azimuth] = -(x_pos * last_real - y_pos * last_imag) / (2.0 * azimuth)
        imag_part[azimuth, azimuth] = -(x_pos * last_imag + y_pos * last_real) / (2.0 * azimuth)
    for azimuth in range(degree_top + 1):
        for degree in range(azimuth + 1, degree_top + 1):
            lower_real = real_part.get((degree - 2, azimuth), zero_field)
            lower_imag = imag_part.get((degree - 2, azimuth), zero_field)
            denom = float((degree - azimuth) * (degree + azimuth))
            real_part[degree, azimuth] = (
                (2 * degree - 1) * z_pos * real_part[degree - 1, azimuth] - radius_sq * lower_real
            ) / denom
            imag_part[degree, azimuth] = (
                (2 * degree - 1) * z_pos * imag_part[degree - 1, azimuth] - radius_sq * lower_imag
            ) / denom
    rows_list = []
    for degree in range(degree_top + 1):
        for azimuth in range(degree + 1):
            rows_list.append(real_part[degree, azimuth])
            if azimuth > 0:
                rows_list.append(imag_part[degree, azimuth])
    stacked = np.stack(rows_list) * inside[None, :]
    row_norms = np.sqrt(np.sum(stacked * stacked, axis=1, keepdims=True))
    return (stacked / row_norms).astype(np.float32)


def leapfrog(padded, previous, wave_speed):
    centre = padded[1:-1, 1:-1]
    along_z = jnp.pad(centre, ((0, 0), (0, 0), (1, 1)))
    beside = padded[2:, 1:-1] + padded[:-2, 1:-1]
    beside = beside + padded[1:-1, 2:] + padded[1:-1, :-2]
    beside = beside + along_z[:, :, 2:] + along_z[:, :, :-2]
    return 2.0 * centre - previous + wave_speed.astype(jnp.float32) * (beside - 6.0 * centre)


def relax_nodes(field, filter_now, node_index, pole_rate, loss_rate):
    flattened = field.reshape(-1)
    filter_next = pole_rate * filter_now + (1.0 - pole_rate) * flattened[node_index]
    flattened = flattened.at[node_index].add(-loss_rate * filter_next)
    return (flattened.reshape(field.shape), filter_next)


def assemble(planes, plane_pos, harmonics):
    select = (plane_pos[:, :, None] == jnp.arange(CUBE, dtype=jnp.int32)[None, None, :]).astype(
        jnp.bfloat16
    )
    cube_cells = jnp.einsum(
        "sap,saq->spq", select, planes, preferred_element_type=jnp.float32
    ).astype(jnp.bfloat16)
    flat_cube = cube_cells.reshape(cube_cells.shape[0], CUBE * CUBE * CUBE)
    return lax.dot_general(
        flat_cube, harmonics, (((1,), (1,)), ((), ())), preferred_element_type=jnp.float32
    )


def shards(
    pressure_now,
    pressure_prev,
    wave_speed,
    node_cell,
    node_material,
    filter_state,
    material_pole,
    material_loss,
    sphere_anchor,
):
    node_index = node_cell.reshape(-1)
    material_ids = jnp.arange(material_pole.shape[0], dtype=jnp.int32)
    matches = node_material.reshape(-1)[:, None] == material_ids[None, :]
    pole_rate = jnp.sum(jnp.where(matches, material_pole[None, :], 0.0), axis=1)
    loss_rate = jnp.sum(jnp.where(matches, material_loss[None, :], 0.0), axis=1)
    filter_now = filter_state.reshape(-1)
    current, previous = (pressure_now, pressure_prev)
    for step in range(STEPS):
        padded = padded_2(current, (("gx", 0), ("gy", 1)), 1)
        advanced = leapfrog(padded, previous, wave_speed)
        advanced, filter_now = relax_nodes(advanced, filter_now, node_index, pole_rate, loss_rate)
        previous, current = (current, advanced)
    probe_field = current.astype(jnp.bfloat16)
    harmonics = jnp.asarray(harmonic_table(), dtype=jnp.bfloat16)
    slab_width = current.shape[0]
    block_y = current.shape[1]
    per_row = NS // lax.axis_size("gy")
    slab_pos = lax.axis_index("gx")
    part_pos = lax.axis_index("gy")
    row_anchor = lax.dynamic_slice_in_dim(sphere_anchor, part_pos * per_row, per_row, 0)
    zero_start = jnp.zeros((), jnp.int32)

    def extract(anchor):
        window = lax.dynamic_slice(
            probe_field,
            (zero_start, anchor[1] - part_pos * block_y, anchor[2]),
            (slab_width, CUBE, CUBE),
        )
        return window.reshape(slab_width, CUBE * CUBE)

    planes = jax.vmap(extract)(row_anchor)
    local_x = jnp.arange(slab_width, dtype=jnp.int32)
    slab_count = lax.axis_size("gx")
    per_owner = max(1, per_row // slab_count)
    slots = slab_count * per_owner
    padded_planes = jnp.pad(planes, ((0, slots - per_row), (0, 0), (0, 0)))
    padded_anchor = jnp.pad(row_anchor, ((0, slots - per_row), (0, 0)))
    outgoing = padded_planes.reshape(per_owner, slab_count, slab_width, CUBE * CUBE)
    arrived = lax.all_to_all(outgoing, "gx", split_axis=1, concat_axis=1, tiled=True)
    owned = lax.dynamic_slice_in_dim(
        padded_anchor.reshape(per_owner, slab_count, 3), slab_pos, 1, 1
    )[:, 0, :]
    source_x = (
        jnp.arange(slab_count, dtype=jnp.int32)[:, None] * slab_width + local_x[None, :]
    ).reshape(-1)
    plane_pos = source_x[None, :] - owned[:, 0:1]
    received = arrived.reshape(per_owner, slab_count * slab_width, CUBE * CUBE)
    fitted = assemble(received, plane_pos, harmonics)
    collected = lax.all_gather(fitted[:, None, :], "gx", axis=1, tiled=True)
    coefficients = collected.reshape(slots, COEFS)[:per_row]
    return (current, previous, filter_now.reshape(filter_state.shape), coefficients)


def solution(mesh):
    placed = (
        P("gx", "gy", None),
        P("gx", "gy", None),
        P("gx", "gy", None),
        P("gx", "gy", None),
        P("gx", "gy", None),
        P("gx", "gy", None),
        P(),
        P(),
        P(),
    )
    return jax.shard_map(
        shards,
        mesh=mesh,
        in_specs=placed,
        out_specs=(P("gx", "gy", None), P("gx", "gy", None), P("gx", "gy", None), P("gy", None)),
        check_vma=False,
    )
```

profile of v0, /device:TPU:0, one launch (start us, length us, event | category | flops | bytes accessed | tf_op | source)
XLA Modules:
  0.0 285.7 jit_solution(12756143532954570234)
XLA Ops:
  3.7 3.0 %collective-permute-start.1 = (f32[1,96,768]{2,1,0:T(8,128)S(1)}, f32[1,96,768]{2,1,0:T(8,128)S(1)}, u32[]{:S(2)}, u32[]{:S(2)}) collective-permute-start(f32[1,96,768]{2,1,0:T(8,128)S(1)} %get-tuple-element.31), channel_id=1, source_target_pairs={{0,4},{4,8},{8,12},{12,16},{16,20},{20,24},{24,28},{1,5},{5,9},{9,... | collective-permute-start | bytes 884744 | tf_op jit(solution)/shard_map/ppermute | solution.py:22
  16.8 6.2 %collective-permute-start.3 = (f32[10,1,768]{2,1,0:T(1,128)}, f32[10,1,768]{2,1,0:T(1,128)}, u32[]{:S(2)}, u32[]{:S(2)}) collective-permute-start(f32[10,1,768]{2,1,0:T(1,128)} %get-tuple-element.27), channel_id=1, source_target_pairs={{0,1},{1,2},{2,3},{4,5},{5,6},{6,7},{8,9},{9,10},{10,11},{12,13},{... | collective-permute-start | bytes 92168 | tf_op jit(solution)/shard_map/ppermute | solution.py:22
  24.2 5.6 %fusion.7 = f32[8,96,768]{2,1,0:T(8,128)} fusion(f32[8,96,768]{2,1,0:T(8,128)S(1)} %copy-done.2, bf16[8,96,768]{2,1,0:T(8,128)(2,1)S(1)} %copy-done.4, f32[10,96,768]{2,1,0:T(8,128)} %copy-done.5, f32[10,1,768]{2,1,0:T(1,128)} %collective-permute-done.3, f32[10,1,768]{2,1,0:T(1,128)} %collective-permute-done.2, f32[1,96,768]{2,1,0:T(8,128)} %copy-done.7, ...), kind=kLoop, calls=%fused_computation.20 | loop fusion | flops 9437184 | bytes 11857920 | tf_op jit(solution)/shard_map/add | solution.py:74
  29.8 2.3 reshape.165
  32.1 20.6 %gather_fusion = f32[2048]{0:T(1024)} fusion(f32[589824]{0:T(1024)S(1)} %reshape.165, s32[2048]{0:T(1024)} %broadcast_clamp_fusion), kind=kCustom, calls=%fused_computation | custom fusion | bytes 24576 | tf_op jit(solution)/shard_map/gather | solution.py:79
  54.1 14.2 %scatter_fusion = f32[589824]{0:T(1024)S(1)} fusion(f32[589824]{0:T(1024)S(1)} %reshape.165, s32[2048]{0:T(1024)S(1)} %bitcast.33, f32[2048]{0:T(1024)} %negate_multiply_fusion), kind=kCustom, calls=%fused_computation.2 | custom fusion | flops 2048 | bytes 32768 | tf_op jit(solution)/shard_map/scatter-add | solution.py:80
  70.9 3.9 %collective-permute-start.5 = (f32[1,96,768]{2,1,0:T(8,128)}, f32[1,96,768]{2,1,0:T(8,128)}, u32[]{:S(2)}, u32[]{:S(2)}) collective-permute-start(f32[1,96,768]{2,1,0:T(8,128)} %slice.115), channel_id=1, source_target_pairs={{0,4},{4,8},{8,12},{12,16},{16,20},{20,24},{24,28},{1,5},{5,9},{9,... | collective-permute-start | bytes 884744 | tf_op jit(solution)/shard_map/ppermute | solution.py:22
  88.3 5.3 %collective-permute-start.7 = (f32[10,1,768]{2,1,0:T(1,128)}, f32[10,1,768]{2,1,0:T(1,128)}, u32[]{:S(2)}, u32[]{:S(2)}) collective-permute-start(f32[10,1,768]{2,1,0:T(1,128)} %get-tuple-element.25), channel_id=1, source_target_pairs={{0,1},{1,2},{2,3},{4,5},{5,6},{6,7},{8,9},{9,10},{10,11},{12,13},{... | collective-permute-start | bytes 92168 | tf_op jit(solution)/shard_map/ppermute | solution.py:22
  94.8 9.8 %fusion.8 = f32[8,96,768]{2,1,0:T(8,128)} fusion(f32[8,96,768]{2,1,0:T(8,128)} %reshape.168, bf16[8,96,768]{2,1,0:T(8,128)(2,1)S(1)} %copy-done.4, f32[10,96,768]{2,1,0:T(8,128)} %copy-done.6, f32[10,1,768]{2,1,0:T(1,128)} %collective-permute-done.7, f32[10,1,768]{2,1,0:T(1,128)} %collective-permute-done.6, f32[1,96,768]{2,1,0:T(8,128)} %collective-permute-done.5, ...), kind=kLoop, calls=%fused_computation.21 | loop fusion | flops 9437184 | bytes 11857920 | tf_op jit(solution)/shard_map/add | solution.py:74
  104.6 2.4 reshape.169
  107.0 11.8 %gather_fusion.1 = f32[2048]{0:T(1024)S(1)} fusion(f32[589824]{0:T(1024)S(1)} %reshape.169, s32[2048]{0:T(1024)S(1)} %copy-done.12), kind=kCustom, calls=%fused_computation.1 | custom fusion | bytes 24576 | tf_op jit(solution)/shard_map/gather | solution.py:79
  118.9 14.1 %scatter_fusion.1 = f32[589824]{0:T(1024)S(1)} fusion(f32[589824]{0:T(1024)S(1)} %reshape.169, s32[2048]{0:T(1024)S(1)} %bitcast.34, f32[2048]{0:T(1024)S(1)} %add_multiply_fusion), kind=kCustom, calls=%fused_computation.3 | custom fusion | flops 2048 | bytes 32768 | tf_op jit(solution)/shard_map/scatter-add | solution.py:80
  136.4 85.0 %while.1 = (s32[]{:T(128)}, bf16[8,96,768]{2,1,0:T(8,128)(2,1)S(1)}, s32[32,3]{0,1:T(4,128)S(1)}, bf16[32,8,48,48]{3,2,1,0:T(8,128)(2,1)}, s32[]{:T(128)}) while((s32[]{:T(128)}, bf16[8,96,768]{2,1,0:T(8,128)(2,1)S(1)}, s32[32,3]{0,1:T(4,128)S(1)}, bf16[32,8,48,48]{3,2,1,0:T(8,128)(2,1)}, s32[]{:T(128)}) %tuple.29), condition=%wide.while_cond, body=%wide.while_body.sunk | while | flops 2 | bytes 136309 | solution.py:131
  150.2 2.1 bitcast_dynamic-update-slice_fusion.2
  152.9 2.1 bitcast_dynamic-update-slice_fusion.2
  155.6 2.1 bitcast_dynamic-update-slice_fusion.2
  160.9 2.1 bitcast_dynamic-update-slice_fusion.2
  174.2 2.1 bitcast_dynamic-update-slice_fusion.2
  184.8 2.1 bitcast_dynamic-update-slice_fusion.2
  221.4 4.7 %reshape.172 = bf16[4,8,8,2304]{3,2,1,0:T(8,128)(2,1)S(1)} reshape(bf16[32,8,48,48]{3,2,1,0:T(8,128)(2,1)} %get-tuple-element.11) | data formatting | bytes 2359296 | tf_op jit(solution)/shard_map/reshape | solution.py:145
  227.2 9.7 %all-to-all-start = ((bf16[4,8,8,2304]{3,2,0,1:T(8,128)(2,1)}), bf16[4,8,8,2304]{3,2,0,1:T(8,128)(2,1)S(1)}, u32[]{:S(2)}, u32[]{:S(2)}) async-start(bf16[4,8,8,2304]{3,2,0,1:T(8,128)(2,1)} %copy.22), calls=%async_computation | async-start | bytes 2359296 | tf_op jit(solution)/shard_map/all_to_all | solution.py:146
  238.0 15.6 %all-to-all-done = bf16[4,8,8,2304]{3,2,0,1:T(8,128)(2,1)S(1)} async-done(((bf16[4,8,8,2304]{3,2,0,1:T(8,128)(2,1)}), bf16[4,8,8,2304]{3,2,0,1:T(8,128)(2,1)S(1)}, u32[]{:S(2)}, u32[]{:S(2)}) %all-to-all-start) | async-done | bytes 1179680 | tf_op jit(solution)/shard_map/all_to_all | solution.py:146
  254.5 21.8 %fusion.23 = f32[4,256]{1,0:T(4,128)S(1)} fusion(bf16[4,110592]{1,0:T(4,128)(2,1)S(1)} %bitcast.31, bf16[256,110592]{1,0:T(8,128)(2,1)} %constant.14.clone), kind=kOutput, calls=%fused_computation.69 | convolution fusion | flops 226492416 | bytes 57511936 | tf_op jit(solution)/shard_map/dot_general | solution.py:92
  276.4 8.7 %all-gather = f32[4,2048]{1,0:T(4,128)S(1)} all-gather(f32[4,256]{1,0:T(4,128)S(1)} %fusion.23), channel_id=2, replica_groups=mesh['gx'=8,'gy'=4] {'gx'}, dimensions={1}, use_global_device_ids=true | all-gather | bytes 36864 | tf_op jit(solution)/shard_map/all_gather | solution.py:156
  (174 shorter events, 112.5 us)
Async XLA Ops:
  0.6 22.4 %copy-start = (s32[128,3]{0,1:T(4,128)S(1)}, s32[128,3]{0,1:T(4,128)}, u32[]{:S(2)}) copy-start(s32[128,3]{0,1:T(4,128)} %param.18) | copy-start | bytes 4612
  2.5 9.8 %collective-permute-start = (f32[1,96,768]{2,1,0:T(8,128)}, f32[1,96,768]{2,1,0:T(8,128)}, u32[]{:S(2)}, u32[]{:S(2)}) collective-permute-start(f32[1,96,768]{2,1,0:T(8,128)} %get-tuple-element.30), channel_id=1, source_target_pairs={{4,0},{8,4},{12,8},{16,12},{20,16},{24,20},{28,24},{5,1},{9,5},{13... | collective-permute-start | bytes 884744 | tf_op jit(solution)/shard_map/ppermute | solution.py:23
  3.7 5.8 %collective-permute-start.1 = (f32[1,96,768]{2,1,0:T(8,128)S(1)}, f32[1,96,768]{2,1,0:T(8,128)S(1)}, u32[]{:S(2)}, u32[]{:S(2)}) collective-permute-start(f32[1,96,768]{2,1,0:T(8,128)S(1)} %get-tuple-element.31), channel_id=1, source_target_pairs={{0,4},{4,8},{8,12},{12,16},{16,20},{20,24},{24,28},{1,5},{5,9},{9,... | collective-permute-start | bytes 884744 | tf_op jit(solution)/shard_map/ppermute | solution.py:22
  10.3 13.9 %copy-start.2 = (f32[8,96,768]{2,1,0:T(8,128)S(1)}, f32[8,96,768]{2,1,0:T(8,128)}, u32[]{:S(2)}) copy-start(f32[8,96,768]{2,1,0:T(8,128)} %param.10) | copy-start | bytes 7077892
  10.3 13.9 %copy-start.4 = (bf16[8,96,768]{2,1,0:T(8,128)(2,1)S(1)}, bf16[8,96,768]{2,1,0:T(8,128)(2,1)}, u32[]{:S(2)}) copy-start(bf16[8,96,768]{2,1,0:T(8,128)(2,1)} %param.12) | copy-start | bytes 3538948
  15.5 7.5 %collective-permute-start.2 = (f32[10,1,768]{2,1,0:T(1,128)}, f32[10,1,768]{2,1,0:T(1,128)}, u32[]{:S(2)}, u32[]{:S(2)}) collective-permute-start(f32[10,1,768]{2,1,0:T(1,128)} %get-tuple-element.26), channel_id=1, source_target_pairs={{1,0},{2,1},{3,2},{5,4},{6,5},{7,6},{9,8},{10,9},{11,10},{13,12},{... | collective-permute-start | bytes 92168 | tf_op jit(solution)/shard_map/ppermute | solution.py:23
  16.8 7.3 %collective-permute-start.3 = (f32[10,1,768]{2,1,0:T(1,128)}, f32[10,1,768]{2,1,0:T(1,128)}, u32[]{:S(2)}, u32[]{:S(2)}) collective-permute-start(f32[10,1,768]{2,1,0:T(1,128)} %get-tuple-element.27), channel_id=1, source_target_pairs={{0,1},{1,2},{2,3},{4,5},{5,6},{6,7},{8,9},{9,10},{10,11},{12,13},{... | collective-permute-start | bytes 92168 | tf_op jit(solution)/shard_map/ppermute | solution.py:22
  23.1 51.7 %copy-start.14 = (s32[32,3]{0,1:T(4,128)}, s32[32,3]{0,1:T(4,128)S(1)}, u32[]{:S(2)}) copy-start(s32[32,3]{0,1:T(4,128)S(1)} %constant_dynamic-slice_fusion.2) | copy-start | bytes 1156
  70.9 9.8 %collective-permute-start.5 = (f32[1,96,768]{2,1,0:T(8,128)}, f32[1,96,768]{2,1,0:T(8,128)}, u32[]{:S(2)}, u32[]{:S(2)}) collective-permute-start(f32[1,96,768]{2,1,0:T(8,128)} %slice.115), channel_id=1, source_target_pairs={{0,4},{4,8},{8,12},{12,16},{16,20},{20,24},{24,28},{1,5},{5,9},{9,... | collective-permute-start | bytes 884744 | tf_op jit(solution)/shard_map/ppermute | solution.py:22
  77.1 6.6 %collective-permute-start.4 = (f32[1,96,768]{2,1,0:T(8,128)}, f32[1,96,768]{2,1,0:T(8,128)}, u32[]{:S(2)}, u32[]{:S(2)}) collective-permute-start(f32[1,96,768]{2,1,0:T(8,128)} %slice.112), channel_id=1, source_target_pairs={{4,0},{8,4},{12,8},{16,12},{20,16},{24,20},{28,24},{5,1},{9,5},{13... | collective-permute-start | bytes 884744 | tf_op jit(solution)/shard_map/ppermute | solution.py:23
  81.6 12.4 %copy-start.15 = (s32[32,3]{0,1:T(4,128)S(1)}, s32[32,3]{0,1:T(4,128)}, u32[]{:S(2)}) copy-start(s32[32,3]{0,1:T(4,128)} %copy-done.14) | copy-start | bytes 1156
  81.7 13.1 %copy-start.3 = (f32[8,96,768]{2,1,0:T(8,128)S(1)}, f32[8,96,768]{2,1,0:T(8,128)}, u32[]{:S(2)}) copy-start(f32[8,96,768]{2,1,0:T(8,128)} %param.10) | copy-start | bytes 7077892
  84.7 1.6 copy-start.6
  87.0 7.8 %collective-permute-start.6 = (f32[10,1,768]{2,1,0:T(1,128)}, f32[10,1,768]{2,1,0:T(1,128)}, u32[]{:S(2)}, u32[]{:S(2)}) collective-permute-start(f32[10,1,768]{2,1,0:T(1,128)} %get-tuple-element.24), channel_id=1, source_target_pairs={{1,0},{2,1},{3,2},{5,4},{6,5},{7,6},{9,8},{10,9},{11,10},{13,12},{... | collective-permute-start | bytes 92168 | tf_op jit(solution)/shard_map/ppermute | solution.py:23
  88.3 6.5 %collective-permute-start.7 = (f32[10,1,768]{2,1,0:T(1,128)}, f32[10,1,768]{2,1,0:T(1,128)}, u32[]{:S(2)}, u32[]{:S(2)}) collective-permute-start(f32[10,1,768]{2,1,0:T(1,128)} %get-tuple-element.25), channel_id=1, source_target_pairs={{0,1},{1,2},{2,3},{4,5},{5,6},{6,7},{8,9},{9,10},{10,11},{12,13},{... | collective-permute-start | bytes 92168 | tf_op jit(solution)/shard_map/ppermute | solution.py:22
  104.6 2.4 copy-start.12
  107.0 11.8 %copy-start.8 = (f32[2048]{0:T(1024)S(1)}, f32[2048]{0:T(1024)}, u32[]{:S(2)}) copy-start(f32[2048]{0:T(1024)} %get-tuple-element.12) | copy-start | bytes 24580
  107.0 11.8 %copy-start.9 = (f32[2048]{0:T(1024)S(1)}, f32[2048]{0:T(1024)}, u32[]{:S(2)}) copy-start(f32[2048]{0:T(1024)} %gather_fusion) | copy-start | bytes 24580
  107.0 11.8 %copy-start.10 = (f32[1,1,2048]{2,1,0:T(1,128)S(1)}, f32[1,1,2048]{2,1,0:T(1,128)}, u32[]{:S(2)}) copy-start(f32[1,1,2048]{2,1,0:T(1,128)} %param.15) | copy-start | bytes 24580
  107.0 11.8 %copy-start.11 = (f32[2048]{0:T(1024)S(1)}, f32[2048]{0:T(1024)}, u32[]{:S(2)}) copy-start(f32[2048]{0:T(1024)} %get-tuple-element.13) | copy-start | bytes 24580
  226.0 10.8 %copy-start.16 = (s32[8]{0:T(128)S(1)}, s32[8]{0:T(128)}, u32[]{:S(2)}) copy-start(s32[8]{0:T(128)} %iota_multiply_fusion) | copy-start | bytes 100
  226.0 11.0 %copy-start.13 = (s32[4,8,3]{1,0,2:T(4,128)S(1)}, s32[4,8,3]{1,0,2:T(4,128)}, u32[]{:S(2)}) copy-start(s32[4,8,3]{1,0,2:T(4,128)} %reshape.171) | copy-start | bytes 1156
  227.2 26.5 %all-to-all-start = ((bf16[4,8,8,2304]{3,2,0,1:T(8,128)(2,1)}), bf16[4,8,8,2304]{3,2,0,1:T(8,128)(2,1)S(1)}, u32[]{:S(2)}, u32[]{:S(2)}) async-start(bf16[4,8,8,2304]{3,2,0,1:T(8,128)(2,1)} %copy.22), calls=%async_computation | async-start | bytes 2359296 | tf_op jit(solution)/shard_map/all_to_all | solution.py:146
  254.5 31.1 %copy-start.1 = (s32[128,3]{0,1:T(4,128)S(1)}, s32[128,3]{0,1:T(4,128)}, u32[]{:S(2)}) copy-start(s32[128,3]{0,1:T(4,128)} %param.18) | copy-start | bytes 4612
  (2 other events, 2.3 us)
where the time goes:
time: 287 us; the launch traced here: 286 us
  local copies, waits for them, and re-layouts  152 us (53%)
  other arithmetic  52.1 us (18%)
  starting transfers between devices  33.2 us (12%)
  matrix products  22.2 us (8%)
  waiting for transfers between devices  16.8 us (6%)
  blocking collectives  8.66 us (3%)
    gather x96, local copies, waits for them, and re-layouts  84.9 us
    gather x2, local copies, waits for them, and re-layouts, relax_nodes(): flattened[node_index]  32.4 us
    scatter-add x2, other arithmetic, relax_nodes(): flattened = flattened.at[node_index].add(-loss_rate * filter_next)  28.3 us
    dot_general x1, matrix products, assemble(): lax.dot_general(flat_cube, harmonics, (((1,), (1,)), ((), ())), preferred...  21.8 us
    ppermute x4, starting transfers between devices, padded_2(): before = lax.ppermute(last, axis, up)  18.4 us
    all_to_all x1, waiting for transfers between devices, shards(): lax.all_to_all(outgoing, 'gx', split_axis=1, concat_axis=1, tiled=True)  15.6 us
    add x2, other arithmetic, leapfrog(): 2.0 * centre - previous  15.5 us
    all_to_all x1, starting transfers between devices, shards(): lax.all_to_all(outgoing, 'gx', split_axis=1, concat_axis=1, tiled=True)  9.68 us
  transfers between devices with their start and end apart: 9, of which 2 were waited for; matrix products, arithmetic and copies ran while one was open for 5% of the time, Pallas kernels for 0%

commit v1 on v0

v1 whole, which is shorter than its diff:
```python
import functools
import math

import jax
import jax.numpy as jnp
import ml_dtypes
import numpy as np
from jax import lax
from jax.experimental import pallas as pl
from jax.experimental.pallas import tpu as pltpu
from jax.sharding import PartitionSpec as P

CUBE = 48
COEFS = 256
DEGREES = 16
LANES = 128
GROUP = 128
F32 = jnp.float32
BF16 = jnp.bfloat16


def halves(table):
    high = table.astype(ml_dtypes.bfloat16)
    low = (table - high.astype(np.float64)).astype(ml_dtypes.bfloat16)
    return high, low


@functools.lru_cache(maxsize=None)
def tables():
    axis = (np.arange(CUBE) + 0.5 - CUBE / 2.0) / (CUBE / 2.0)
    u, v = np.meshgrid(axis, axis, indexing="ij")
    planar_index, planar = {}, []
    for degree in range(DEGREES):
        for m in range(degree % 2, degree + 1, 2):
            k = (degree - m) // 2
            value = (-(u + 1j * v)) ** m * (u * u + v * v) ** k
            for part in range(2 if m else 1):
                planar_index[m, k, part] = len(planar)
                planar.append(value.imag if part else value.real)
    planar = np.stack(planar)
    axial = np.stack([axis**q for q in range(DEGREES)])
    poly = {}
    for m in range(DEGREES):
        poly[m, m] = {0: 1.0}
        for n in range(m + 1, DEGREES):
            entry = {}
            for k, c in poly[n - 1, m].items():
                entry[k] = entry.get(k, 0.0) + (2 * n - 1) * c
            for k, c in poly.get((n - 2, m), {}).items():
                entry[k] = entry.get(k, 0.0) - c
                entry[k + 1] = entry.get(k + 1, 0.0) - c
            poly[n, m] = {k: c / ((n - m) * (n + m)) for k, c in entry.items()}
    mix = np.zeros((DEGREES, len(planar), COEFS))
    row = 0
    for n in range(DEGREES):
        for m in range(n + 1):
            for part in range(2 if m else 1):
                for k, c in poly[n, m].items():
                    mix[n - m - 2 * k, planar_index[m, k, part], row] = c
                row += 1
    ball = (
        axis[:, None, None] ** 2 + axis[None, :, None] ** 2 + axis[None, None, :] ** 2
    ) <= 1.0
    along = np.einsum("qbr,ql->rbl", mix, axial)
    norms = np.zeros(COEFS)
    for i in range(CUBE):
        plane = np.einsum("rbl,bj->rjl", along, planar[:, i])
        norms += np.sum(np.where(ball[i], plane, 0.0) ** 2, axis=(1, 2))
    mix /= np.sqrt(norms)
    return planar, axial, mix


def plane_pairs(slab):
    planar, _, _ = tables()
    count = planar.shape[0]
    starts = range(-slab, CUBE + slab)
    out = np.zeros((2 * count, len(starts), LANES), ml_dtypes.bfloat16)
    high, low = halves(planar)
    for at, a in enumerate(starts):
        for side in range(2):
            if 0 <= a + side < CUBE:
                lanes = slice(side * CUBE, (side + 1) * CUBE)
                out[:count, at, lanes] = high[:, a + side]
                out[count:, at, lanes] = low[:, a + side]
    return out.reshape(2 * count, len(starts) * LANES)


def axial_windows(nz):
    _, axial, _ = tables()
    high, low = halves(axial)
    out = np.zeros((nz // CUBE, 2 * DEGREES, 2 * LANES), ml_dtypes.bfloat16)
    for tile in range(nz // CUBE):
        offset = tile * CUBE - window_start(tile * CUBE, nz)
        out[tile, :DEGREES, offset : offset + CUBE] = high
        out[tile, DEGREES:, offset : offset + CUBE] = low
    return out


def window_start(z, nz):
    if isinstance(z, int):
        return min(z // LANES * LANES, nz - 2 * LANES)
    return jnp.minimum(lax.shift_right_logical(z, 7) * LANES, nz - 2 * LANES)


def mix_table():
    _, _, mix = tables()
    count = mix.shape[1]
    high, low = halves(mix)
    out = np.zeros((DEGREES, 2 * count, COEFS), ml_dtypes.bfloat16)
    out[:, :count], out[:, count:] = high, low
    return out


def dot(a, b):
    return jnp.dot(a, b, preferred_element_type=F32)


def split(value):
    high = value.astype(BF16)
    return high, (value - high.astype(F32)).astype(BF16)


def iota(shape, axis):
    return lax.broadcasted_iota(jnp.int32, shape, axis)


def lookup(index, scalars, first):
    out = jnp.zeros(index.shape, F32)
    for at in range(scalars.shape[0]):
        out = jnp.where(index == at + first, scalars[at], out)
    return out


def columns(row):
    eye = iota((GROUP, GROUP), 0) == iota((GROUP, GROUP), 1)
    ones = jnp.ones((GROUP, GROUP), BF16)
    spread = jnp.where(eye, row, 0.0)
    out, rest = None, spread
    for _ in range(3):
        part = rest.astype(BF16)
        rest = rest - part.astype(F32)
        term = dot(part, ones)
        out = term if out is None else out + term
    return out


def columns_small(row):
    eye = iota((GROUP, GROUP), 0) == iota((GROUP, GROUP), 1)
    return dot(jnp.where(eye, row, 0.0).astype(BF16), jnp.ones((GROUP, GROUP), BF16))


def stencil(field, previous, speed, kinds, states, pole_ref, loss_ref, out, shift):
    slab, rows, nz = previous.shape
    groups, chunks = nz // LANES, rows // 8
    lane, sub = iota((8, LANES), 1), iota((8, LANES), 0)
    first_lane, last_lane = lane == 0, lane == LANES - 1
    first_sub, last_sub = sub == 0, sub == 7
    pole = jnp.zeros((8, LANES), F32)
    gain = jnp.zeros((8, LANES), F32)
    for at in range(pole_ref.shape[0]):
        pole = jnp.where(lane == at + 1, pole_ref[at], pole)
        gain = jnp.where(lane == at + 1, loss_ref[at] * (1.0 - pole_ref[at]), gain)

    def tile(ref, x, j, g):
        return ref[x, 8 * j : 8 * j + 8, LANES * g : LANES * (g + 1)]

    def body(x, carry):
        centre = {}
        for j in range(chunks):
            for g in range(groups):
                centre[j, g] = tile(field, x + 1, j, g)
        for j in range(chunks):
            for g in range(groups):
                here = centre[j, g]
                left = pltpu.roll(here, 1, 1)
                left = jnp.where(
                    first_lane, pltpu.roll(centre[j, g - 1], 1, 1) if g else 0.0, left
                )
                right = pltpu.roll(here, LANES - 1, 1)
                right = jnp.where(
                    last_lane,
                    pltpu.roll(centre[j, g + 1], LANES - 1, 1) if g + 1 < groups else 0.0,
                    right,
                )
                up = pltpu.roll(here, 1, 0)
                up = jnp.where(first_sub, pltpu.roll(centre[j - 1, g], 1, 0) if j else 0.0, up)
                down = pltpu.roll(here, 7, 0)
                down = jnp.where(
                    last_sub, pltpu.roll(centre[j + 1, g], 7, 0) if j + 1 < chunks else 0.0, down
                )
                beside = tile(field, x, j, g) + tile(field, x + 2, j, g)
                beside = beside + up + down + left + right
                value = 2.0 * here - tile(previous, x, j, g)
                value = value + tile(speed, x, j, g).astype(F32) * (beside - 6.0 * here)
                at = pl.ds((x * rows + 8 * j) * groups + g, 8, stride=groups)
                kind = kinds[at, :].astype(jnp.int32)
                state = jnp.take_along_axis(pole, kind, axis=1) * states[at, :]
                state = state + jnp.take_along_axis(gain, kind, axis=1) * value
                states[at, :] = state
                out[x + shift, 8 * j : 8 * j + 8, LANES * g : LANES * (g + 1)] = value - state
        return carry

    lax.fori_loop(0, slab, body, 0)


def first_step(
    cell_ref, pole_ref, loss_ref, now, prev, speed, cells, material, state,
    out, kinds, states, field, lanes, kind_cols, state_cols,
):
    slab, rows, nz = prev.shape
    nodes = cells.shape[1]
    field[0] = jnp.zeros((rows, nz), F32)
    field[slab + 1] = jnp.zeros((rows, nz), F32)
    for x in range(slab):
        field[x + 1] = now[x]
    kinds[...] = jnp.zeros_like(kinds)
    states[...] = jnp.zeros_like(states)
    scaled = lookup(material[...], loss_ref, 0) * state[...]
    kind_row = (material[...] + 1).astype(F32)
    lane_row = (cells[...] & (LANES - 1)).astype(F32)
    for at in range(nodes // GROUP):
        part = slice(at * GROUP, (at + 1) * GROUP)
        lanes[part, :] = columns_small(lane_row[:, part])
        kind_cols[part, :] = columns_small(kind_row[:, part])
        state_cols[part, :] = columns(scaled[:, part])
    lane = iota((1, LANES), 1).astype(F32)

    def place(k, carry):
        row = pl.ds(lax.shift_right_logical(cell_ref[0, k], 7), 1)
        source = pl.ds(k, 1)
        mask = lanes[source, :] == lane
        pltpu.store(kinds.at[row, :], kind_cols[source, :], mask=mask)
        pltpu.store(states.at[row, :], state_cols[source, :], mask=mask)
        return carry

    lax.fori_loop(0, nodes, place, 0, unroll=8)
    stencil(field, prev, speed, kinds, states, pole_ref, loss_ref, out, 0)


def add_rows(value, speed, low, high):
    rows = value.shape[0]
    row = iota(value.shape, 0)
    term = jnp.where(row == 0, low, jnp.where(row == rows - 1, high, 0.0))
    return value + speed * term


def send_planes(first, last, top, bottom, c_first, c_last, c_top, c_bottom,
                x_low, x_high, y_low, y_high, sx_low, sx_high, sy_low, sy_high):
    slab = top.shape[0]
    for at, value, speed, halo, out in (
        (0, first, c_first, x_low, sx_low),
        (slab - 1, last, c_last, x_high, sx_high),
    ):
        c = speed[0].astype(F32)
        plane = value[0] + c * halo[...].astype(F32)
        low = y_low[at : at + 1, :].astype(F32)
        high = y_high[at : at + 1, :].astype(F32)
        out[...] = add_rows(plane, c, low, high).astype(BF16)
    for value, speed, halo, out, r, xr in (
        (top, c_top, y_low, sy_low, 0, 0),
        (bottom, c_bottom, y_high, sy_high, top.shape[1] - 1, x_low.shape[0] - 1),
    ):
        rows = []
        for x in range(slab):
            c = speed[x, r : r + 1, :].astype(F32)
            line = value[x, r : r + 1, :] + c * halo[x : x + 1, :].astype(F32)
            if x == 0:
                line = line + c * x_low[xr : xr + 1, :].astype(F32)
            if x == slab - 1:
                line = line + c * x_high[xr : xr + 1, :].astype(F32)
            rows.append(line)
        out[...] = jnp.concatenate(rows, axis=0).astype(BF16)


def fix_halo(field, speed, x_low, x_high, y_low, y_high, shift):
    slab, rows, _ = speed.shape
    for x in range(slab):
        at = x + shift
        if x == 0:
            field[at] = field[at] + speed[x].astype(F32) * x_low[...].astype(F32)
        if x == slab - 1:
            field[at] = field[at] + speed[x].astype(F32) * x_high[...].astype(F32)
        c = speed[x, 0:1, :].astype(F32)
        field[at, 0:1, :] = field[at, 0:1, :] + c * y_low[x : x + 1, :].astype(F32)
        c = speed[x, rows - 1 : rows, :].astype(F32)
        last = slice(rows - 1, rows)
        field[at, last, :] = field[at, last, :] + c * y_high[x : x + 1, :].astype(F32)


def second_step(
    cell_ref, pole_ref, loss_ref, now, prev, speed, kinds, states_in, cells, material,
    x_low, x_high, y_low, y_high, before, out, filter_out, field, states, picked,
):
    slab, rows, nz = prev.shape
    nodes = cells.shape[1]
    field[0] = jnp.zeros((rows, nz), F32)
    field[slab + 1] = jnp.zeros((rows, nz), F32)
    for x in range(slab):
        field[x + 1] = now[x]
    states[...] = states_in[...]
    fix_halo(field, speed, x_low, x_high, y_low, y_high, 1)
    for x in range(slab):
        before[x] = field[x + 1]
    stencil(field, prev, speed, kinds, states, pole_ref, loss_ref, out, 0)

    def pick(k, carry):
        row = lax.shift_right_logical(cell_ref[0, k], 7)
        picked[pl.ds(k, 1), :] = states[pl.ds(row, 1), :]
        return carry

    lax.fori_loop(0, nodes, pick, 0, unroll=8)
    lane_row = (cells[...] & (LANES - 1)).astype(F32)
    inverse = 1.0 / lookup(material[...], loss_ref, 0)
    lane = iota((GROUP, LANES), 1).astype(F32)
    for at in range(nodes // GROUP):
        part = slice(at * GROUP, (at + 1) * GROUP)
        chosen = jnp.where(columns_small(lane_row[:, part]) == lane, picked[part, :], 0.0)
        line = lax.dot_general(
            jnp.ones((8, LANES), F32), chosen, (((1,), (1,)), ((), ())),
            precision=lax.Precision.HIGHEST, preferred_element_type=F32,
        )
        filter_out[:, part] = line[0:1, :] * inverse[:, part]


def fit(anchor_ref, place_ref, pressure_in, speed, x_low, x_high, y_low, y_high,
        pairs, axial, mix, pressure, partial, *products):
    slab, rows, nz = speed.shape
    spheres = partial.shape[0]
    count = pairs.shape[0] // 2
    x_first, y_first, s_first = place_ref[0], place_ref[1], place_ref[2]
    for x in range(slab):
        pressure[x] = pressure_in[x]
    fix_halo(pressure, speed, x_low, x_high, y_low, y_high, 0)
    limit = CUBE * CUBE
    odd_y = 2 * iota((CUBE, 2 * LANES), 0) - (CUBE - 1)
    y_square = odd_y * odd_y
    lane = iota((CUBE, 2 * LANES), 1)
    products[1][...] = jnp.zeros_like(products[1])

    def sphere(s, carry):
        base = 3 * (s_first + s)
        x0 = anchor_ref[base]
        y0 = pl.multiple_of(anchor_ref[base + 1] - y_first, CUBE)
        z0 = anchor_ref[base + 2]
        start = pl.multiple_of(window_start(z0, nz), LANES)
        odd_z = 2 * (lane - (z0 - start)) - (CUBE - 1)
        square = y_square + odd_z * odd_z
        a0 = x_first - x0
        planes = []
        for i in range(slab):
            odd_x = 2 * (a0 + i) - (CUBE - 1)
            cells = pressure[i, pl.ds(y0, CUBE), pl.ds(start, 2 * LANES)]
            planes.append(jnp.where(square <= limit - odd_x * odd_x, cells, 0.0).astype(BF16))
        blank = jnp.zeros((LANES - 2 * CUBE, 2 * LANES), BF16)
        total = None
        first = jnp.clip(a0, -slab, CUBE) + slab
        left, right = [], []
        for i in range(0, slab, 2):
            at = pl.multiple_of(jnp.minimum(first + i, CUBE + 2 * slab - 1) * LANES, LANES)
            left.append(pairs[:, pl.ds(at, LANES)])
            right += [planes[i], planes[i + 1], blank]
        total = dot(jnp.concatenate(left, axis=1), jnp.concatenate(right, axis=0))
        high, low = split(total[:count] + total[count:])
        tile = lax.shift_right_logical(z0 * 1366, 16)
        factor = axial[tile]
        contract = (((1,), (1,)), ((), ()))
        one = lax.dot_general(factor, high, contract, preferred_element_type=F32)
        two = lax.dot_general(factor[:DEGREES], low, contract, preferred_element_type=F32)
        moment = one[:DEGREES] + one[DEGREES:] + two
        at = pl.ds(pl.multiple_of(s * DEGREES, DEGREES), DEGREES)
        products[0][at, :] = moment[:, :LANES]
        products[1][at, 0 : count - LANES] = moment[:, LANES:]
        return carry

    lax.fori_loop(0, spheres, sphere, 0, unroll=2)
    result = jnp.zeros((spheres, COEFS), F32)
    for q in range(DEGREES):
        at = pl.ds(q, spheres, stride=DEGREES)
        moment = jnp.concatenate([products[0][at, :], products[1][at, :]], axis=1)
        high, low = split(moment[:, :count])
        upper, lower = mix[q, :count], mix[q, count:]
        result = result + (dot(high, upper) + (dot(low, upper) + dot(high, lower)))
    partial[...] = result


def whole(memory=pltpu.VMEM):
    return pl.BlockSpec(memory_space=memory)


def shards(now, prev, speed, node_cell, node_material, filter_state, pole, loss, anchors):
    slab, rows, nz = now.shape
    nodes = node_cell.shape[-1]
    slabs, parts = lax.axis_size("gx"), lax.axis_size("gy")
    gx, gy = lax.axis_index("gx"), lax.axis_index("gy")
    spheres = anchors.shape[0] // parts
    cells = node_cell.reshape(1, nodes)
    material = node_material.reshape(1, nodes)
    state = filter_state.reshape(1, nodes)
    dense = jax.ShapeDtypeStruct((slab * rows * nz // LANES, LANES), F32)
    block = jax.ShapeDtypeStruct((slab, rows, nz), F32)
    params = pltpu.CompilerParams(vmem_limit_bytes=56 << 20)

    def up(count):
        return [(i, i + 1) for i in range(count - 1)]

    def down(count):
        return [(i + 1, i) for i in range(count - 1)]

    def exchange(x_first, x_last, y_first, y_last):
        return (
            lax.ppermute(x_last, "gx", up(slabs)),
            lax.ppermute(x_first, "gx", down(slabs)),
            lax.ppermute(y_last, "gy", up(parts)),
            lax.ppermute(y_first, "gy", down(parts)),
        )

    halo = exchange(
        now[0].astype(BF16), now[-1].astype(BF16),
        now[:, 0, :].astype(BF16), now[:, -1, :].astype(BF16),
    )
    half, kinds, states = pl.pallas_call(
        first_step,
        out_shape=(block, dense, dense),
        in_specs=[whole(pltpu.SMEM)] * 3 + [whole()] * 6,
        out_specs=(whole(),) * 3,
        scratch_shapes=[pltpu.VMEM((slab + 2, rows, nz), F32)]
        + [pltpu.VMEM((nodes, LANES), F32)] * 3,
        compiler_params=params,
        name="first_step",
    )(cells, pole, loss, now, prev, speed, cells, material, state)

    def plane_at(x):
        return pl.BlockSpec((1, rows, nz), lambda i: (x, 0, 0))

    def rows_at(y, height):
        return pl.BlockSpec((slab, height, nz), lambda i: (0, y // height, 0))

    edges = [plane_at(0), plane_at(slab - 1), rows_at(0, 16), rows_at(rows - 16, 16)]
    sent = pl.pallas_call(
        send_planes,
        grid=(1,),
        out_shape=(jax.ShapeDtypeStruct((rows, nz), BF16),) * 2
        + (jax.ShapeDtypeStruct((slab, nz), BF16),) * 2,
        in_specs=edges + edges + [whole()] * 4,
        out_specs=(whole(),) * 4,
        compiler_params=params,
        name="send_planes",
    )(half, half, half, half, speed, speed, speed, speed, *halo)
    halo_next = exchange(*sent)
    before, partly, filter_out = pl.pallas_call(
        second_step,
        out_shape=(block, block, jax.ShapeDtypeStruct((1, nodes), F32)),
        in_specs=[whole(pltpu.SMEM)] * 3 + [whole()] * 11,
        out_specs=(whole(),) * 3,
        scratch_shapes=[
            pltpu.VMEM((slab + 2, rows, nz), F32),
            pltpu.VMEM(dense.shape, F32),
            pltpu.VMEM((nodes, LANES), F32),
        ],
        compiler_params=params,
        name="second_step",
    )(cells, pole, loss, half, now, speed, kinds, states, cells, material, *halo)
    place = jnp.stack([gx * slab, gy * rows, gy * spheres]).astype(jnp.int32)
    pressure, partial = pl.pallas_call(
        fit,
        out_shape=(block, jax.ShapeDtypeStruct((spheres, COEFS), F32)),
        in_specs=[whole(pltpu.SMEM)] * 2 + [whole()] * 9,
        out_specs=(whole(),) * 2,
        scratch_shapes=[pltpu.VMEM((spheres * DEGREES, LANES), F32)] * 2,
        compiler_params=params,
        name="fit",
    )(
        anchors.reshape(-1), place, partly, speed, *halo_next,
        jnp.asarray(plane_pairs(slab)), jnp.asarray(axial_windows(nz)), jnp.asarray(mix_table()),
    )
    coefficients = jnp.sum(lax.all_gather(partial, "gx", axis=0, tiled=False), axis=0)
    return pressure, before, filter_out.reshape(filter_state.shape), coefficients


def solution(mesh):
    grid = P("gx", "gy", None)
    return jax.shard_map(
        shards,
        mesh=mesh,
        in_specs=(grid,) * 6 + (P(), P(), P()),
        out_specs=(grid, grid, grid, P("gy", None)),
        check_vma=False,
    )
```

time: 287 us -> 95.8 us (0.33)
  local copies, waits for them, and re-layouts: 152 us -> 5.63 us
  Pallas kernels: 0 us -> 53.1 us
  other arithmetic: 52.1 us -> 1.3 us
  matrix products: 22.2 us -> 0 us
  waiting for transfers between devices: 16.8 us -> 0.02 us
  starting transfers between devices: 33.2 us -> 20.1 us
  blocking collectives: 8.66 us -> 14.1 us
    gather x98 -> x0, local copies, waits for them, and re-layouts: 117 us -> none
    pallas_call x0 -> x4, Pallas kernels: none -> 53.1 us  [the longest x1 18.5 us: shards(): pl.pallas_call(fit, out_shape=(block, jax.ShapeDtypeStruct((spheres, COEF...]
    scatter-add x2 -> x0, other arithmetic: 28.3 us -> none  [relax_nodes(): flattened = flattened.at[node_index].add(-loss_rate * filter_next)]
    dot_general x2 -> x0, matrix products: 22.2 us -> none  [the longest x1 21.8 us: assemble(): lax.dot_general(flat_cube, harmonics, (((1,), (1,)), ((), ())), preferred...]
    add x4 -> x0, other arithmetic: 16.2 us -> none  [the longest x2 15.5 us: leapfrog(): 2.0 * centre - previous]
    all_to_all x1 -> x0, waiting for transfers between devices: 15.6 us -> none  [shards(): lax.all_to_all(outgoing, 'gx', split_axis=1, concat_axis=1, tiled=True)]
    reshape x8 -> x1, local copies, waits for them, and re-layouts: 15.1 us -> 0.8 us  [shards(): anchors.reshape(-1)]
    all_to_all x1 -> x0, starting transfers between devices: 9.68 us -> none  [shards(): lax.all_to_all(outgoing, 'gx', split_axis=1, concat_axis=1, tiled=True)]
  transfers between devices with their start and end apart: 9 -> 8, of which waited for: 2 -> 0; matrix products, arithmetic and copies ran while one was open for 5% -> 2% of each run, Pallas kernels for 0% -> 34%
where the time goes in v1:
time: 95.8 us; the launch traced here: 95.2 us
  Pallas kernels  53.1 us (55%)
  starting transfers between devices  20.1 us (21%)
  blocking collectives  14.1 us (15%)
  local copies, waits for them, and re-layouts  5.63 us (6%)
  other arithmetic  1.3 us (1%)
    pallas_call x1, Pallas kernels, shards(): pl.pallas_call(fit, out_shape=(block, jax.ShapeDtypeStruct((spheres, COEF...  18.5 us
    pallas_call x1, Pallas kernels, shards(): pl.pallas_call(second_step, out_shape=(block, block, jax.ShapeDtypeStruct...  16.8 us
    pallas_call x1, Pallas kernels, shards(): pl.pallas_call(first_step, out_shape=(block, dense, dense), in_specs=[who...  15.4 us
    all_gather x1, blocking collectives, shards(): lax.all_gather(partial, 'gx', axis=0, tiled=False)  14.1 us
    ppermute x2, starting transfers between devices, exchange(): lax.ppermute(y_last, 'gy', up(parts))  8.57 us
    ppermute x2, starting transfers between devices, exchange(): lax.ppermute(x_last, 'gx', up(slabs))  6.39 us
    unnamed x22, local copies, waits for them, and re-layouts  4.44 us
    ppermute x2, starting transfers between devices, exchange(): lax.ppermute(x_first, 'gx', down(slabs))  2.58 us
  transfers between devices with their start and end apart: 8, of which 0 were waited for; matrix products, arithmetic and copies ran while one was open for 2% of the time, Pallas kernels for 34%

profile of v1, /device:TPU:0, one launch (start us, length us, event | category | flops | bytes accessed | tf_op | source)
XLA Modules:
  0.0 95.2 jit_solution(15415011472995968433)
XLA Ops:
  0.6 2.9 %copy.24 = bf16[8,96,768]{2,0,1:T(8,128)(2,1)S(1)} copy(f32[8,96,768]{2,1,0:T(8,128)} %prev.3) | data formatting | bytes 3538944 | tf_op args[0]
  3.6 0.4 fusion
  4.0 2.4 %collective-permute-start = (bf16[96,768]{1,0:T(8,128)(2,1)S(1)}, bf16[96,768]{1,0:T(8,128)(2,1)S(1)}, u32[]{:S(2)}, u32[]{:S(2)}) collective-permute-start(bf16[96,768]{1,0:T(8,128)(2,1)S(1)} %bitcast.19), channel_id=1, source_target_pairs={{0,4},{4,8},{8,12},{12,16},{16,20},{20,24},{24,28},{1,5},{5,9},{9,... | collective-permute-start | bytes 442376 | tf_op jit(solution)/shard_map/ppermute | solution.py:411
  6.4 1.3 %collective-permute-start.1 = (bf16[96,768]{1,0:T(8,128)(2,1)S(1)}, bf16[96,768]{1,0:T(8,128)(2,1)S(1)}, u32[]{:S(2)}, u32[]{:S(2)}) collective-permute-start(bf16[96,768]{1,0:T(8,128)(2,1)S(1)} %bitcast.20), channel_id=1, source_target_pairs={{4,0},{8,4},{12,8},{16,12},{20,16},{24,20},{28,24},{5,1},{9,5},{13... | collective-permute-start | bytes 442376 | tf_op jit(solution)/shard_map/ppermute | solution.py:412
  7.7 4.3 %collective-permute-start.2 = (bf16[8,768]{1,0:T(8,128)(2,1)S(1)}, bf16[8,768]{1,0:T(8,128)(2,1)S(1)}, u32[]{:S(2)}, u32[]{:S(2)}) collective-permute-start(bf16[8,768]{1,0:T(8,128)(2,1)S(1)} %get-tuple-element.29), channel_id=1, source_target_pairs={{0,1},{1,2},{2,3},{4,5},{5,6},{6,7},{8,9},{9,10},{10,11},{12,13},{... | collective-permute-start | bytes 36872 | tf_op jit(solution)/shard_map/ppermute | solution.py:413
  12.0 1.3 %collective-permute-start.3 = (bf16[8,768]{1,0:T(8,128)(2,1)S(1)}, bf16[8,768]{1,0:T(8,128)(2,1)S(1)}, u32[]{:S(2)}, u32[]{:S(2)}) collective-permute-start(bf16[8,768]{1,0:T(8,128)(2,1)S(1)} %get-tuple-element.28), channel_id=1, source_target_pairs={{1,0},{2,1},{3,2},{5,4},{6,5},{7,6},{9,8},{10,9},{11,10},{13,12},{... | collective-permute-start | bytes 36872 | tf_op jit(solution)/shard_map/ppermute | solution.py:414
  13.3 15.4 %first_step.1 = (f32[8,96,768]{2,1,0:T(8,128)}, f32[4608,128]{1,0:T(8,128)}, f32[4608,128]{1,0:T(8,128)}) custom-call(s32[1,2048]{1,0:T(1,128)} %bitcast.21, f32[8]{0:T(128)} %pole_ref.3, f32[8]{0:T(128)} %loss_ref.3, f32[8,96,768]{2,1,0:T(8,128)} %prev.3, f32[8,96,768]{2,1,0:T(8,128)} %prev.2, bf16[8,96,768]{2,1,0:T(8,128)(2,1)} %speed.5, ...), custom_call_target="tpu_custom_call" | custom-call | tf_op jit(solution)/shard_map/first_step/pallas_call | solution.py:421
  28.8 0.5 copy-done.4
  29.3 0.1 copy-done
  29.5 2.4 %send_planes.1 = (bf16[96,768]{1,0:T(8,128)(2,1)}, bf16[96,768]{1,0:T(8,128)(2,1)}, bf16[8,768]{1,0:T(8,128)(2,1)}, bf16[8,768]{1,0:T(8,128)(2,1)}) custom-call(f32[8,96,768]{2,1,0:T(8,128)} %get-tuple-element.16.now.first.last.top.bottom, f32[8,96,768]{2,1,0:T(8,128)} %get-tuple-element.16.now.first.last.top.bottom, ...), custom_call_target="tpu_custom_call" | custom-call | tf_op jit(solution)/shard_map/send_planes/pallas_call | solution.py:439
  31.9 4.0 %collective-permute-start.4 = (bf16[96,768]{1,0:T(8,128)(2,1)}, bf16[96,768]{1,0:T(8,128)(2,1)S(1)}, u32[]{:S(2)}, u32[]{:S(2)}) collective-permute-start(bf16[96,768]{1,0:T(8,128)(2,1)} %get-tuple-element.20), channel_id=1, source_target_pairs={{0,4},{4,8},{8,12},{12,16},{16,20},{20,24},{24,28},{1,5},{5,9},{9,... | collective-permute-start | bytes 442376 | tf_op jit(solution)/shard_map/ppermute | solution.py:411
  35.9 1.3 %collective-permute-start.5 = (bf16[96,768]{1,0:T(8,128)(2,1)}, bf16[96,768]{1,0:T(8,128)(2,1)S(1)}, u32[]{:S(2)}, u32[]{:S(2)}) collective-permute-start(bf16[96,768]{1,0:T(8,128)(2,1)} %get-tuple-element.21), channel_id=1, source_target_pairs={{4,0},{8,4},{12,8},{16,12},{20,16},{24,20},{28,24},{5,1},{9,5},{13... | collective-permute-start | bytes 442376 | tf_op jit(solution)/shard_map/ppermute | solution.py:412
  37.2 4.3 %collective-permute-start.6 = (bf16[8,768]{1,0:T(8,128)(2,1)}, bf16[8,768]{1,0:T(8,128)(2,1)S(1)}, u32[]{:S(2)}, u32[]{:S(2)}) collective-permute-start(bf16[8,768]{1,0:T(8,128)(2,1)} %get-tuple-element.22), channel_id=1, source_target_pairs={{0,1},{1,2},{2,3},{4,5},{5,6},{6,7},{8,9},{9,10},{10,11},{12,13},{... | collective-permute-start | bytes 36872 | tf_op jit(solution)/shard_map/ppermute | solution.py:413
  41.5 1.3 %collective-permute-start.7 = (bf16[8,768]{1,0:T(8,128)(2,1)}, bf16[8,768]{1,0:T(8,128)(2,1)S(1)}, u32[]{:S(2)}, u32[]{:S(2)}) collective-permute-start(bf16[8,768]{1,0:T(8,128)(2,1)} %get-tuple-element.23), channel_id=1, source_target_pairs={{1,0},{2,1},{3,2},{5,4},{6,5},{7,6},{9,8},{10,9},{11,10},{13,12},{... | collective-permute-start | bytes 36872 | tf_op jit(solution)/shard_map/ppermute | solution.py:414
  42.8 0.7 pad_add_fusion.place_ref
  43.5 0.1 copy.17
  43.6 0.8 reshape.27.anchor_ref
  44.4 16.8 %second_step.1 = (f32[8,96,768]{2,1,0:T(8,128)}, f32[8,96,768]{2,1,0:T(8,128)}, f32[1,2048]{1,0:T(1,128)}) custom-call(s32[1,2048]{1,0:T(1,128)} %bitcast.23, f32[8]{0:T(128)} %pole_ref.3, f32[8]{0:T(128)} %loss_ref.3, f32[8,96,768]{2,1,0:T(8,128)} %get-tuple-element.16.now.first.last.top.bottom, f32[8,96,768]{2,1,0:T(8,128)} %prev.3, ...), custom_call_target="tpu_custom_call" | custom-call | tf_op jit(solution)/shard_map/second_step/pallas_call | solution.py:450
  61.3 0.5 copy-done.6
  61.8 0.1 copy-done.2
  61.9 0.1 copy-done.3
  61.9 18.5 %fit.1 = (f32[8,96,768]{2,1,0:T(8,128)}, f32[32,256]{1,0:T(8,128)}) custom-call(s32[384]{0:T(512)} %reshape.27.anchor_ref, s32[3]{0:T(128)} %pad_add_fusion.place_ref, f32[8,96,768]{2,1,0:T(8,128)} %get-tuple-element.19.pressure_in, bf16[8,96,768]{2,1,0:T(8,128)(2,1)} %speed.5, bf16[96,768]{1,0:T(8,128)(2,1)} %copy-done.2, bf16[96,768]{1,0:T(8,128)(2,1)} %copy-done.3, ...), custom_call_target="tpu_custom_call" | custom-call | tf_op jit(solution)/shard_map/fit/pallas_call | solution.py:464
  80.4 14.1 %all-gather = f32[256,256]{1,0:T(8,128)S(1)} all-gather(f32[32,256]{1,0:T(8,128)} %get-tuple-element.27), channel_id=2, replica_groups=mesh['gx'=8,'gy'=4] {'gx'}, dimensions={0}, use_global_device_ids=true | all-gather | bytes 294912 | tf_op jit(solution)/shard_map/all_gather | solution.py:476
  94.5 0.6 reduce_sum.9
  (24 shorter events, 0.2 us)
Async XLA Ops:
  4.0 24.8 %collective-permute-start = (bf16[96,768]{1,0:T(8,128)(2,1)S(1)}, bf16[96,768]{1,0:T(8,128)(2,1)S(1)}, u32[]{:S(2)}, u32[]{:S(2)}) collective-permute-start(bf16[96,768]{1,0:T(8,128)(2,1)S(1)} %bitcast.19), channel_id=1, source_target_pairs={{0,4},{4,8},{8,12},{12,16},{16,20},{20,24},{24,28},{1,5},{5,9},{9,... | collective-permute-start | bytes 442376 | tf_op jit(solution)/shard_map/ppermute | solution.py:411
  6.4 22.4 %collective-permute-start.1 = (bf16[96,768]{1,0:T(8,128)(2,1)S(1)}, bf16[96,768]{1,0:T(8,128)(2,1)S(1)}, u32[]{:S(2)}, u32[]{:S(2)}) collective-permute-start(bf16[96,768]{1,0:T(8,128)(2,1)S(1)} %bitcast.20), channel_id=1, source_target_pairs={{4,0},{8,4},{12,8},{16,12},{20,16},{24,20},{28,24},{5,1},{9,5},{13... | collective-permute-start | bytes 442376 | tf_op jit(solution)/shard_map/ppermute | solution.py:412
  7.7 21.0 %collective-permute-start.2 = (bf16[8,768]{1,0:T(8,128)(2,1)S(1)}, bf16[8,768]{1,0:T(8,128)(2,1)S(1)}, u32[]{:S(2)}, u32[]{:S(2)}) collective-permute-start(bf16[8,768]{1,0:T(8,128)(2,1)S(1)} %get-tuple-element.29), channel_id=1, source_target_pairs={{0,1},{1,2},{2,3},{4,5},{5,6},{6,7},{8,9},{9,10},{10,11},{12,13},{... | collective-permute-start | bytes 36872 | tf_op jit(solution)/shard_map/ppermute | solution.py:413
  12.0 16.7 %collective-permute-start.3 = (bf16[8,768]{1,0:T(8,128)(2,1)S(1)}, bf16[8,768]{1,0:T(8,128)(2,1)S(1)}, u32[]{:S(2)}, u32[]{:S(2)}) collective-permute-start(bf16[8,768]{1,0:T(8,128)(2,1)S(1)} %get-tuple-element.28), channel_id=1, source_target_pairs={{1,0},{2,1},{3,2},{5,4},{6,5},{7,6},{9,8},{10,9},{11,10},{13,12},{... | collective-permute-start | bytes 36872 | tf_op jit(solution)/shard_map/ppermute | solution.py:414
  28.7 0.6 copy-start.4
  28.7 0.6 copy-start.5
  28.8 0.6 copy-start
  28.8 0.7 copy-start.1
  29.5 14.0 %copy-start.8 = (s32[128,3]{0,1:T(4,128)S(1)}, s32[128,3]{0,1:T(4,128)}, u32[]{:S(2)}) copy-start(s32[128,3]{0,1:T(4,128)} %param.20) | copy-start | bytes 4612
  31.9 29.3 %collective-permute-start.4 = (bf16[96,768]{1,0:T(8,128)(2,1)}, bf16[96,768]{1,0:T(8,128)(2,1)S(1)}, u32[]{:S(2)}, u32[]{:S(2)}) collective-permute-start(bf16[96,768]{1,0:T(8,128)(2,1)} %get-tuple-element.20), channel_id=1, source_target_pairs={{0,4},{4,8},{8,12},{12,16},{16,20},{20,24},{24,28},{1,5},{5,9},{9,... | collective-permute-start | bytes 442376 | tf_op jit(solution)/shard_map/ppermute | solution.py:411
  35.9 25.3 %collective-permute-start.5 = (bf16[96,768]{1,0:T(8,128)(2,1)}, bf16[96,768]{1,0:T(8,128)(2,1)S(1)}, u32[]{:S(2)}, u32[]{:S(2)}) collective-permute-start(bf16[96,768]{1,0:T(8,128)(2,1)} %get-tuple-element.21), channel_id=1, source_target_pairs={{4,0},{8,4},{12,8},{16,12},{20,16},{24,20},{28,24},{5,1},{9,5},{13... | collective-permute-start | bytes 442376 | tf_op jit(solution)/shard_map/ppermute | solution.py:412
  37.2 24.0 %collective-permute-start.6 = (bf16[8,768]{1,0:T(8,128)(2,1)}, bf16[8,768]{1,0:T(8,128)(2,1)S(1)}, u32[]{:S(2)}, u32[]{:S(2)}) collective-permute-start(bf16[8,768]{1,0:T(8,128)(2,1)} %get-tuple-element.22), channel_id=1, source_target_pairs={{0,1},{1,2},{2,3},{4,5},{5,6},{6,7},{8,9},{9,10},{10,11},{12,13},{... | collective-permute-start | bytes 36872 | tf_op jit(solution)/shard_map/ppermute | solution.py:413
  41.5 19.7 %collective-permute-start.7 = (bf16[8,768]{1,0:T(8,128)(2,1)}, bf16[8,768]{1,0:T(8,128)(2,1)S(1)}, u32[]{:S(2)}, u32[]{:S(2)}) collective-permute-start(bf16[8,768]{1,0:T(8,128)(2,1)} %get-tuple-element.23), channel_id=1, source_target_pairs={{1,0},{2,1},{3,2},{5,4},{6,5},{7,6},{9,8},{10,9},{11,10},{13,12},{... | collective-permute-start | bytes 36872 | tf_op jit(solution)/shard_map/ppermute | solution.py:414
  61.2 0.6 copy-start.6
  61.2 0.6 copy-start.7
  61.2 0.7 copy-start.2
  61.2 0.7 copy-start.3

commit v2 on v1

v2 whole, which is shorter than its diff:
```python
import functools
import math

import jax
import jax.numpy as jnp
import ml_dtypes
import numpy as np
from jax import lax
from jax.experimental import pallas as pl
from jax.experimental.pallas import tpu as pltpu
from jax.sharding import PartitionSpec as P

CUBE = 48
COEFS = 256
DEGREES = 16
LANES = 128
GROUP = 128
F32 = jnp.float32
BF16 = jnp.bfloat16


def halves(table):
    high = table.astype(ml_dtypes.bfloat16)
    low = (table - high.astype(np.float64)).astype(ml_dtypes.bfloat16)
    return high, low


@functools.lru_cache(maxsize=None)
def tables():
    axis = (np.arange(CUBE) + 0.5 - CUBE / 2.0) / (CUBE / 2.0)
    u, v = np.meshgrid(axis, axis, indexing="ij")
    planar_index, planar = {}, []
    for degree in range(DEGREES):
        for m in range(degree % 2, degree + 1, 2):
            k = (degree - m) // 2
            value = (-(u + 1j * v)) ** m * (u * u + v * v) ** k
            for part in range(2 if m else 1):
                planar_index[m, k, part] = len(planar)
                planar.append(value.imag if part else value.real)
    planar = np.stack(planar)
    axial = np.stack([axis**q for q in range(DEGREES)])
    poly = {}
    for m in range(DEGREES):
        poly[m, m] = {0: 1.0}
        for n in range(m + 1, DEGREES):
            entry = {}
            for k, c in poly[n - 1, m].items():
                entry[k] = entry.get(k, 0.0) + (2 * n - 1) * c
            for k, c in poly.get((n - 2, m), {}).items():
                entry[k] = entry.get(k, 0.0) - c
                entry[k + 1] = entry.get(k + 1, 0.0) - c
            poly[n, m] = {k: c / ((n - m) * (n + m)) for k, c in entry.items()}
    mix = np.zeros((DEGREES, len(planar), COEFS))
    row = 0
    for n in range(DEGREES):
        for m in range(n + 1):
            for part in range(2 if m else 1):
                for k, c in poly[n, m].items():
                    mix[n - m - 2 * k, planar_index[m, k, part], row] = c
                row += 1
    ball = (
        axis[:, None, None] ** 2 + axis[None, :, None] ** 2 + axis[None, None, :] ** 2
    ) <= 1.0
    along = np.einsum("qbr,ql->rbl", mix, axial)
    norms = np.zeros(COEFS)
    for i in range(CUBE):
        plane = np.einsum("rbl,bj->rjl", along, planar[:, i])
        norms += np.sum(np.where(ball[i], plane, 0.0) ** 2, axis=(1, 2))
    mix /= np.sqrt(norms)
    return planar, axial, mix


def plane_pairs(slab):
    planar, _, _ = tables()
    count = planar.shape[0]
    starts = range(-slab, CUBE + slab)
    out = np.zeros((2 * count, len(starts), LANES), ml_dtypes.bfloat16)
    high, low = halves(planar)
    for at, a in enumerate(starts):
        for side in range(2):
            if 0 <= a + side < CUBE:
                lanes = slice(side * CUBE, (side + 1) * CUBE)
                out[:count, at, lanes] = high[:, a + side]
                out[count:, at, lanes] = low[:, a + side]
    return out.reshape(2 * count, len(starts) * LANES)


def axial_windows(nz):
    _, axial, _ = tables()
    high, low = halves(axial)
    out = np.zeros((nz // CUBE, 2 * DEGREES, 2 * LANES), ml_dtypes.bfloat16)
    for tile in range(nz // CUBE):
        offset = tile * CUBE - window_start(tile * CUBE, nz)
        out[tile, :DEGREES, offset : offset + CUBE] = high
        out[tile, DEGREES:, offset : offset + CUBE] = low
    return out


def window_start(z, nz):
    if isinstance(z, int):
        return min(z // LANES * LANES, nz - 2 * LANES)
    return jnp.minimum(lax.shift_right_logical(z, 7) * LANES, nz - 2 * LANES)


def mix_rows(q):
    sizes = [-(-(DEGREES - at) * (DEGREES + 1 - at) // 2 // 16) * 16 for at in range(DEGREES)]
    return sum(sizes[:q]), sizes[q]


def mix_table():
    _, _, mix = tables()
    high, low = halves(mix)
    first, size = mix_rows(DEGREES - 1)
    out = np.zeros((2, first + size, COEFS), ml_dtypes.bfloat16)
    for q in range(DEGREES):
        first, size = mix_rows(q)
        size = min(size, mix.shape[1])
        out[0, first : first + size] = high[q, :size]
        out[1, first : first + size] = low[q, :size]
    return out


def dot(a, b):
    return jnp.dot(a, b, preferred_element_type=F32)


def split(value):
    high = value.astype(BF16)
    return high, (value - high.astype(F32)).astype(BF16)


def iota(shape, axis):
    return lax.broadcasted_iota(jnp.int32, shape, axis)


def lookup(index, scalars, first):
    out = jnp.zeros(index.shape, F32)
    for at in range(scalars.shape[0]):
        out = jnp.where(index == at + first, scalars[at], out)
    return out


def columns(row):
    eye = iota((GROUP, GROUP), 0) == iota((GROUP, GROUP), 1)
    ones = jnp.ones((GROUP, GROUP), BF16)
    spread = jnp.where(eye, row, 0.0)
    out, rest = None, spread
    for _ in range(3):
        part = rest.astype(BF16)
        rest = rest - part.astype(F32)
        term = dot(part, ones)
        out = term if out is None else out + term
    return out


def columns_small(row):
    eye = iota((GROUP, GROUP), 0) == iota((GROUP, GROUP), 1)
    return dot(jnp.where(eye, row, 0.0).astype(BF16), jnp.ones((GROUP, GROUP), BF16))


def node_maps(
    cell_ref, loss_ref, cells, material, state, kinds, states, lanes, kind_cols, state_cols
):
    nodes = cells.shape[1]
    scaled = lookup(material[...], loss_ref, 0) * state[...]
    kind_row = (material[...] + 1).astype(F32)
    lane_row = (cells[...] & (LANES - 1)).astype(F32)
    for at in range(nodes // GROUP):
        part = slice(at * GROUP, (at + 1) * GROUP)
        lanes[part, :] = columns_small(lane_row[:, part])
        kind_cols[part, :] = columns_small(kind_row[:, part])
        state_cols[part, :] = columns(scaled[:, part])
    kinds[...] = jnp.zeros_like(kinds)
    states[...] = jnp.zeros_like(states)
    lane = iota((1, LANES), 1).astype(F32)

    def place(k, carry):
        row = pl.ds(lax.shift_right_logical(cell_ref[0, k], 7), 1)
        source = pl.ds(k, 1)
        mask = lanes[source, :] == lane
        pltpu.store(kinds.at[row, :], kind_cols[source, :], mask=mask)
        pltpu.store(states.at[row, :], state_cols[source, :], mask=mask)
        return carry

    lax.fori_loop(0, nodes, place, 0, unroll=32)


def stencil(pole_ref, loss_ref, below, here_ref, above, previous, speed, kinds, states, out,
            states_out):
    _, rows, nz = previous.shape
    groups, chunks = nz // LANES, rows // 8
    x, last = pl.program_id(0), pl.num_programs(0) - 1
    lane, sub = iota((8, LANES), 1), iota((8, LANES), 0)
    first_lane, last_lane = lane == 0, lane == LANES - 1
    first_sub, last_sub = sub == 0, sub == 7
    pole = jnp.zeros((8, LANES), F32)
    gain = jnp.zeros((8, LANES), F32)
    for at in range(pole_ref.shape[0]):
        pole = jnp.where(lane == at + 1, pole_ref[at], pole)
        gain = jnp.where(lane == at + 1, loss_ref[at] * (1.0 - pole_ref[at]), gain)
    has_below = jnp.where(x > 0, 1.0, 0.0)
    has_above = jnp.where(x < last, 1.0, 0.0)

    def tile(ref, j, g):
        return ref[0, 8 * j : 8 * j + 8, LANES * g : LANES * (g + 1)]

    for j in range(chunks):
        for g in range(groups):
            here = tile(here_ref, j, g)
            left = pltpu.roll(here, 1, 1)
            left = jnp.where(
                first_lane, pltpu.roll(tile(here_ref, j, g - 1), 1, 1) if g else 0.0, left
            )
            right = pltpu.roll(here, LANES - 1, 1)
            right = jnp.where(
                last_lane,
                pltpu.roll(tile(here_ref, j, g + 1), LANES - 1, 1) if g + 1 < groups else 0.0,
                right,
            )
            up = pltpu.roll(here, 1, 0)
            up = jnp.where(first_sub, pltpu.roll(tile(here_ref, j - 1, g), 1, 0) if j else 0.0, up)
            down = pltpu.roll(here, 7, 0)
            down = jnp.where(
                last_sub,
                pltpu.roll(tile(here_ref, j + 1, g), 7, 0) if j + 1 < chunks else 0.0,
                down,
            )
            beside = has_below * tile(below, j, g) + has_above * tile(above, j, g)
            beside = beside + up + down + left + right
            value = 2.0 * here - tile(previous, j, g)
            value = value + tile(speed, j, g).astype(F32) * (beside - 6.0 * here)
            at = pl.ds(8 * j * groups + g, 8, stride=groups)
            kind = kinds[at, :].astype(jnp.int32)
            state = jnp.take_along_axis(pole, kind, axis=1) * states[at, :]
            state = state + jnp.take_along_axis(gain, kind, axis=1) * value
            states_out[at, :] = state
            out[0, 8 * j : 8 * j + 8, LANES * g : LANES * (g + 1)] = value - state


def flags():
    out = []
    for axis in ("gx", "gy"):
        at = lax.axis_index(axis)
        out.append(jnp.where(at > 0, 1.0, 0.0))
        out.append(jnp.where(at < lax.axis_size(axis) - 1, 1.0, 0.0))
    return out


def edges(first, last, top, bottom, sx_low, sx_high, sy_low, sy_high):
    sx_low[...] = first[0].astype(BF16)
    sx_high[...] = last[0].astype(BF16)
    for x in range(top.shape[0]):
        sy_low[x : x + 1, :] = top[x, 0:1, :].astype(BF16)
        sy_high[x : x + 1, :] = bottom[x, bottom.shape[1] - 1 :, :].astype(BF16)


def fix_planes(first, last, top, bottom, c_first, c_last, c_top, c_bottom, halo):
    x_low, x_high, y_low, y_high = halo
    has = flags()
    slab, rows = top.shape[0], first.shape[1]
    final = top.shape[1] - 1
    for at, value, speed, ref, flag in (
        (0, first, c_first, x_low, has[0]),
        (slab - 1, last, c_last, x_high, has[1]),
    ):
        value[0] = value[0] + speed[0].astype(F32) * (flag * ref[...].astype(F32))
        for row, beside, there in ((0, y_low, has[2]), (rows - 1, y_high, has[3])):
            one = slice(row, row + 1)
            term = speed[0, one, :].astype(F32) * (there * beside[at : at + 1, :].astype(F32))
            value[0, one, :] = value[0, one, :] + term
    for x in range(slab):
        if x in (0, slab - 1):
            plane = first if x == 0 else last
            top[x] = plane[0, : final + 1, :]
            bottom[x] = plane[0, rows - final - 1 :, :]
            continue
        c = c_top[x, 0:1, :].astype(F32)
        top[x, 0:1, :] = top[x, 0:1, :] + c * (has[2] * y_low[x : x + 1, :].astype(F32))
        c = c_bottom[x, 15:16, :].astype(F32)
        term = c * (has[3] * y_high[x : x + 1, :].astype(F32))
        bottom[x, final : final + 1, :] = bottom[x, final : final + 1, :] + term


def fix_and_send(field_in, c_first, c_last, c_top, c_bottom, x_low, x_high, y_low, y_high,
                 field, sx_low, sx_high, sy_low, sy_high, first, last, top, bottom, sems):
    slab, rows = top.shape[0], first.shape[1]
    places = (
        (pl.ds(0, 1), pl.ds(0, rows), first),
        (pl.ds(slab - 1, 1), pl.ds(0, rows), last),
        (pl.ds(0, slab), pl.ds(0, 8), top),
        (pl.ds(0, slab), pl.ds(rows - 8, 8), bottom),
    )
    copies = [
        pltpu.make_async_copy(field_in.at[x, y], ref, sems.at[at])
        for at, (x, y, ref) in enumerate(places)
    ]
    for copy in copies:
        copy.start()
    for copy in copies:
        copy.wait()
    fix_planes(first, last, top, bottom, c_first, c_last, c_top, c_bottom,
               (x_low, x_high, y_low, y_high))
    copies = [
        pltpu.make_async_copy(ref, field.at[x, y], sems.at[at])
        for at, (x, y, ref) in enumerate(places[:2])
    ]
    inner = pl.ds(1, slab - 2)
    copies += [
        pltpu.make_async_copy(ref.at[inner], field.at[inner, y], sems.at[at + 2])
        for at, (_, y, ref) in enumerate(places[2:])
    ]
    for copy in copies:
        copy.start()
    edges(first, last, top, bottom, sx_low, sx_high, sy_low, sy_high)
    for copy in copies:
        copy.wait()


def gather_nodes(cell_ref, loss_ref, states, cells, material, filter_out, picked):
    nodes = cells.shape[1]

    def pick(k, carry):
        row = lax.shift_right_logical(cell_ref[0, k], 7)
        picked[pl.ds(k, 1), :] = states[pl.ds(row, 1), :]
        return carry

    lax.fori_loop(0, nodes, pick, 0, unroll=32)
    lane_row = (cells[...] & (LANES - 1)).astype(F32)
    inverse = 1.0 / lookup(material[...], loss_ref, 0)
    lane = iota((GROUP, LANES), 1).astype(F32)
    for at in range(nodes // GROUP):
        part = slice(at * GROUP, (at + 1) * GROUP)
        chosen = jnp.where(columns_small(lane_row[:, part]) == lane, picked[part, :], 0.0)
        line = lax.dot_general(
            jnp.ones((8, LANES), F32), chosen, (((1,), (1,)), ((), ())),
            precision=lax.Precision.HIGHEST, preferred_element_type=F32,
        )
        filter_out[:, part] = line[0:1, :] * inverse[:, part]


def fit(anchor_ref, pressure_in, c_first, c_last, c_top, c_bottom, x_low, x_high, y_low, y_high,
        pairs, axial, mix, pressure, partial, *products):
    slab, rows, nz = pressure.shape
    spheres = partial.shape[0]
    count = pairs.shape[0] // 2
    x_first = lax.axis_index("gx") * slab
    y_first = lax.axis_index("gy") * rows
    s_first = lax.axis_index("gy") * spheres
    for x in range(slab):
        pressure[x] = pressure_in[x]
    has = flags()
    for at, speed, ref, flag in ((0, c_first, x_low, has[0]), (slab - 1, c_last, x_high, has[1])):
        term = speed[0].astype(F32) * (flag * ref[...].astype(F32))
        pressure[at] = pressure[at] + term
    for x in range(slab):
        for row, speed, r, ref, flag in (
            (0, c_top, 0, y_low, has[2]),
            (rows - 1, c_bottom, 15, y_high, has[3]),
        ):
            one = slice(row, row + 1)
            term = speed[x, r : r + 1, :].astype(F32) * (flag * ref[x : x + 1, :].astype(F32))
            pressure[x, one, :] = pressure[x, one, :] + term
    limit = CUBE * CUBE
    odd_y = 2 * iota((CUBE, 2 * LANES), 0) - (CUBE - 1)
    y_square = odd_y * odd_y
    lane = iota((CUBE, 2 * LANES), 1)
    products[1][...] = jnp.zeros_like(products[1])

    def sphere(s, carry):
        base = s_first + s
        x0 = anchor_ref[base, 0]
        y0 = pl.multiple_of(anchor_ref[base, 1] - y_first, CUBE)
        z0 = anchor_ref[base, 2]
        start = pl.multiple_of(window_start(z0, nz), LANES)
        odd_z = 2 * (lane - (z0 - start)) - (CUBE - 1)
        square = y_square + odd_z * odd_z
        a0 = x_first - x0
        planes = []
        for i in range(slab):
            odd_x = 2 * (a0 + i) - (CUBE - 1)
            cells = pressure[i, pl.ds(y0, CUBE), pl.ds(start, 2 * LANES)]
            planes.append(jnp.where(square <= limit - odd_x * odd_x, cells, 0.0).astype(BF16))
        blank = jnp.zeros((LANES - 2 * CUBE, 2 * LANES), BF16)
        total = None
        first = jnp.clip(a0, -slab, CUBE) + slab
        left, right = [], []
        for i in range(0, slab, 2):
            at = pl.multiple_of(jnp.minimum(first + i, CUBE + 2 * slab - 1) * LANES, LANES)
            left.append(pairs[:, pl.ds(at, LANES)])
            right += [planes[i], planes[i + 1], blank]
        total = dot(jnp.concatenate(left, axis=1), jnp.concatenate(right, axis=0))
        high, low = split(total[:count] + total[count:])
        tile = lax.shift_right_logical(z0 * 1366, 16)
        factor = axial[tile]
        contract = (((1,), (1,)), ((), ()))
        one = lax.dot_general(factor, high, contract, preferred_element_type=F32)
        two = lax.dot_general(factor[:DEGREES], low, contract, preferred_element_type=F32)
        moment = one[:DEGREES] + one[DEGREES:] + two
        at = pl.ds(pl.multiple_of(s * DEGREES, DEGREES), DEGREES)
        products[0][at, :] = moment[:, :LANES]
        products[1][at, 0 : count - LANES] = moment[:, LANES:]
        return carry

    lax.fori_loop(0, spheres, sphere, 0, unroll=4)
    result = jnp.zeros((spheres, COEFS), F32)
    for q in range(DEGREES):
        at = pl.ds(q, spheres, stride=DEGREES)
        moment = jnp.concatenate([products[0][at, :], products[1][at, :]], axis=1)
        first, size = mix_rows(q)
        high, low = split(moment[:, :size])
        upper, lower = mix[0, first : first + size], mix[1, first : first + size]
        result = result + (dot(high, upper) + (dot(low, upper) + dot(high, lower)))
    partial[...] = result


def whole(memory=pltpu.VMEM):
    return pl.BlockSpec(memory_space=memory)


def after(value, *others):
    return lax.optimization_barrier((value, *others))


def shards(now, prev, speed, node_cell, node_material, filter_state, pole, loss, anchors):
    slab, rows, nz = now.shape
    nodes = node_cell.shape[-1]
    spheres = anchors.shape[0] // lax.axis_size("gy")
    per_plane = rows * nz // LANES
    cells = node_cell.reshape(1, nodes)
    material = node_material.reshape(1, nodes)
    state = filter_state.reshape(1, nodes)
    dense = jax.ShapeDtypeStruct((slab * per_plane, LANES), F32)
    block = jax.ShapeDtypeStruct((slab, rows, nz), F32)
    sends = (jax.ShapeDtypeStruct((rows, nz), BF16),) * 2
    sends += (jax.ShapeDtypeStruct((slab, nz), BF16),) * 2
    smem = whole(pltpu.SMEM)

    def params(mebibytes):
        return pltpu.CompilerParams(vmem_limit_bytes=mebibytes << 20)

    def shift(value, axis, step):
        count = lax.axis_size(axis)
        return lax.ppermute(value, axis, [(i, (i + step) % count) for i in range(count)])

    def plane_at(x):
        return pl.BlockSpec((1, rows, nz), lambda i: (x, 0, 0))

    def rows_at(y, height):
        return pl.BlockSpec((slab, height, nz), lambda i: (0, y // height, 0))

    speeds = [speed] * 4
    edge_specs = [plane_at(0), plane_at(slab - 1), rows_at(0, 16), rows_at(rows - 16, 16)]

    def step(centre, previous, kinds, states):
        def plane(move):
            return pl.BlockSpec(
                (1, rows, nz), lambda i: (jnp.clip(i + move, 0, slab - 1), 0, 0)
            )

        map_spec = pl.BlockSpec((per_plane, LANES), lambda i: (i, 0))
        return pl.pallas_call(
            stencil,
            grid=(slab,),
            out_shape=(block, dense),
            in_specs=[smem] * 2 + [plane(-1), plane(0), plane(1), plane(0), plane(0)]
            + [map_spec] * 2,
            out_specs=(plane(0), map_spec),
            compiler_params=params(16),
            name="stencil",
        )(pole, loss, centre, centre, centre, previous, speed, kinds, states)

    x_first, x_last, y_first, y_last = pl.pallas_call(
        edges,
        grid=(1,),
        out_shape=sends,
        in_specs=[plane_at(0), plane_at(slab - 1), rows_at(0, 8), rows_at(rows - 8, 8)],
        out_specs=(whole(),) * 4,
        compiler_params=params(16),
        name="edges",
    )(now, now, now, now)
    x_low = shift(x_last, "gx", 1)
    x_high = shift(x_first, "gx", -1)
    kinds, states = pl.pallas_call(
        node_maps,
        out_shape=(dense, dense),
        in_specs=[smem] * 2 + [whole()] * 3,
        out_specs=(whole(),) * 2,
        scratch_shapes=[pltpu.VMEM((nodes, LANES), F32)] * 3,
        compiler_params=params(16),
        name="node_maps",
    )(cells, loss, cells, material, state)
    y_first, y_last, kinds = after(y_first, y_last, kinds)
    y_low = shift(y_last, "gy", 1)
    y_high = shift(y_first, "gy", -1)
    half, states = step(now, prev, kinds, states)
    before, x_first, x_last, y_first, y_last = pl.pallas_call(
        fix_and_send,
        grid=(1,),
        out_shape=(block,) + sends,
        in_specs=[whole(pl.ANY)] + edge_specs + [whole()] * 4,
        out_specs=(whole(pl.ANY),) + (whole(),) * 4,
        scratch_shapes=[pltpu.VMEM((1, rows, nz), F32)] * 2
        + [pltpu.VMEM((slab, 8, nz), F32)] * 2
        + [pltpu.SemaphoreType.DMA((4,))],
        input_output_aliases={0: 0},
        compiler_params=params(16),
        name="fix_and_send",
    )(half, *speeds, x_low, x_high, y_low, y_high)
    x_low = shift(x_last, "gx", 1)
    x_high = shift(x_first, "gx", -1)
    partly, states = step(before, now, kinds, states)
    y_first, y_last, states = after(y_first, y_last, states)
    y_low = shift(y_last, "gy", 1)
    y_high = shift(y_first, "gy", -1)
    filter_out = pl.pallas_call(
        gather_nodes,
        out_shape=jax.ShapeDtypeStruct((1, nodes), F32),
        in_specs=[smem] * 2 + [whole()] * 3,
        out_specs=whole(),
        scratch_shapes=[pltpu.VMEM((nodes, LANES), F32)],
        compiler_params=params(16),
        name="gather_nodes",
    )(cells, loss, states, cells, material)
    pressure, partial = pl.pallas_call(
        fit,
        grid=(1,),
        out_shape=(block, jax.ShapeDtypeStruct((spheres, COEFS), F32)),
        in_specs=[smem, whole()] + edge_specs + [whole()] * 7,
        out_specs=(whole(),) * 2,
        scratch_shapes=[pltpu.VMEM((spheres * DEGREES, LANES), F32)] * 2,
        compiler_params=params(32),
        name="fit",
    )(
        anchors, partly, *speeds, x_low, x_high, y_low, y_high,
        jnp.asarray(plane_pairs(slab)), jnp.asarray(axial_windows(nz)), jnp.asarray(mix_table()),
    )
    coefficients = jnp.sum(lax.all_gather(partial, "gx", axis=0, tiled=False), axis=0)
    return pressure, before, filter_out.reshape(filter_state.shape), coefficients


def solution(mesh):
    grid = P("gx", "gy", None)
    return jax.shard_map(
        shards,
        mesh=mesh,
        in_specs=(grid,) * 6 + (P(), P(), P()),
        out_specs=(grid, grid, grid, P("gy", None)),
        check_vma=False,
    )
```

time: 95.8 us -> 82.4 us (0.86)
  Pallas kernels: 53.1 us -> 44.6 us
  local copies, waits for them, and re-layouts: 5.63 us -> 12.1 us
  starting transfers between devices: 20.1 us -> 14.4 us
  blocking collectives: 14.1 us -> 9.46 us
    pallas_call x4 -> x7, Pallas kernels: 53.1 us -> 44.6 us  [the longest x1 15.4 us: shards(): pl.pallas_call(fit, grid=(1,), out_shape=(block, jax.ShapeDtypeStruct((sp...]
    unnamed x22 -> x35, local copies, waits for them, and re-layouts: 4.44 us -> 12.1 us
    ppermute x8, starting transfers between devices: 20.1 us -> 14.4 us  [shift(): lax.ppermute(value, axis, [(i, (i + step) % count) for i in range(count)])]
    all_gather x1, blocking collectives: 14.1 us -> 9.46 us  [shards(): lax.all_gather(partial, 'gx', axis=0, tiled=False)]
  transfers between devices with their start and end apart: 8 -> 8, of which waited for: 0 -> 0; matrix products, arithmetic and copies ran while one was open for 2% -> 2% of each run, Pallas kernels for 34% -> 32%
where the time goes in v2:
time: 82.4 us; the launch traced here: 81.9 us
  Pallas kernels  44.6 us (54%)
  starting transfers between devices  14.4 us (17%)
  local copies, waits for them, and re-layouts  12.1 us (15%)
  blocking collectives  9.46 us (11%)
    pallas_call x1, Pallas kernels, shards(): pl.pallas_call(fit, grid=(1,), out_shape=(block, jax.ShapeDtypeStruct((sp...  15.4 us
    pallas_call x2, Pallas kernels, step(): pl.pallas_call(stencil, grid=(slab,), out_shape=(block, dense), in_specs=...  14.9 us
    ppermute x8, starting transfers between devices, shift(): lax.ppermute(value, axis, [(i, (i + step) % count) for i in range(count)])  14.4 us
    unnamed x35, local copies, waits for them, and re-layouts  12.1 us
    all_gather x1, blocking collectives, shards(): lax.all_gather(partial, 'gx', axis=0, tiled=False)  9.46 us
    pallas_call x1, Pallas kernels, shards(): pl.pallas_call(gather_nodes, out_shape=jax.ShapeDtypeStruct((1, nodes), F...  6.54 us
    pallas_call x1, Pallas kernels, shards(): pl.pallas_call(node_maps, out_shape=(dense, dense), in_specs=[smem] * 2 +...  4.71 us
    pallas_call x1, Pallas kernels, shards(): pl.pallas_call(fix_and_send, grid=(1,), out_shape=(block,) + sends, in_sp...  2.92 us
  transfers between devices with their start and end apart: 8, of which 0 were waited for; matrix products, arithmetic and copies ran while one was open for 2% of the time, Pallas kernels for 32%

profile of v2, /device:TPU:0, one launch (start us, length us, event | category | flops | bytes accessed | tf_op | source)
XLA Modules:
  0.0 81.9 jit_solution(18284738347429540621)
XLA Ops:
  0.6 1.7 %copy-done = f32[8,96,768]{2,1,0:T(8,128)S(1)} copy-done((f32[8,96,768]{2,1,0:T(8,128)S(1)}, f32[8,96,768]{2,1,0:T(8,128)}, u32[]{:S(2)}) %copy-start) | copy-done | bytes 2359320
  2.4 0.1 edges.1
  2.5 0.5 collective-permute-start
  3.0 2.9 %collective-permute-start.1 = (bf16[96,768]{1,0:T(8,128)(2,1)S(1)}, bf16[96,768]{1,0:T(8,128)(2,1)S(1)}, u32[]{:S(2)}, u32[]{:S(2)}) collective-permute-start(bf16[96,768]{1,0:T(8,128)(2,1)S(1)} %get-tuple-element.34), channel_id=1, source_target_pairs={{0,28},{4,0},{8,4},{12,8},{16,12},{20,16},{24,20},{28,24},{1,29},{... | collective-permute-start | bytes 442376 | tf_op jit(solution)/shard_map/ppermute | solution.py:443
  5.9 4.7 %node_maps.1 = (f32[4608,128]{1,0:T(8,128)S(1)}, f32[4608,128]{1,0:T(8,128)S(1)}) custom-call(s32[1,2048]{1,0:T(1,128)S(1)} %bitcast.5, f32[8]{0:T(128)S(1)} %copy-done.14, s32[1,2048]{1,0:T(1,128)S(1)} %bitcast.6, s32[1,2048]{1,0:T(1,128)S(1)} %bitcast.9, f32[1,2048]{1,0:T(1,128)S(1)} %bitcast.11), custom_call_target="tpu_custom_call" | custom-call | tf_op jit(solution)/shard_map/node_maps/pallas_call | solution.py:483
  10.7 2.3 %collective-permute-start.2 = (bf16[8,768]{1,0:T(8,128)(2,1)S(1)}, bf16[8,768]{1,0:T(8,128)(2,1)S(1)}, u32[]{:S(2)}, u32[]{:S(2)}) collective-permute-start(bf16[8,768]{1,0:T(8,128)(2,1)S(1)} %get-tuple-element.35), channel_id=1, source_target_pairs={{0,1},{1,2},{2,3},{3,0},{4,5},{5,6},{6,7},{7,4},{8,9},{9,10},{10,1... | collective-permute-start | bytes 36872 | tf_op jit(solution)/shard_map/ppermute | solution.py:443
  13.0 2.1 %collective-permute-start.3 = (bf16[8,768]{1,0:T(8,128)(2,1)S(1)}, bf16[8,768]{1,0:T(8,128)(2,1)S(1)}, u32[]{:S(2)}, u32[]{:S(2)}) collective-permute-start(bf16[8,768]{1,0:T(8,128)(2,1)S(1)} %get-tuple-element.36), channel_id=1, source_target_pairs={{0,3},{1,0},{2,1},{3,2},{4,7},{5,4},{6,5},{7,6},{8,11},{9,8},{10,9... | collective-permute-start | bytes 36872 | tf_op jit(solution)/shard_map/ppermute | solution.py:443
  15.1 7.9 %stencil.2 = (f32[8,96,768]{2,1,0:T(8,128)}, f32[4608,128]{1,0:T(8,128)S(1)}) custom-call(f32[8]{0:T(128)S(1)} %copy-done.16, f32[8]{0:T(128)S(1)} %copy-done.14, f32[8,96,768]{2,1,0:T(8,128)S(1)} %copy-done.1, f32[8,96,768]{2,1,0:T(8,128)S(1)} %copy-done.1, f32[8,96,768]{2,1,0:T(8,128)S(1)} %copy-done.1, f32[8,96,768]{2,1,0:T(8,128)S(1)} %copy-done.7, ...), custom_call_target="tpu_custom_call" | custom-call | tf_op jit(solution)/shard_map/stencil/pallas_call | solution.py:461
  23.0 2.9 %fix_and_send.1 = (f32[8,96,768]{2,1,0:T(8,128)}, bf16[96,768]{1,0:T(8,128)(2,1)}, bf16[96,768]{1,0:T(8,128)(2,1)}, bf16[8,768]{1,0:T(8,128)(2,1)}, bf16[8,768]{1,0:T(8,128)(2,1)}) custom-call(f32[8,96,768]{2,1,0:T(8,128)} %get-tuple-element.32.field_in, bf16[8,96,768]{2,1,0:T(8,128)(2,1)S(1)} %copy-done.2, ...), custom_call_target="tpu_custom_call", output_to_operand_aliasing={{0}: (0, {})} | custom-call | tf_op jit(solution)/shard_map/fix_and_send/pallas_call | solution.py:496
  26.0 2.6 %collective-permute-start.5 = (bf16[96,768]{1,0:T(8,128)(2,1)}, bf16[96,768]{1,0:T(8,128)(2,1)}, u32[]{:S(2)}, u32[]{:S(2)}) collective-permute-start(bf16[96,768]{1,0:T(8,128)(2,1)} %get-tuple-element.41), channel_id=1, source_target_pairs={{0,28},{4,0},{8,4},{12,8},{16,12},{20,16},{24,20},{28,24},{1,29},{... | collective-permute-start | bytes 442376 | tf_op jit(solution)/shard_map/ppermute | solution.py:443
  28.6 1.7 %copy-done.3 = f32[8,96,768]{2,1,0:T(8,128)S(1)} copy-done((f32[8,96,768]{2,1,0:T(8,128)S(1)}, f32[8,96,768]{2,1,0:T(8,128)}, u32[]{:S(2)}) %copy-start.3) | copy-done | bytes 2359320
  30.3 7.0 %stencil.3 = (f32[8,96,768]{2,1,0:T(8,128)S(1)}, f32[4608,128]{1,0:T(8,128)S(1)}) custom-call(f32[8]{0:T(128)S(1)} %copy-done.16, f32[8]{0:T(128)S(1)} %copy-done.14, f32[8,96,768]{2,1,0:T(8,128)S(1)} %copy-done.3, f32[8,96,768]{2,1,0:T(8,128)S(1)} %copy-done.3, f32[8,96,768]{2,1,0:T(8,128)S(1)} %copy-done.3, f32[8,96,768]{2,1,0:T(8,128)S(1)} %copy-done.1, ...), custom_call_target="tpu_custom_call" | custom-call | tf_op jit(solution)/shard_map/stencil/pallas_call | solution.py:461
  37.3 1.4 %copy-done.5 = f32[8,96,768]{2,1,0:T(8,128)} copy-done((f32[8,96,768]{2,1,0:T(8,128)}, f32[8,96,768]{2,1,0:T(8,128)S(1)}, u32[]{:S(2)}) %copy-start.5) | copy-done | bytes 2359320
  38.7 3.8 %collective-permute-start.7 = (bf16[8,768]{1,0:T(8,128)(2,1)}, bf16[8,768]{1,0:T(8,128)(2,1)}, u32[]{:S(2)}, u32[]{:S(2)}) collective-permute-start(bf16[8,768]{1,0:T(8,128)(2,1)} %get-tuple-element.46), channel_id=1, source_target_pairs={{0,3},{1,0},{2,1},{3,2},{4,7},{5,4},{6,5},{7,6},{8,11},{9,8},{10,9... | collective-permute-start | bytes 36872 | tf_op jit(solution)/shard_map/ppermute | solution.py:443
  42.5 1.4 %copy.17.anchor_ref = s32[128,3]{1,0:T(8,128)} copy(s32[128,3]{0,1:T(4,128)} %param.20) | data formatting | bytes 3072 | tf_op args[8]
  44.0 0.7 copy-done.15
  44.6 6.5 %gather_nodes.1 = f32[1,2048]{1,0:T(1,128)} custom-call(s32[1,2048]{1,0:T(1,128)S(1)} %bitcast.7, f32[8]{0:T(128)S(1)} %copy-done.15, f32[4608,128]{1,0:T(8,128)S(1)} %get-tuple-element.48.states, s32[1,2048]{1,0:T(1,128)S(1)} %bitcast.8, s32[1,2048]{1,0:T(1,128)S(1)} %bitcast.10), custom_call_target="tpu_custom_call" | custom-call | tf_op jit(solution)/shard_map/gather_nodes/pallas_call | solution.py:515
  51.2 2.3 %copy-done.4 = bf16[272,8192]{1,0:T(8,128)(2,1)S(1)} copy-done((bf16[272,8192]{1,0:T(8,128)(2,1)S(1)}, bf16[272,8192]{1,0:T(8,128)(2,1)}, u32[]{:S(2)}) %copy-start.4) | copy-done | bytes 4456472
  53.5 1.2 %copy-done.8 = bf16[2,944,256]{2,1,0:T(8,128)(2,1)S(1)} copy-done((bf16[2,944,256]{2,1,0:T(8,128)(2,1)S(1)}, bf16[2,944,256]{2,1,0:T(8,128)(2,1)}, u32[]{:S(2)}) %copy-start.8) | copy-done | bytes 966680
  54.7 0.8 %copy-done.9 = s32[128,3]{1,0:T(8,128)S(1)} copy-done((s32[128,3]{1,0:T(8,128)S(1)}, s32[128,3]{1,0:T(8,128)}, u32[]{:S(2)}) %copy-start.9) | copy-done | bytes 1560
  55.5 0.9 %copy-done.10 = bf16[16,32,256]{2,1,0:T(8,128)(2,1)S(1)} copy-done((bf16[16,32,256]{2,1,0:T(8,128)(2,1)S(1)}, bf16[16,32,256]{2,1,0:T(8,128)(2,1)}, u32[]{:S(2)}) %copy-start.10) | copy-done | bytes 262168
  56.4 15.4 %fit.1 = (f32[8,96,768]{2,1,0:T(8,128)}, f32[32,256]{1,0:T(8,128)S(1)}) custom-call(s32[128,3]{1,0:T(8,128)S(1)} %copy-done.9, f32[8,96,768]{2,1,0:T(8,128)S(1)} %copy-done.6, bf16[8,96,768]{2,1,0:T(8,128)(2,1)S(1)} %copy-done.2, bf16[8,96,768]{2,1,0:T(8,128)(2,1)S(1)} %copy-done.2, bf16[8,96,768]{2,1,0:T(8,128)(2,1)S(1)} %copy-done.2, ...), custom_call_target="tpu_custom_call" | custom-call | tf_op jit(solution)/shard_map/fit/pallas_call | solution.py:524
  71.8 9.5 %all-gather = f32[256,256]{1,0:T(8,128)S(1)} all-gather(f32[32,256]{1,0:T(8,128)S(1)} %get-tuple-element.49), channel_id=2, replica_groups=mesh['gx'=8,'gy'=4] {'gx'}, dimensions={0}, use_global_device_ids=true | all-gather | bytes 294912 | tf_op jit(solution)/shard_map/all_gather | solution.py:537
  81.3 0.6 reduce_sum.9
  (36 shorter events, 0.1 us)
Async XLA Ops:
  0.6 1.7 %copy-start = (f32[8,96,768]{2,1,0:T(8,128)S(1)}, f32[8,96,768]{2,1,0:T(8,128)}, u32[]{:S(2)}) copy-start(f32[8,96,768]{2,1,0:T(8,128)} %previous.3) | copy-start | bytes 7077892
  2.3 3.6 %copy-start.11 = (s32[1,1,2048]{2,1,0:T(1,128)S(1)}, s32[1,1,2048]{2,1,0:T(1,128)}, u32[]{:S(2)}) copy-start(s32[1,1,2048]{2,1,0:T(1,128)} %param.15) | copy-start | bytes 24580
  2.3 3.6 %copy-start.12 = (s32[1,1,2048]{2,1,0:T(1,128)S(1)}, s32[1,1,2048]{2,1,0:T(1,128)}, u32[]{:S(2)}) copy-start(s32[1,1,2048]{2,1,0:T(1,128)} %param.16) | copy-start | bytes 24580
  2.3 3.6 %copy-start.13 = (f32[1,1,2048]{2,1,0:T(1,128)S(1)}, f32[1,1,2048]{2,1,0:T(1,128)}, u32[]{:S(2)}) copy-start(f32[1,1,2048]{2,1,0:T(1,128)} %param.17) | copy-start | bytes 24580
  2.3 3.6 %copy-start.14 = (f32[8]{0:T(128)S(1)}, f32[8]{0:T(128)}, u32[]{:S(2)}) copy-start(f32[8]{0:T(128)} %loss_ref.7) | copy-start | bytes 100
  2.3 12.8 %copy-start.1 = (f32[8,96,768]{2,1,0:T(8,128)S(1)}, f32[8,96,768]{2,1,0:T(8,128)}, u32[]{:S(2)}) copy-start(f32[8,96,768]{2,1,0:T(8,128)} %previous.3) | copy-start | bytes 7077892
  2.3 12.8 %copy-start.2 = (bf16[8,96,768]{2,1,0:T(8,128)(2,1)S(1)}, bf16[8,96,768]{2,1,0:T(8,128)(2,1)}, u32[]{:S(2)}) copy-start(bf16[8,96,768]{2,1,0:T(8,128)(2,1)} %c_bottom.3) | copy-start | bytes 3538948
  2.3 12.7 %copy-start.7 = (f32[8,96,768]{2,1,0:T(8,128)S(1)}, f32[8,96,768]{2,1,0:T(8,128)}, u32[]{:S(2)}) copy-start(f32[8,96,768]{2,1,0:T(8,128)} %previous.2) | copy-start | bytes 7077892
  2.3 12.7 %copy-start.16 = (f32[8]{0:T(128)S(1)}, f32[8]{0:T(128)}, u32[]{:S(2)}) copy-start(f32[8]{0:T(128)} %pole_ref.3) | copy-start | bytes 100
  2.5 20.5 %collective-permute-start = (bf16[96,768]{1,0:T(8,128)(2,1)S(1)}, bf16[96,768]{1,0:T(8,128)(2,1)S(1)}, u32[]{:S(2)}, u32[]{:S(2)}) collective-permute-start(bf16[96,768]{1,0:T(8,128)(2,1)S(1)} %get-tuple-element.33), channel_id=1, source_target_pairs={{0,4},{4,8},{8,12},{12,16},{16,20},{20,24},{24,28},{28,0},{1,5},{5... | collective-permute-start | bytes 442376 | tf_op jit(solution)/shard_map/ppermute | solution.py:443
  3.0 20.0 %collective-permute-start.1 = (bf16[96,768]{1,0:T(8,128)(2,1)S(1)}, bf16[96,768]{1,0:T(8,128)(2,1)S(1)}, u32[]{:S(2)}, u32[]{:S(2)}) collective-permute-start(bf16[96,768]{1,0:T(8,128)(2,1)S(1)} %get-tuple-element.34), channel_id=1, source_target_pairs={{0,28},{4,0},{8,4},{12,8},{16,12},{20,16},{24,20},{28,24},{1,29},{... | collective-permute-start | bytes 442376 | tf_op jit(solution)/shard_map/ppermute | solution.py:443
  10.7 12.3 %collective-permute-start.2 = (bf16[8,768]{1,0:T(8,128)(2,1)S(1)}, bf16[8,768]{1,0:T(8,128)(2,1)S(1)}, u32[]{:S(2)}, u32[]{:S(2)}) collective-permute-start(bf16[8,768]{1,0:T(8,128)(2,1)S(1)} %get-tuple-element.35), channel_id=1, source_target_pairs={{0,1},{1,2},{2,3},{3,0},{4,5},{5,6},{6,7},{7,4},{8,9},{9,10},{10,1... | collective-permute-start | bytes 36872 | tf_op jit(solution)/shard_map/ppermute | solution.py:443
  13.0 10.0 %collective-permute-start.3 = (bf16[8,768]{1,0:T(8,128)(2,1)S(1)}, bf16[8,768]{1,0:T(8,128)(2,1)S(1)}, u32[]{:S(2)}, u32[]{:S(2)}) collective-permute-start(bf16[8,768]{1,0:T(8,128)(2,1)S(1)} %get-tuple-element.36), channel_id=1, source_target_pairs={{0,3},{1,0},{2,1},{3,2},{4,7},{5,4},{6,5},{7,6},{8,11},{9,8},{10,9... | collective-permute-start | bytes 36872 | tf_op jit(solution)/shard_map/ppermute | solution.py:443
  25.9 25.2 %collective-permute-start.4 = (bf16[96,768]{1,0:T(8,128)(2,1)}, bf16[96,768]{1,0:T(8,128)(2,1)}, u32[]{:S(2)}, u32[]{:S(2)}) collective-permute-start(bf16[96,768]{1,0:T(8,128)(2,1)} %get-tuple-element.40), channel_id=1, source_target_pairs={{0,4},{4,8},{8,12},{12,16},{16,20},{20,24},{24,28},{28,0},{1,5},{5... | collective-permute-start | bytes 442376 | tf_op jit(solution)/shard_map/ppermute | solution.py:443
  26.0 25.2 %collective-permute-start.5 = (bf16[96,768]{1,0:T(8,128)(2,1)}, bf16[96,768]{1,0:T(8,128)(2,1)}, u32[]{:S(2)}, u32[]{:S(2)}) collective-permute-start(bf16[96,768]{1,0:T(8,128)(2,1)} %get-tuple-element.41), channel_id=1, source_target_pairs={{0,28},{4,0},{8,4},{12,8},{16,12},{20,16},{24,20},{28,24},{1,29},{... | collective-permute-start | bytes 442376 | tf_op jit(solution)/shard_map/ppermute | solution.py:443
  28.6 1.7 %copy-start.3 = (f32[8,96,768]{2,1,0:T(8,128)S(1)}, f32[8,96,768]{2,1,0:T(8,128)}, u32[]{:S(2)}) copy-start(f32[8,96,768]{2,1,0:T(8,128)} %get-tuple-element.24.below.here_ref.above) | copy-start | bytes 7077892
  37.3 1.4 %copy-start.5 = (f32[8,96,768]{2,1,0:T(8,128)}, f32[8,96,768]{2,1,0:T(8,128)S(1)}, u32[]{:S(2)}) copy-start(f32[8,96,768]{2,1,0:T(8,128)S(1)} %get-tuple-element.39.pressure_in) | copy-start | bytes 7077892
  38.7 12.4 %collective-permute-start.6 = (bf16[8,768]{1,0:T(8,128)(2,1)}, bf16[8,768]{1,0:T(8,128)(2,1)}, u32[]{:S(2)}, u32[]{:S(2)}) collective-permute-start(bf16[8,768]{1,0:T(8,128)(2,1)} %get-tuple-element.45), channel_id=1, source_target_pairs={{0,1},{1,2},{2,3},{3,0},{4,5},{5,6},{6,7},{7,4},{8,9},{9,10},{10,1... | collective-permute-start | bytes 36872 | tf_op jit(solution)/shard_map/ppermute | solution.py:443
  38.7 12.4 %collective-permute-start.7 = (bf16[8,768]{1,0:T(8,128)(2,1)}, bf16[8,768]{1,0:T(8,128)(2,1)}, u32[]{:S(2)}, u32[]{:S(2)}) collective-permute-start(bf16[8,768]{1,0:T(8,128)(2,1)} %get-tuple-element.46), channel_id=1, source_target_pairs={{0,3},{1,0},{2,1},{3,2},{4,7},{5,4},{6,5},{7,6},{8,11},{9,8},{10,9... | collective-permute-start | bytes 36872 | tf_op jit(solution)/shard_map/ppermute | solution.py:443
  44.6 6.6 %copy-start.6 = (f32[8,96,768]{2,1,0:T(8,128)S(1)}, f32[8,96,768]{2,1,0:T(8,128)}, u32[]{:S(2)}) copy-start(f32[8,96,768]{2,1,0:T(8,128)} %copy-done.5) | copy-start | bytes 7077892
  51.2 2.3 %copy-start.4 = (bf16[272,8192]{1,0:T(8,128)(2,1)S(1)}, bf16[272,8192]{1,0:T(8,128)(2,1)}, u32[]{:S(2)}) copy-start(bf16[272,8192]{1,0:T(8,128)(2,1)} %constant.8.clone.pairs) | copy-start | bytes 13369348
  53.5 1.2 %copy-start.8 = (bf16[2,944,256]{2,1,0:T(8,128)(2,1)S(1)}, bf16[2,944,256]{2,1,0:T(8,128)(2,1)}, u32[]{:S(2)}) copy-start(bf16[2,944,256]{2,1,0:T(8,128)(2,1)} %constant.10.clone.mix) | copy-start | bytes 2899972
  54.7 0.8 %copy-start.9 = (s32[128,3]{1,0:T(8,128)S(1)}, s32[128,3]{1,0:T(8,128)}, u32[]{:S(2)}) copy-start(s32[128,3]{1,0:T(8,128)} %copy.17.anchor_ref) | copy-start | bytes 4612
  55.5 0.9 %copy-start.10 = (bf16[16,32,256]{2,1,0:T(8,128)(2,1)S(1)}, bf16[16,32,256]{2,1,0:T(8,128)(2,1)}, u32[]{:S(2)}) copy-start(bf16[16,32,256]{2,1,0:T(8,128)(2,1)} %constant.9.clone.axial) | copy-start | bytes 786436
  (1 other events, 0.7 us)

commit v3 on v2

--- a/solution.py
+++ b/solution.py
@@ -185,11 +185,13 @@
     lax.fori_loop(0, nodes, place, 0, unroll=32)
 
 
-def stencil(pole_ref, loss_ref, below, here_ref, above, previous, speed, kinds, states, out,
-            states_out):
+def stencil(start, last, pole_ref, loss_ref, below, here_ref, above, previous, speed, kinds,
+            states, *outs):
+    copies = len(outs) in (3, 6)
+    out, states_out = outs[-3:-1] if copies else outs[-2:]
     _, rows, nz = previous.shape
     groups, chunks = nz // LANES, rows // 8
-    x, last = pl.program_id(0), pl.num_programs(0) - 1
+    x = start + pl.program_id(0)
     lane, sub = iota((8, LANES), 1), iota((8, LANES), 0)
     first_lane, last_lane = lane == 0, lane == LANES - 1
     first_sub, last_sub = sub == 0, sub == 7
@@ -204,27 +206,24 @@
     def tile(ref, j, g):
         return ref[0, 8 * j : 8 * j + 8, LANES * g : LANES * (g + 1)]
 
+    def row_tiles(j):
+        tiles = [tile(here_ref, j, g) for g in range(groups)]
+        return tiles, [pltpu.roll(t, 1, 0) for t in tiles], [pltpu.roll(t, 7, 0) for t in tiles]
+
+    zero = jnp.zeros((8, LANES), F32)
+    blank = [zero] * groups
+    behind, current = (blank,) * 3, row_tiles(0)
     for j in range(chunks):
+        ahead = row_tiles(j + 1) if j + 1 < chunks else (blank,) * 3
+        heres, downs, ups = current
+        lefts = [zero] + [pltpu.roll(t, 1, 1) for t in heres]
+        rights = [pltpu.roll(t, LANES - 1, 1) for t in heres] + [zero]
         for g in range(groups):
-            here = tile(here_ref, j, g)
-            left = pltpu.roll(here, 1, 1)
-            left = jnp.where(
-                first_lane, pltpu.roll(tile(here_ref, j, g - 1), 1, 1) if g else 0.0, left
-            )
-            right = pltpu.roll(here, LANES - 1, 1)
-            right = jnp.where(
-                last_lane,
-                pltpu.roll(tile(here_ref, j, g + 1), LANES - 1, 1) if g + 1 < groups else 0.0,
-                right,
-            )
-            up = pltpu.roll(here, 1, 0)
-            up = jnp.where(first_sub, pltpu.roll(tile(here_ref, j - 1, g), 1, 0) if j else 0.0, up)
-            down = pltpu.roll(here, 7, 0)
-            down = jnp.where(
-                last_sub,
-                pltpu.roll(tile(here_ref, j + 1, g), 7, 0) if j + 1 < chunks else 0.0,
-                down,
-            )
+            here = heres[g]
+            left = jnp.where(first_lane, lefts[g], lefts[g + 1])
+            right = jnp.where(last_lane, rights[g + 1], rights[g])
+            up = jnp.where(first_sub, behind[1][g], downs[g])
+            down = jnp.where(last_sub, ahead[2][g], ups[g])
             beside = has_below * tile(below, j, g) + has_above * tile(above, j, g)
             beside = beside + up + down + left + right
             value = 2.0 * here - tile(previous, j, g)
@@ -235,54 +234,80 @@
             state = state + jnp.take_along_axis(gain, kind, axis=1) * value
             states_out[at, :] = state
             out[0, 8 * j : 8 * j + 8, LANES * g : LANES * (g + 1)] = value - state
-
-
-def flags():
-    out = []
-    for axis in ("gx", "gy"):
-        at = lax.axis_index(axis)
-        out.append(jnp.where(at > 0, 1.0, 0.0))
-        out.append(jnp.where(at < lax.axis_size(axis) - 1, 1.0, 0.0))
-    return out
-
-
-def edges(first, last, top, bottom, sx_low, sx_high, sy_low, sy_high):
-    sx_low[...] = first[0].astype(BF16)
-    sx_high[...] = last[0].astype(BF16)
+            if copies:
+                outs[-1][0, 8 * j : 8 * j + 8, LANES * g : LANES * (g + 1)] = here
+        behind, current = current, ahead
+
+
+def received(one, two, axis):
+    at = lax.axis_index(axis)
+    even = lax.rem(at, 2) == 0
+    one, two = one[...].astype(F32), two[...].astype(F32)
+    has_low = jnp.where(at > 0, 1.0, 0.0)
+    has_high = jnp.where(at < lax.axis_size(axis) - 1, 1.0, 0.0)
+    return has_low * jnp.where(even, two, one), has_high * jnp.where(even, one, two)
+
+
+def paired(low, high, axis):
+    even = lax.rem(lax.axis_index(axis), 2) == 0
+    return jnp.where(even, high, low).astype(BF16), jnp.where(even, low, high).astype(BF16)
+
+
+def edges(first, last, top, bottom, sx_one, sx_two, sy_one, sy_two):
+    sx_one[...], sx_two[...] = paired(first[0], last[0], "gx")
+    final = bottom.shape[1] - 1
     for x in range(top.shape[0]):
-        sy_low[x : x + 1, :] = top[x, 0:1, :].astype(BF16)
-        sy_high[x : x + 1, :] = bottom[x, bottom.shape[1] - 1 :, :].astype(BF16)
-
-
-def fix_planes(first, last, top, bottom, c_first, c_last, c_top, c_bottom, halo):
-    x_low, x_high, y_low, y_high = halo
-    has = flags()
+        line = slice(x, x + 1)
+        sy_one[line, :], sy_two[line, :] = paired(
+            top[x, 0:1, :], bottom[x, final : final + 1, :], "gy"
+        )
+
+
+def edge_places(slab, rows):
+    return (
+        (pl.ds(0, 1), pl.ds(0, rows)),
+        (pl.ds(slab - 1, 1), pl.ds(0, rows)),
+        (pl.ds(0, slab), pl.ds(0, 8)),
+        (pl.ds(0, slab), pl.ds(rows - 8, 8)),
+    )
+
+
+def first_edges(field, sx_one, sx_two, sy_one, sy_two, first, last, top, bottom, sems):
+    layers = (first, last, top, bottom)
+    copies = [
+        pltpu.make_async_copy(field.at[x, y], ref, sems.at[at])
+        for at, ((x, y), ref) in enumerate(zip(edge_places(*field.shape[:2]), layers))
+    ]
+    for copy in copies:
+        copy.start()
+    for copy in copies:
+        copy.wait()
+    edges(*layers, sx_one, sx_two, sy_one, sy_two)
+
+
+def fix_planes(first, last, top, bottom, c_first, c_last, c_top, c_bottom, x_halo, y_halo):
     slab, rows = top.shape[0], first.shape[1]
     final = top.shape[1] - 1
-    for at, value, speed, ref, flag in (
-        (0, first, c_first, x_low, has[0]),
-        (slab - 1, last, c_last, x_high, has[1]),
+    for at, value, speed, halo in (
+        (0, first, c_first, x_halo[0]),
+        (slab - 1, last, c_last, x_halo[1]),
     ):
-        value[0] = value[0] + speed[0].astype(F32) * (flag * ref[...].astype(F32))
-        for row, beside, there in ((0, y_low, has[2]), (rows - 1, y_high, has[3])):
+        value[0] = value[0] + speed[0].astype(F32) * halo
+        for row, beside in ((0, y_halo[0]), (rows - 1, y_halo[1])):
             one = slice(row, row + 1)
-            term = speed[0, one, :].astype(F32) * (there * beside[at : at + 1, :].astype(F32))
+            term = speed[0, one, :].astype(F32) * beside[at : at + 1, :]
             value[0, one, :] = value[0, one, :] + term
-    for x in range(slab):
-        if x in (0, slab - 1):
-            plane = first if x == 0 else last
-            top[x] = plane[0, : final + 1, :]
-            bottom[x] = plane[0, rows - final - 1 :, :]
-            continue
-        c = c_top[x, 0:1, :].astype(F32)
-        top[x, 0:1, :] = top[x, 0:1, :] + c * (has[2] * y_low[x : x + 1, :].astype(F32))
-        c = c_bottom[x, 15:16, :].astype(F32)
-        term = c * (has[3] * y_high[x : x + 1, :].astype(F32))
+    top[0], bottom[0] = first[0, :8, :], first[0, rows - 8 :, :]
+    top[slab - 1], bottom[slab - 1] = last[0, :8, :], last[0, rows - 8 :, :]
+    for x in range(1, slab - 1):
+        term = c_top[x, 0:1, :].astype(F32) * y_halo[0][x : x + 1, :]
+        top[x, 0:1, :] = top[x, 0:1, :] + term
+        term = c_bottom[x, 15:16, :].astype(F32) * y_halo[1][x : x + 1, :]
         bottom[x, final : final + 1, :] = bottom[x, final : final + 1, :] + term
 
 
-def fix_and_send(field_in, c_first, c_last, c_top, c_bottom, x_low, x_high, y_low, y_high,
-                 field, sx_low, sx_high, sy_low, sy_high, first, last, top, bottom, sems):
+def fix_and_send(field_in, c_first, c_last, c_top, c_bottom, x_one, x_two, y_one, y_two,
+                 field, sx_one, sx_two, sy_one, sy_two, first, last, top, bottom, sems):
     slab, rows = top.shape[0], first.shape[1]
     places = (
         (pl.ds(0, 1), pl.ds(0, rows), first),
@@ -299,7 +324,7 @@
     for copy in copies:
         copy.wait()
     fix_planes(first, last, top, bottom, c_first, c_last, c_top, c_bottom,
-               (x_low, x_high, y_low, y_high))
+               received(x_one, x_two, "gx"), received(y_one, y_two, "gy"))
     copies = [
         pltpu.make_async_copy(ref, field.at[x, y], sems.at[at])
         for at, (x, y, ref) in enumerate(places[:2])
@@ -311,7 +336,7 @@
     ]
     for copy in copies:
         copy.start()
-    edges(first, last, top, bottom, sx_low, sx_high, sy_low, sy_high)
+    edges(first, last, top, bottom, sx_one, sx_two, sy_one, sy_two)
     for copy in copies:
         copy.wait()
 
@@ -328,49 +353,65 @@
     lane_row = (cells[...] & (LANES - 1)).astype(F32)
     inverse = 1.0 / lookup(material[...], loss_ref, 0)
     lane = iota((GROUP, LANES), 1).astype(F32)
+    ones = jnp.ones((8, LANES), BF16)
     for at in range(nodes // GROUP):
         part = slice(at * GROUP, (at + 1) * GROUP)
-        chosen = jnp.where(columns_small(lane_row[:, part]) == lane, picked[part, :], 0.0)
-        line = lax.dot_general(
-            jnp.ones((8, LANES), F32), chosen, (((1,), (1,)), ((), ())),
-            precision=lax.Precision.HIGHEST, preferred_element_type=F32,
-        )
+        rest = jnp.where(columns_small(lane_row[:, part]) == lane, picked[part, :], 0.0)
+        line = jnp.zeros((8, GROUP), F32)
+        for _ in range(3):
+            piece = rest.astype(BF16)
+            rest = rest - piece.astype(F32)
+            line = line + lax.dot_general(
+                ones, piece, (((1,), (1,)), ((), ())), preferred_element_type=F32
+            )
         filter_out[:, part] = line[0:1, :] * inverse[:, part]
 
 
-def fit(anchor_ref, pressure_in, c_first, c_last, c_top, c_bottom, x_low, x_high, y_low, y_high,
-        pairs, axial, mix, pressure, partial, *products):
+def finish(cell_ref, loss_ref, anchor_ref, pressure_in, states_in, cells, material,
+           c_first, c_last, c_top, c_bottom, x_one, x_two, y_one, y_two,
+           pairs_in, axial_in, mix_in, pressure_out, partial, filter_out,
+           pressure, states, pairs, axial, mix, picked, planar, products_low, products_high, sems):
     slab, rows, nz = pressure.shape
     spheres = partial.shape[0]
     count = pairs.shape[0] // 2
+    incoming = [
+        pltpu.make_async_copy(source, target, sems.at[at])
+        for at, (source, target) in enumerate((
+            (states_in, states), (pressure_in, pressure), (pairs_in, pairs),
+            (axial_in, axial), (mix_in, mix),
+        ))
+    ]
+    for copy in incoming:
+        copy.start()
+    products = (products_low, products_high)
+    products_high[...] = jnp.zeros_like(products_high)
+    incoming[0].wait()
+    gather_nodes(cell_ref, loss_ref, states, cells, material, filter_out, picked)
+    incoming[1].wait()
     x_first = lax.axis_index("gx") * slab
     y_first = lax.axis_index("gy") * rows
     s_first = lax.axis_index("gy") * spheres
+    x_halo, y_halo = received(x_one, x_two, "gx"), received(y_one, y_two, "gy")
+    for at, speed, halo in ((0, c_first, x_halo[0]), (slab - 1, c_last, x_halo[1])):
+        pressure[at] = pressure[at] + speed[0].astype(F32) * halo
     for x in range(slab):
-        pressure[x] = pressure_in[x]
-    has = flags()
-    for at, speed, ref, flag in ((0, c_first, x_low, has[0]), (slab - 1, c_last, x_high, has[1])):
-        term = speed[0].astype(F32) * (flag * ref[...].astype(F32))
-        pressure[at] = pressure[at] + term
-    for x in range(slab):
-        for row, speed, r, ref, flag in (
-            (0, c_top, 0, y_low, has[2]),
-            (rows - 1, c_bottom, 15, y_high, has[3]),
-        ):
+        for row, speed, r, halo in ((0, c_top, 0, y_halo[0]), (rows - 1, c_bottom, 15, y_halo[1])):
             one = slice(row, row + 1)
-            term = speed[x, r : r + 1, :].astype(F32) * (flag * ref[x : x + 1, :].astype(F32))
+            term = speed[x, r : r + 1, :].astype(F32) * halo[x : x + 1, :]
             pressure[x, one, :] = pressure[x, one, :] + term
+    outgoing = pltpu.make_async_copy(pressure, pressure_out, sems.at[0])
+    outgoing.start()
+    for copy in incoming[2:]:
+        copy.wait()
     limit = CUBE * CUBE
     odd_y = 2 * iota((CUBE, 2 * LANES), 0) - (CUBE - 1)
     y_square = odd_y * odd_y
     lane = iota((CUBE, 2 * LANES), 1)
-    products[1][...] = jnp.zeros_like(products[1])
-
-    def sphere(s, carry):
-        base = s_first + s
-        x0 = anchor_ref[base, 0]
-        y0 = pl.multiple_of(anchor_ref[base, 1] - y_first, CUBE)
-        z0 = anchor_ref[base, 2]
+
+    def across(s, carry):
+        x0 = anchor_ref[0, s_first + s]
+        y0 = pl.multiple_of(anchor_ref[1, s_first + s] - y_first, CUBE)
+        z0 = anchor_ref[2, s_first + s]
         start = pl.multiple_of(window_start(z0, nz), LANES)
         odd_z = 2 * (lane - (z0 - start)) - (CUBE - 1)
         square = y_square + odd_z * odd_z
@@ -378,10 +419,9 @@
         planes = []
         for i in range(slab):
             odd_x = 2 * (a0 + i) - (CUBE - 1)
-            cells = pressure[i, pl.ds(y0, CUBE), pl.ds(start, 2 * LANES)]
-            planes.append(jnp.where(square <= limit - odd_x * odd_x, cells, 0.0).astype(BF16))
+            values = pressure[i, pl.ds(y0, CUBE), pl.ds(start, 2 * LANES)]
+            planes.append(jnp.where(square <= limit - odd_x * odd_x, values, 0.0).astype(BF16))
         blank = jnp.zeros((LANES - 2 * CUBE, 2 * LANES), BF16)
-        total = None
         first = jnp.clip(a0, -slab, CUBE) + slab
         left, right = [], []
         for i in range(0, slab, 2):
@@ -389,9 +429,12 @@
             left.append(pairs[:, pl.ds(at, LANES)])
             right += [planes[i], planes[i + 1], blank]
         total = dot(jnp.concatenate(left, axis=1), jnp.concatenate(right, axis=0))
-        high, low = split(total[:count] + total[count:])
-        tile = lax.shift_right_logical(z0 * 1366, 16)
-        factor = axial[tile]
+        planar[s] = total[:count] + total[count:]
+        return carry
+
+    def along(s, carry):
+        high, low = split(planar[s])
+        factor = axial[lax.shift_right_logical(anchor_ref[2, s_first + s] * 1366, 16)]
         contract = (((1,), (1,)), ((), ()))
         one = lax.dot_general(factor, high, contract, preferred_element_type=F32)
         two = lax.dot_general(factor[:DEGREES], low, contract, preferred_element_type=F32)
@@ -401,7 +444,8 @@
         products[1][at, 0 : count - LANES] = moment[:, LANES:]
         return carry
 
-    lax.fori_loop(0, spheres, sphere, 0, unroll=4)
+    lax.fori_loop(0, spheres, across, 0, unroll=4)
+    lax.fori_loop(0, spheres, along, 0, unroll=8)
     result = jnp.zeros((spheres, COEFS), F32)
     for q in range(DEGREES):
         at = pl.ds(q, spheres, stride=DEGREES)
@@ -411,6 +455,7 @@
         upper, lower = mix[0, first : first + size], mix[1, first : first + size]
         result = result + (dot(high, upper) + (dot(low, upper) + dot(high, lower)))
     partial[...] = result
+    outgoing.wait()
 
 
 def whole(memory=pltpu.VMEM):
@@ -438,9 +483,10 @@
     def params(mebibytes):
         return pltpu.CompilerParams(vmem_limit_bytes=mebibytes << 20)
 
-    def shift(value, axis, step):
+    def swap(value, axis, side):
         count = lax.axis_size(axis)
-        return lax.ppermute(value, axis, [(i, (i + step) % count) for i in range(count)])
+        moves = [1 - 2 * (i % 2) if side == 0 else 2 * (i % 2) - 1 for i in range(count)]
+        return lax.ppermute(value, axis, [(i, (i + moves[i]) % count) for i in range(count)])
 
     def plane_at(x):
         return pl.BlockSpec((1, rows, nz), lambda i: (x, 0, 0))
@@ -451,35 +497,39 @@
     speeds = [speed] * 4
     edge_specs = [plane_at(0), plane_at(slab - 1), rows_at(0, 16), rows_at(rows - 16, 16)]
 
-    def step(centre, previous, kinds, states):
+    def step(centre, previous, kinds, states, part, limit, copies, done=()):
+        start, stop = part
+
         def plane(move):
             return pl.BlockSpec(
-                (1, rows, nz), lambda i: (jnp.clip(i + move, 0, slab - 1), 0, 0)
+                (1, rows, nz), lambda i: (jnp.clip(i + start + move, 0, slab - 1), 0, 0)
             )
 
-        map_spec = pl.BlockSpec((per_plane, LANES), lambda i: (i, 0))
+        map_spec = pl.BlockSpec((per_plane, LANES), lambda i: (i + start, 0))
         return pl.pallas_call(
-            stencil,
-            grid=(slab,),
-            out_shape=(block, dense),
+            functools.partial(stencil, start, slab - 1),
+            grid=(stop - start,),
+            out_shape=(block, dense) + (block,) * copies,
             in_specs=[smem] * 2 + [plane(-1), plane(0), plane(1), plane(0), plane(0)]
-            + [map_spec] * 2,
-            out_specs=(plane(0), map_spec),
-            compiler_params=params(16),
+            + [map_spec] * 2 + [whole(pl.ANY)] * len(done),
+            out_specs=(plane(0), map_spec) + (plane(0),) * copies,
+            input_output_aliases={9 + at: at for at in range(len(done))},
+            compiler_params=params(limit),
             name="stencil",
-        )(pole, loss, centre, centre, centre, previous, speed, kinds, states)
-
-    x_first, x_last, y_first, y_last = pl.pallas_call(
-        edges,
-        grid=(1,),
+        )(pole, loss, centre, centre, centre, previous, speed, kinds, states, *done)
+
+    layers = [pltpu.VMEM((1, rows, nz), F32)] * 2 + [pltpu.VMEM((slab, 8, nz), F32)] * 2
+    layers += [pltpu.SemaphoreType.DMA((4,))]
+    sx_one, sx_two, sy_one, sy_two = pl.pallas_call(
+        first_edges,
         out_shape=sends,
-        in_specs=[plane_at(0), plane_at(slab - 1), rows_at(0, 8), rows_at(rows - 8, 8)],
+        in_specs=[whole(pltpu.HBM)],
         out_specs=(whole(),) * 4,
+        scratch_shapes=layers,
         compiler_params=params(16),
         name="edges",
-    )(now, now, now, now)
-    x_low = shift(x_last, "gx", 1)
-    x_high = shift(x_first, "gx", -1)
+    )(now)
+    x_one, x_two = swap(sx_one, "gx", 0), swap(sx_two, "gx", 1)
     kinds, states = pl.pallas_call(
         node_maps,
         out_shape=(dense, dense),
@@ -489,52 +539,62 @@
         compiler_params=params(16),
         name="node_maps",
     )(cells, loss, cells, material, state)
-    y_first, y_last, kinds = after(y_first, y_last, kinds)
-    y_low = shift(y_last, "gy", 1)
-    y_high = shift(y_first, "gy", -1)
-    half, states = step(now, prev, kinds, states)
-    before, x_first, x_last, y_first, y_last = pl.pallas_call(
+    sy_one, sy_two, kinds = after(sy_one, sy_two, kinds)
+    y_one, y_two = swap(sy_one, "gy", 0), swap(sy_two, "gy", 1)
+    half, states = step(now, prev, kinds, states, (0, slab), 16, False)
+    half, sx_one, sx_two, sy_one, sy_two = pl.pallas_call(
         fix_and_send,
         grid=(1,),
         out_shape=(block,) + sends,
         in_specs=[whole(pl.ANY)] + edge_specs + [whole()] * 4,
         out_specs=(whole(pl.ANY),) + (whole(),) * 4,
-        scratch_shapes=[pltpu.VMEM((1, rows, nz), F32)] * 2
-        + [pltpu.VMEM((slab, 8, nz), F32)] * 2
-        + [pltpu.SemaphoreType.DMA((4,))],
+        scratch_shapes=layers,
         input_output_aliases={0: 0},
         compiler_params=params(16),
         name="fix_and_send",
-    )(half, *speeds, x_low, x_high, y_low, y_high)
-    x_low = shift(x_last, "gx", 1)
-    x_high = shift(x_first, "gx", -1)
-    partly, states = step(before, now, kinds, states)
-    y_first, y_last, states = after(y_first, y_last, states)
-    y_low = shift(y_last, "gy", 1)
-    y_high = shift(y_first, "gy", -1)
-    filter_out = pl.pallas_call(
-        gather_nodes,
-        out_shape=jax.ShapeDtypeStruct((1, nodes), F32),
-        in_specs=[smem] * 2 + [whole()] * 3,
-        out_specs=whole(),
-        scratch_shapes=[pltpu.VMEM((nodes, LANES), F32)],
-        compiler_params=params(16),
-        name="gather_nodes",
-    )(cells, loss, states, cells, material)
-    pressure, partial = pl.pallas_call(
-        fit,
+    )(half, *speeds, x_one, x_two, y_one, y_two)
+    x_one, x_two = swap(sx_one, "gx", 0), swap(sx_two, "gx", 1)
+    first_part = step(half, now, kinds, states, (0, slab // 2), 16, True)
+    sy_one, sy_two, *first_part = after(sy_one, sy_two, *first_part)
+    y_one, y_two = swap(sy_one, "gy", 0), swap(sy_two, "gy", 1)
+    partly, states, before = step(
+        half, now, kinds, states, (slab // 2, slab), 16, True, first_part
+    )
+    fit_tables = (plane_pairs(slab), axial_windows(nz), mix_table())
+    pressure, partial, filter_out = pl.pallas_call(
+        finish,
         grid=(1,),
-        out_shape=(block, jax.ShapeDtypeStruct((spheres, COEFS), F32)),
-        in_specs=[smem, whole()] + edge_specs + [whole()] * 7,
-        out_specs=(whole(),) * 2,
-        scratch_shapes=[pltpu.VMEM((spheres * DEGREES, LANES), F32)] * 2,
+        out_shape=(
+            block,
+            jax.ShapeDtypeStruct((spheres, COEFS), F32),
+            jax.ShapeDtypeStruct((1, nodes), F32),
+        ),
+        in_specs=[smem] * 3 + [whole(pl.ANY)] * 2 + [whole()] * 2 + edge_specs + [whole()] * 4
+        + [whole(pltpu.HBM)] * 3,
+        out_specs=(whole(pl.ANY), whole(), whole()),
+        scratch_shapes=[pltpu.VMEM(block.shape, F32), pltpu.VMEM(dense.shape, F32)]
+        + [pltpu.VMEM(table.shape, BF16) for table in fit_tables]
+        + [
+            pltpu.VMEM((nodes, LANES), F32),
+            pltpu.VMEM((spheres, fit_tables[0].shape[0] // 2, 2 * LANES), F32),
+            pltpu.VMEM((spheres * DEGREES, LANES), F32),
+            pltpu.VMEM((spheres * DEGREES, LANES), F32),
+            pltpu.SemaphoreType.DMA((5,)),
+        ],
         compiler_params=params(32),
-        name="fit",
+        name="finish",
     )(
-        anchors, partly, *speeds, x_low, x_high, y_low, y_high,
-        jnp.asarray(plane_pairs(slab)), jnp.asarray(axial_windows(nz)), jnp.asarray(mix_table()),
+        cells, loss, anchors.T, partly, states, cells, material, *speeds,
+        x_one, x_two, y_one, y_two, *(jnp.asarray(table) for table in fit_tables),
     )
-    coefficients = jnp.sum(lax.all_gather(partial, "gx", axis=0, tiled=False), axis=0)
+    if lax.axis_size("gx") == 8:
+        partial = partial + swap(partial, "gx", 0)
+        others = [
+            lax.ppermute(partial, "gx", [(i, i ^ move) for i in range(8)]) for move in (2, 4, 6)
+        ]
+        coefficients = (partial + others[0]) + (others[1] + others[2])
+    else:
+        coefficients = jnp.sum(lax.all_gather(partial, "gx", axis=0, tiled=False), axis=0)
     return pressure, before, filter_out.reshape(filter_state.shape), coefficients
 
 

time: 82.4 us -> 58.5 us (0.71)
  Pallas kernels: 44.6 us -> 32.1 us
  blocking collectives: 9.46 us -> 0 us
  local copies, waits for them, and re-layouts: 12.1 us -> 5.13 us
  waiting for transfers between devices: 0.02 us -> 5.5 us
    pallas_call x5, Pallas kernels: 37 us -> 26.6 us  [the longest x1 13.4 us: shards(): pl.pallas_call(finish, grid=(1,), out_shape=(block, jax.ShapeDtypeStruct(...]
    all_gather x1 -> x0, blocking collectives: 9.46 us -> none  [shards(): lax.all_gather(partial, 'gx', axis=0, tiled=False)]
    unnamed x35 -> x28, local copies, waits for them, and re-layouts: 12.1 us -> 5.13 us
    ppermute x8 -> x12, waiting for transfers between devices: 0.02 us -> 5.5 us  [the longest x3 3.37 us: shards(): lax.ppermute(partial, 'gx', [(i, i ^ move) for i in range(8)])]
    pallas_call x1, Pallas kernels: 2.92 us -> 0.85 us  [shards(): pl.pallas_call(fix_and_send, grid=(1,), out_shape=(block,) + sends, in_sp...]
    ppermute x8 -> x12, starting transfers between devices: 14.4 us -> 14.1 us  [the longest x9 10.6 us: swap(): lax.ppermute(value, axis, [(i, (i + moves[i]) % count) for i in range(cou...]
  transfers between devices with their start and end apart: 8 -> 12, of which waited for: 0 -> 5; matrix products, arithmetic and copies ran while one was open for 2% -> 0% of each run, Pallas kernels for 32% -> 30%
where the time goes in v3:
time: 58.5 us; the launch traced here: 58.3 us
  Pallas kernels  32.1 us (55%)
  starting transfers between devices  14.1 us (24%)
  waiting for transfers between devices  5.5 us (9%)
  local copies, waits for them, and re-layouts  5.13 us (9%)
  between operations  0.83 us (1%)
  other arithmetic  0.63 us (1%)
    pallas_call x1, Pallas kernels, shards(): pl.pallas_call(finish, grid=(1,), out_shape=(block, jax.ShapeDtypeStruct(...  13.4 us
    pallas_call x3, Pallas kernels, step(): pl.pallas_call(functools.partial(stencil, start, slab - 1), grid=(stop -...  12.8 us
    ppermute x9, starting transfers between devices, swap(): lax.ppermute(value, axis, [(i, (i + moves[i]) % count) for i in range(cou...  10.6 us
    unnamed x28, local copies, waits for them, and re-layouts  5.13 us
    pallas_call x1, Pallas kernels, shards(): pl.pallas_call(node_maps, out_shape=(dense, dense), in_specs=[smem] * 2 +...  4.71 us
    ppermute x3, starting transfers between devices, shards(): lax.ppermute(partial, 'gx', [(i, i ^ move) for i in range(8)])  3.49 us
    ppermute x3, waiting for transfers between devices, shards(): lax.ppermute(partial, 'gx', [(i, i ^ move) for i in range(8)])  3.37 us
    ppermute x9, waiting for transfers between devices, swap(): lax.ppermute(value, axis, [(i, (i + moves[i]) % count) for i in range(cou...  2.13 us
  transfers between devices with their start and end apart: 12, of which 5 were waited for; matrix products, arithmetic and copies ran while one was open for 0% of the time, Pallas kernels for 30%

profile of v3, /device:TPU:0, one launch (start us, length us, event | category | flops | bytes accessed | tf_op | source)
XLA Modules:
  0.0 58.3 jit_solution(13343579134914638120)
XLA Ops:
  0.7 1.8 %copy-done.1 = f32[8,96,768]{2,1,0:T(8,128)S(1)} copy-done((f32[8,96,768]{2,1,0:T(8,128)S(1)}, f32[8,96,768]{2,1,0:T(8,128)}, u32[]{:S(2)}) %copy-start.1) | copy-done | bytes 2359320
  3.3 3.6 %collective-permute-start.1 = (bf16[96,768]{1,0:T(8,128)(2,1)S(1)}, bf16[96,768]{1,0:T(8,128)(2,1)S(1)}, u32[]{:S(2)}, u32[]{:S(2)}) collective-permute-start(bf16[96,768]{1,0:T(8,128)(2,1)S(1)} %get-tuple-element.41), channel_id=1, source_target_pairs={{0,28},{4,8},{8,4},{12,16},{16,12},{20,24},{24,20},{28,0},{1,29},{... | collective-permute-start | bytes 442376 | tf_op jit(solution)/shard_map/ppermute | solution.py:489
  6.9 4.7 %node_maps.1 = (f32[4608,128]{1,0:T(8,128)S(1)}, f32[4608,128]{1,0:T(8,128)S(1)}) custom-call(s32[1,2048]{1,0:T(1,128)S(1)} %bitcast.7, f32[8]{0:T(128)S(1)} %copy-done.8, s32[1,2048]{1,0:T(1,128)S(1)} %bitcast.8, s32[1,2048]{1,0:T(1,128)S(1)} %bitcast.11, f32[1,2048]{1,0:T(1,128)S(1)} %bitcast.13), custom_call_target="tpu_custom_call" | custom-call | tf_op jit(solution)/shard_map/node_maps/pallas_call | solution.py:533
  11.6 1.6 %collective-permute-start.2 = (bf16[8,768]{1,0:T(8,128)(2,1)S(1)}, bf16[8,768]{1,0:T(8,128)(2,1)S(1)}, u32[]{:S(2)}, u32[]{:S(2)}) collective-permute-start(bf16[8,768]{1,0:T(8,128)(2,1)S(1)} %get-tuple-element.42), channel_id=1, source_target_pairs={{0,1},{1,0},{2,3},{3,2},{4,5},{5,4},{6,7},{7,6},{8,9},{9,8},{10,11... | collective-permute-start | bytes 36872 | tf_op jit(solution)/shard_map/ppermute | solution.py:489
  13.2 2.5 %collective-permute-start.3 = (bf16[8,768]{1,0:T(8,128)(2,1)S(1)}, bf16[8,768]{1,0:T(8,128)(2,1)S(1)}, u32[]{:S(2)}, u32[]{:S(2)}) collective-permute-start(bf16[8,768]{1,0:T(8,128)(2,1)S(1)} %get-tuple-element.43), channel_id=1, source_target_pairs={{0,3},{1,2},{2,1},{3,0},{4,7},{5,6},{6,5},{7,4},{8,11},{9,10},{10,... | collective-permute-start | bytes 36872 | tf_op jit(solution)/shard_map/ppermute | solution.py:489
  15.7 1.7 %copy-done.2 = f32[8,96,768]{2,1,0:T(8,128)S(1)} copy-done((f32[8,96,768]{2,1,0:T(8,128)S(1)}, f32[8,96,768]{2,1,0:T(8,128)}, u32[]{:S(2)}) %copy-start.2) | copy-done | bytes 2359320
  17.4 1.7 %copy-done.3 = f32[8,96,768]{2,1,0:T(8,128)S(1)} copy-done((f32[8,96,768]{2,1,0:T(8,128)S(1)}, f32[8,96,768]{2,1,0:T(8,128)}, u32[]{:S(2)}) %copy-start.3) | copy-done | bytes 2359320
  19.1 5.5 %stencil.3 = (f32[8,96,768]{2,1,0:T(8,128)S(1)}, f32[4608,128]{1,0:T(8,128)S(1)}) custom-call(f32[8]{0:T(128)S(1)} %copy-done.10, f32[8]{0:T(128)S(1)} %copy-done.8, f32[8,96,768]{2,1,0:T(8,128)S(1)} %copy-done.2, f32[8,96,768]{2,1,0:T(8,128)S(1)} %copy-done.2, f32[8,96,768]{2,1,0:T(8,128)S(1)} %copy-done.2, f32[8,96,768]{2,1,0:T(8,128)S(1)} %copy-done.3, ...), custom_call_target="tpu_custom_call" | custom-call | tf_op jit(solution)/shard_map/stencil/pallas_call | solution.py:509
  24.6 0.9 %fix_and_send.1 = (f32[8,96,768]{2,1,0:T(8,128)S(1)}, bf16[96,768]{1,0:T(8,128)(2,1)S(1)}, bf16[96,768]{1,0:T(8,128)(2,1)S(1)}, bf16[8,768]{1,0:T(8,128)(2,1)S(1)}, bf16[8,768]{1,0:T(8,128)(2,1)S(1)}) custom-call(f32[8,96,768]{2,1,0:T(8,128)S(1)} %get-tuple-element.39.field_in, bf16[8,96,768]{2,1,0:T(8,128)(2,1)S(1)} %copy-done, ...), custom_call_target="tpu_custom_call", output_to_operand_aliasing={{0}: (0, {})} | custom-call | tf_op jit(solution)/shard_map/fix_and_send/pallas_call | solution.py:545
  25.6 0.6 %collective-permute-start.5 = (bf16[96,768]{1,0:T(8,128)(2,1)S(1)}, bf16[96,768]{1,0:T(8,128)(2,1)S(1)}, u32[]{:S(2)}, u32[]{:S(2)}) collective-permute-start(bf16[96,768]{1,0:T(8,128)(2,1)S(1)} %get-tuple-element.57), channel_id=1, source_target_pairs={{0,28},{4,8},{8,4},{12,16},{16,12},{20,24},{24,20},{28,0},{1,29},{... | collective-permute-start | bytes 442376 | tf_op jit(solution)/shard_map/ppermute | solution.py:489
  26.2 3.7 %stencil.4 = (f32[8,96,768]{2,1,0:T(8,128)S(1)}, f32[4608,128]{1,0:T(8,128)S(1)}, f32[8,96,768]{2,1,0:T(8,128)}) custom-call(f32[8]{0:T(128)S(1)} %copy-done.10, f32[8]{0:T(128)S(1)} %copy-done.8, f32[8,96,768]{2,1,0:T(8,128)S(1)} %get-tuple-element.44.below.here_ref.above, f32[8,96,768]{2,1,0:T(8,128)S(1)} %get-tuple-element.44.below.here_ref.above, ...), custom_call_target="tpu_custom_call" | custom-call | tf_op jit(solution)/shard_map/stencil/pallas_call | solution.py:509
  29.9 0.7 %collective-permute-start.6 = (bf16[8,768]{1,0:T(8,128)(2,1)S(1)}, bf16[8,768]{1,0:T(8,128)(2,1)S(1)}, u32[]{:S(2)}, u32[]{:S(2)}) collective-permute-start(bf16[8,768]{1,0:T(8,128)(2,1)S(1)} %get-tuple-element.58), channel_id=1, source_target_pairs={{0,1},{1,0},{2,3},{3,2},{4,5},{5,4},{6,7},{7,6},{8,9},{9,8},{10,11... | collective-permute-start | bytes 36872 | tf_op jit(solution)/shard_map/ppermute | solution.py:489
  30.6 0.9 %collective-permute-start.7 = (bf16[8,768]{1,0:T(8,128)(2,1)S(1)}, bf16[8,768]{1,0:T(8,128)(2,1)S(1)}, u32[]{:S(2)}, u32[]{:S(2)}) collective-permute-start(bf16[8,768]{1,0:T(8,128)(2,1)S(1)} %get-tuple-element.59), channel_id=1, source_target_pairs={{0,3},{1,2},{2,1},{3,0},{4,7},{5,6},{6,5},{7,4},{8,11},{9,10},{10,... | collective-permute-start | bytes 36872 | tf_op jit(solution)/shard_map/ppermute | solution.py:489
  31.5 3.7 %stencil.5 = (f32[8,96,768]{2,1,0:T(8,128)S(1)}, f32[4608,128]{1,0:T(8,128)S(1)}, f32[8,96,768]{2,1,0:T(8,128)}) custom-call(f32[8]{0:T(128)S(1)} %copy-done.10, f32[8]{0:T(128)S(1)} %copy-done.8, f32[8,96,768]{2,1,0:T(8,128)S(1)} %get-tuple-element.44.below.here_ref.above, ...), custom_call_target="tpu_custom_call", output_to_operand_aliasing={{0}: (9, {}), {1}: (10, {}), {2}: (11, {})} | custom-call | tf_op jit(solution)/shard_map/stencil/pallas_call | solution.py:509
  35.2 0.9 %collective-permute-done.7.y_two = bf16[8,768]{1,0:T(8,128)(2,1)S(1)} collective-permute-done((bf16[8,768]{1,0:T(8,128)(2,1)S(1)}, bf16[8,768]{1,0:T(8,128)(2,1)S(1)}, u32[]{:S(2)}, u32[]{:S(2)}) %collective-permute-start.7) | collective-permute-done | bytes 12320 | tf_op jit(solution)/shard_map/ppermute | solution.py:489
  36.2 13.4 %finish.1 = (f32[8,96,768]{2,1,0:T(8,128)}, f32[32,256]{1,0:T(8,128)S(1)}, f32[1,2048]{1,0:T(1,128)}) custom-call(s32[1,2048]{1,0:T(1,128)S(1)} %bitcast.9, f32[8]{0:T(128)S(1)} %copy-done.8, s32[3,128]{1,0:T(4,128)S(1)} %bitcast.14, f32[8,96,768]{2,1,0:T(8,128)S(1)} %get-tuple-element.54.pressure_in, f32[4608,128]{1,0:T(8,128)S(1)} %get-tuple-element.55.states_in, ...), custom_call_target="tpu_custom_call" | custom-call | tf_op jit(solution)/shard_map/finish/pallas_call | solution.py:564
  49.6 1.2 %collective-permute-done.8 = f32[32,256]{1,0:T(8,128)S(1)} collective-permute-done((f32[32,256]{1,0:T(8,128)S(1)}, f32[32,256]{1,0:T(8,128)S(1)}, u32[]{:S(2)}, u32[]{:S(2)}) %collective-permute-start.8) | collective-permute-done | bytes 32800 | tf_op jit(solution)/shard_map/ppermute | solution.py:489
  50.8 1.4 %collective-permute-start.11 = (f32[32,256]{1,0:T(8,128)S(1)}, f32[32,256]{1,0:T(8,128)S(1)}, u32[]{:S(2)}, u32[]{:S(2)}) collective-permute-start(f32[32,256]{1,0:T(8,128)S(1)} %add.12), channel_id=1, source_target_pairs={{0,24},{4,28},{8,16},{12,20},{16,8},{20,12},{24,0},{28,4},{1,25},{... | collective-permute-start | bytes 98312 | tf_op jit(solution)/shard_map/ppermute | solution.py:593
  52.3 1.5 %collective-permute-start.10 = (f32[32,256]{1,0:T(8,128)S(1)}, f32[32,256]{1,0:T(8,128)S(1)}, u32[]{:S(2)}, u32[]{:S(2)}) collective-permute-start(f32[32,256]{1,0:T(8,128)S(1)} %add.12), channel_id=1, source_target_pairs={{0,16},{4,20},{8,24},{12,28},{16,0},{20,4},{24,8},{28,12},{1,17},{... | collective-permute-start | bytes 98312 | tf_op jit(solution)/shard_map/ppermute | solution.py:593
  53.8 0.5 collective-permute-start.9
  54.3 1.3 %collective-permute-done.11 = f32[32,256]{1,0:T(8,128)S(1)} collective-permute-done((f32[32,256]{1,0:T(8,128)S(1)}, f32[32,256]{1,0:T(8,128)S(1)}, u32[]{:S(2)}, u32[]{:S(2)}) %collective-permute-start.11) | collective-permute-done | bytes 32800 | tf_op jit(solution)/shard_map/ppermute | solution.py:593
  55.6 0.5 collective-permute-done.10
  56.2 1.5 %collective-permute-done.9 = f32[32,256]{1,0:T(8,128)S(1)} collective-permute-done((f32[32,256]{1,0:T(8,128)S(1)}, f32[32,256]{1,0:T(8,128)S(1)}, u32[]{:S(2)}, u32[]{:S(2)}) %collective-permute-start.9) | collective-permute-done | bytes 32800 | tf_op jit(solution)/shard_map/ppermute | solution.py:593
  57.7 0.6 %add_add_fusion = f32[32,256]{1,0:T(8,128)} fusion(f32[32,256]{1,0:T(8,128)S(1)} %collective-permute-done.10, f32[32,256]{1,0:T(8,128)S(1)} %collective-permute-done.11, f32[32,256]{1,0:T(8,128)S(1)} %add.12, f32[32,256]{1,0:T(8,128)S(1)} %collective-permute-done.9), kind=kLoop, calls=%fused_computation | loop fusion | flops 24576 | bytes 163840 | tf_op jit(solution)/shard_map/add | solution.py:595
  (38 shorter events, 1.1 us)
Async XLA Ops:
  0.6 15.1 %copy-start = (bf16[8,96,768]{2,1,0:T(8,128)(2,1)S(1)}, bf16[8,96,768]{2,1,0:T(8,128)(2,1)}, u32[]{:S(2)}) copy-start(bf16[8,96,768]{2,1,0:T(8,128)(2,1)} %c_bottom.3) | copy-start | bytes 3538948
  0.6 1.8 %copy-start.1 = (f32[8,96,768]{2,1,0:T(8,128)S(1)}, f32[8,96,768]{2,1,0:T(8,128)}, u32[]{:S(2)}) copy-start(f32[8,96,768]{2,1,0:T(8,128)} %previous.5) | copy-start | bytes 7077892
  2.4 4.5 %copy-start.6 = (s32[1,1,2048]{2,1,0:T(1,128)S(1)}, s32[1,1,2048]{2,1,0:T(1,128)}, u32[]{:S(2)}) copy-start(s32[1,1,2048]{2,1,0:T(1,128)} %param.15) | copy-start | bytes 24580
  2.4 4.5 %copy-start.7 = (s32[1,1,2048]{2,1,0:T(1,128)S(1)}, s32[1,1,2048]{2,1,0:T(1,128)}, u32[]{:S(2)}) copy-start(s32[1,1,2048]{2,1,0:T(1,128)} %param.16) | copy-start | bytes 24580
  2.4 4.5 %copy-start.8 = (f32[8]{0:T(128)S(1)}, f32[8]{0:T(128)}, u32[]{:S(2)}) copy-start(f32[8]{0:T(128)} %loss_ref.9) | copy-start | bytes 100
  2.4 4.5 %copy-start.9 = (f32[1,1,2048]{2,1,0:T(1,128)S(1)}, f32[1,1,2048]{2,1,0:T(1,128)}, u32[]{:S(2)}) copy-start(f32[1,1,2048]{2,1,0:T(1,128)} %param.17) | copy-start | bytes 24580
  2.4 13.3 %copy-start.10 = (f32[8]{0:T(128)S(1)}, f32[8]{0:T(128)}, u32[]{:S(2)}) copy-start(f32[8]{0:T(128)} %pole_ref.5) | copy-start | bytes 100
  2.8 21.8 %collective-permute-start = (bf16[96,768]{1,0:T(8,128)(2,1)S(1)}, bf16[96,768]{1,0:T(8,128)(2,1)S(1)}, u32[]{:S(2)}, u32[]{:S(2)}) collective-permute-start(bf16[96,768]{1,0:T(8,128)(2,1)S(1)} %get-tuple-element.40), channel_id=1, source_target_pairs={{0,4},{4,0},{8,12},{12,8},{16,20},{20,16},{24,28},{28,24},{1,5},{5... | collective-permute-start | bytes 442376 | tf_op jit(solution)/shard_map/ppermute | solution.py:489
  3.3 21.3 %collective-permute-start.1 = (bf16[96,768]{1,0:T(8,128)(2,1)S(1)}, bf16[96,768]{1,0:T(8,128)(2,1)S(1)}, u32[]{:S(2)}, u32[]{:S(2)}) collective-permute-start(bf16[96,768]{1,0:T(8,128)(2,1)S(1)} %get-tuple-element.41), channel_id=1, source_target_pairs={{0,28},{4,8},{8,4},{12,16},{16,12},{20,24},{24,20},{28,0},{1,29},{... | collective-permute-start | bytes 442376 | tf_op jit(solution)/shard_map/ppermute | solution.py:489
  11.6 13.0 %collective-permute-start.2 = (bf16[8,768]{1,0:T(8,128)(2,1)S(1)}, bf16[8,768]{1,0:T(8,128)(2,1)S(1)}, u32[]{:S(2)}, u32[]{:S(2)}) collective-permute-start(bf16[8,768]{1,0:T(8,128)(2,1)S(1)} %get-tuple-element.42), channel_id=1, source_target_pairs={{0,1},{1,0},{2,3},{3,2},{4,5},{5,4},{6,7},{7,6},{8,9},{9,8},{10,11... | collective-permute-start | bytes 36872 | tf_op jit(solution)/shard_map/ppermute | solution.py:489
  13.2 11.4 %collective-permute-start.3 = (bf16[8,768]{1,0:T(8,128)(2,1)S(1)}, bf16[8,768]{1,0:T(8,128)(2,1)S(1)}, u32[]{:S(2)}, u32[]{:S(2)}) collective-permute-start(bf16[8,768]{1,0:T(8,128)(2,1)S(1)} %get-tuple-element.43), channel_id=1, source_target_pairs={{0,3},{1,2},{2,1},{3,0},{4,7},{5,6},{6,5},{7,4},{8,11},{9,10},{10,... | collective-permute-start | bytes 36872 | tf_op jit(solution)/shard_map/ppermute | solution.py:489
  25.5 10.6 %collective-permute-start.4 = (bf16[96,768]{1,0:T(8,128)(2,1)S(1)}, bf16[96,768]{1,0:T(8,128)(2,1)S(1)}, u32[]{:S(2)}, u32[]{:S(2)}) collective-permute-start(bf16[96,768]{1,0:T(8,128)(2,1)S(1)} %get-tuple-element.56), channel_id=1, source_target_pairs={{0,4},{4,0},{8,12},{12,8},{16,20},{20,16},{24,28},{28,24},{1,5},{5... | collective-permute-start | bytes 442376 | tf_op jit(solution)/shard_map/ppermute | solution.py:489
  25.6 10.6 %collective-permute-start.5 = (bf16[96,768]{1,0:T(8,128)(2,1)S(1)}, bf16[96,768]{1,0:T(8,128)(2,1)S(1)}, u32[]{:S(2)}, u32[]{:S(2)}) collective-permute-start(bf16[96,768]{1,0:T(8,128)(2,1)S(1)} %get-tuple-element.57), channel_id=1, source_target_pairs={{0,28},{4,8},{8,4},{12,16},{16,12},{20,24},{24,20},{28,0},{1,29},{... | collective-permute-start | bytes 442376 | tf_op jit(solution)/shard_map/ppermute | solution.py:489
  29.9 6.3 %slice-start = ((s8[4456448]{0:T(1024)(128)(4,1)}), s8[4194304]{0:T(1024)(128)(4,1)S(1)}, s32[]{:S(2)}) async-start(s8[4456448]{0:T(1024)(128)(4,1)} %bitcast.5), calls=%async_computation | async-start | bytes 8388608
  29.9 6.3 %slice-start.1 = ((s8[4456448]{0:T(1024)(128)(4,1)}), s8[262144]{0:T(1024)(128)(4,1)S(1)}, s32[]{:S(2)}) async-start(s8[4456448]{0:T(1024)(128)(4,1)} %bitcast.5), calls=%async_computation.1 | async-start | bytes 524288
  29.9 6.3 %copy-start.4 = (bf16[2,944,256]{2,1,0:T(8,128)(2,1)S(1)}, bf16[2,944,256]{2,1,0:T(8,128)(2,1)}, u32[]{:S(2)}) copy-start(bf16[2,944,256]{2,1,0:T(8,128)(2,1)} %constant.8.clone.mix_in) | copy-start | bytes 2899972
  29.9 6.3 %copy-start.5 = (bf16[16,32,256]{2,1,0:T(8,128)(2,1)S(1)}, bf16[16,32,256]{2,1,0:T(8,128)(2,1)}, u32[]{:S(2)}) copy-start(bf16[16,32,256]{2,1,0:T(8,128)(2,1)} %constant.7.clone.axial_in) | copy-start | bytes 786436
  29.9 6.3 %copy-start.11 = (s32[128,3]{0,1:T(4,128)S(1)}, s32[128,3]{0,1:T(4,128)}, u32[]{:S(2)}) copy-start(s32[128,3]{0,1:T(4,128)} %param.20) | copy-start | bytes 4612
  29.9 5.3 %collective-permute-start.6 = (bf16[8,768]{1,0:T(8,128)(2,1)S(1)}, bf16[8,768]{1,0:T(8,128)(2,1)S(1)}, u32[]{:S(2)}, u32[]{:S(2)}) collective-permute-start(bf16[8,768]{1,0:T(8,128)(2,1)S(1)} %get-tuple-element.58), channel_id=1, source_target_pairs={{0,1},{1,0},{2,3},{3,2},{4,5},{5,4},{6,7},{7,6},{8,9},{9,8},{10,11... | collective-permute-start | bytes 36872 | tf_op jit(solution)/shard_map/ppermute | solution.py:489
  30.6 5.5 %collective-permute-start.7 = (bf16[8,768]{1,0:T(8,128)(2,1)S(1)}, bf16[8,768]{1,0:T(8,128)(2,1)S(1)}, u32[]{:S(2)}, u32[]{:S(2)}) collective-permute-start(bf16[8,768]{1,0:T(8,128)(2,1)S(1)} %get-tuple-element.59), channel_id=1, source_target_pairs={{0,3},{1,2},{2,1},{3,0},{4,7},{5,6},{6,5},{7,4},{8,11},{9,10},{10,... | collective-permute-start | bytes 36872 | tf_op jit(solution)/shard_map/ppermute | solution.py:489
  49.6 1.3 %collective-permute-start.8 = (f32[32,256]{1,0:T(8,128)S(1)}, f32[32,256]{1,0:T(8,128)S(1)}, u32[]{:S(2)}, u32[]{:S(2)}) collective-permute-start(f32[32,256]{1,0:T(8,128)S(1)} %get-tuple-element.63), channel_id=1, source_target_pairs={{0,4},{4,0},{8,12},{12,8},{16,20},{20,16},{24,28},{28,24},{1,5},{5... | collective-permute-start | bytes 98312 | tf_op jit(solution)/shard_map/ppermute | solution.py:489
  50.8 4.8 %collective-permute-start.11 = (f32[32,256]{1,0:T(8,128)S(1)}, f32[32,256]{1,0:T(8,128)S(1)}, u32[]{:S(2)}, u32[]{:S(2)}) collective-permute-start(f32[32,256]{1,0:T(8,128)S(1)} %add.12), channel_id=1, source_target_pairs={{0,24},{4,28},{8,16},{12,20},{16,8},{20,12},{24,0},{28,4},{1,25},{... | collective-permute-start | bytes 98312 | tf_op jit(solution)/shard_map/ppermute | solution.py:593
  52.3 3.9 %collective-permute-start.10 = (f32[32,256]{1,0:T(8,128)S(1)}, f32[32,256]{1,0:T(8,128)S(1)}, u32[]{:S(2)}, u32[]{:S(2)}) collective-permute-start(f32[32,256]{1,0:T(8,128)S(1)} %add.12), channel_id=1, source_target_pairs={{0,16},{4,20},{8,24},{12,28},{16,0},{20,4},{24,8},{28,12},{1,17},{... | collective-permute-start | bytes 98312 | tf_op jit(solution)/shard_map/ppermute | solution.py:593
  53.8 3.9 %collective-permute-start.9 = (f32[32,256]{1,0:T(8,128)S(1)}, f32[32,256]{1,0:T(8,128)S(1)}, u32[]{:S(2)}, u32[]{:S(2)}) collective-permute-start(f32[32,256]{1,0:T(8,128)S(1)} %add.12), channel_id=1, source_target_pairs={{0,8},{4,12},{8,0},{12,4},{16,24},{20,28},{24,16},{28,20},{1,9},{5... | collective-permute-start | bytes 98312 | tf_op jit(solution)/shard_map/ppermute | solution.py:593
  (2 other events, 3.3 us)

commit v4 on v3

--- a/solution.py
+++ b/solution.py
@@ -263,28 +263,6 @@
         )
 
 
-def edge_places(slab, rows):
-    return (
-        (pl.ds(0, 1), pl.ds(0, rows)),
-        (pl.ds(slab - 1, 1), pl.ds(0, rows)),
-        (pl.ds(0, slab), pl.ds(0, 8)),
-        (pl.ds(0, slab), pl.ds(rows - 8, 8)),
-    )
-
-
-def first_edges(field, sx_one, sx_two, sy_one, sy_two, first, last, top, bottom, sems):
-    layers = (first, last, top, bottom)
-    copies = [
-        pltpu.make_async_copy(field.at[x, y], ref, sems.at[at])
-        for at, ((x, y), ref) in enumerate(zip(edge_places(*field.shape[:2]), layers))
-    ]
-    for copy in copies:
-        copy.start()
-    for copy in copies:
-        copy.wait()
-    edges(*layers, sx_one, sx_two, sy_one, sy_two)
-
-
 def fix_planes(first, last, top, bottom, c_first, c_last, c_top, c_bottom, x_halo, y_halo):
     slab, rows = top.shape[0], first.shape[1]
     final = top.shape[1] - 1
@@ -341,7 +319,7 @@
         copy.wait()
 
 
-def gather_nodes(cell_ref, loss_ref, states, cells, material, filter_out, picked):
+def gather_nodes(cell_ref, loss_ref, states, cells, material, order, filter_out, picked):
     nodes = cells.shape[1]
 
     def pick(k, carry):
@@ -367,18 +345,16 @@
         filter_out[:, part] = line[0:1, :] * inverse[:, part]
 
 
-def finish(cell_ref, loss_ref, anchor_ref, pressure_in, states_in, cells, material,
-           c_first, c_last, c_top, c_bottom, x_one, x_two, y_one, y_two,
-           pairs_in, axial_in, mix_in, pressure_out, partial, filter_out,
-           pressure, states, pairs, axial, mix, picked, planar, products_low, products_high, sems):
+def finish(anchor_ref, pressure_in, c_first, c_last, c_top, c_bottom, x_one, x_two, y_one, y_two,
+           pairs_in, axial_in, mix_in, pressure_out, partial,
+           pressure, pairs, axial, mix, planar, products_low, products_high, sems):
     slab, rows, nz = pressure.shape
     spheres = partial.shape[0]
     count = pairs.shape[0] // 2
     incoming = [
         pltpu.make_async_copy(source, target, sems.at[at])
         for at, (source, target) in enumerate((
-            (states_in, states), (pressure_in, pressure), (pairs_in, pairs),
-            (axial_in, axial), (mix_in, mix),
+            (pressure_in, pressure), (pairs_in, pairs), (axial_in, axial), (mix_in, mix),
         ))
     ]
     for copy in incoming:
@@ -386,8 +362,6 @@
     products = (products_low, products_high)
     products_high[...] = jnp.zeros_like(products_high)
     incoming[0].wait()
-    gather_nodes(cell_ref, loss_ref, states, cells, material, filter_out, picked)
-    incoming[1].wait()
     x_first = lax.axis_index("gx") * slab
     y_first = lax.axis_index("gy") * rows
     s_first = lax.axis_index("gy") * spheres
@@ -401,7 +375,7 @@
             pressure[x, one, :] = pressure[x, one, :] + term
     outgoing = pltpu.make_async_copy(pressure, pressure_out, sems.at[0])
     outgoing.start()
-    for copy in incoming[2:]:
+    for copy in incoming[1:]:
         copy.wait()
     limit = CUBE * CUBE
     odd_y = 2 * iota((CUBE, 2 * LANES), 0) - (CUBE - 1)
@@ -444,8 +418,8 @@
         products[1][at, 0 : count - LANES] = moment[:, LANES:]
         return carry
 
-    lax.fori_loop(0, spheres, across, 0, unroll=4)
-    lax.fori_loop(0, spheres, along, 0, unroll=8)
+    lax.fori_loop(0, spheres, across, 0, unroll=8)
+    lax.fori_loop(0, spheres, along, 0, unroll=16)
     result = jnp.zeros((spheres, COEFS), F32)
     for q in range(DEGREES):
         at = pl.ds(q, spheres, stride=DEGREES)
@@ -521,15 +495,16 @@
     layers = [pltpu.VMEM((1, rows, nz), F32)] * 2 + [pltpu.VMEM((slab, 8, nz), F32)] * 2
     layers += [pltpu.SemaphoreType.DMA((4,))]
     sx_one, sx_two, sy_one, sy_two = pl.pallas_call(
-        first_edges,
+        edges,
+        grid=(1,),
         out_shape=sends,
-        in_specs=[whole(pltpu.HBM)],
+        in_specs=[plane_at(0), plane_at(slab - 1), rows_at(0, 8), rows_at(rows - 8, 8)],
         out_specs=(whole(),) * 4,
-        scratch_shapes=layers,
         compiler_params=params(16),
         name="edges",
-    )(now)
+    )(now, now, now, now)
     x_one, x_two = swap(sx_one, "gx", 0), swap(sx_two, "gx", 1)
+    y_one, y_two = swap(sy_one, "gy", 0), swap(sy_two, "gy", 1)
     kinds, states = pl.pallas_call(
         node_maps,
         out_shape=(dense, dense),
@@ -539,8 +514,7 @@
         compiler_params=params(16),
         name="node_maps",
     )(cells, loss, cells, material, state)
-    sy_one, sy_two, kinds = after(sy_one, sy_two, kinds)
-    y_one, y_two = swap(sy_one, "gy", 0), swap(sy_two, "gy", 1)
+    (kinds,) = after(kinds)
     half, states = step(now, prev, kinds, states, (0, slab), 16, False)
     half, sx_one, sx_two, sy_one, sy_two = pl.pallas_call(
         fix_and_send,
@@ -561,33 +535,28 @@
         half, now, kinds, states, (slab // 2, slab), 16, True, first_part
     )
     fit_tables = (plane_pairs(slab), axial_windows(nz), mix_table())
-    pressure, partial, filter_out = pl.pallas_call(
+    pressure, partial = pl.pallas_call(
         finish,
         grid=(1,),
-        out_shape=(
-            block,
-            jax.ShapeDtypeStruct((spheres, COEFS), F32),
-            jax.ShapeDtypeStruct((1, nodes), F32),
-        ),
-        in_specs=[smem] * 3 + [whole(pl.ANY)] * 2 + [whole()] * 2 + edge_specs + [whole()] * 4
-        + [whole(pltpu.HBM)] * 3,
-        out_specs=(whole(pl.ANY), whole(), whole()),
-        scratch_shapes=[pltpu.VMEM(block.shape, F32), pltpu.VMEM(dense.shape, F32)]
+        out_shape=(block, jax.ShapeDtypeStruct((spheres, COEFS), F32)),
+        in_specs=[smem, whole(pl.ANY)] + edge_specs + [whole()] * 4 + [whole(pltpu.HBM)] * 3,
+        out_specs=(whole(pl.ANY), whole()),
+        scratch_shapes=[pltpu.VMEM(block.shape, F32)]
         + [pltpu.VMEM(table.shape, BF16) for table in fit_tables]
         + [
-            pltpu.VMEM((nodes, LANES), F32),
             pltpu.VMEM((spheres, fit_tables[0].shape[0] // 2, 2 * LANES), F32),
             pltpu.VMEM((spheres * DEGREES, LANES), F32),
             pltpu.VMEM((spheres * DEGREES, LANES), F32),
-            pltpu.SemaphoreType.DMA((5,)),
+            pltpu.SemaphoreType.DMA((4,)),
         ],
         compiler_params=params(32),
         name="finish",
     )(
-        cells, loss, anchors.T, partly, states, cells, material, *speeds,
+        anchors.T, partly, *speeds,
         x_one, x_two, y_one, y_two, *(jnp.asarray(table) for table in fit_tables),
     )
-    if lax.axis_size("gx") == 8:
+    eight = lax.axis_size("gx") == 8
+    if eight:
         partial = partial + swap(partial, "gx", 0)
         others = [
             lax.ppermute(partial, "gx", [(i, i ^ move) for i in range(8)]) for move in (2, 4, 6)
@@ -595,6 +564,15 @@
         coefficients = (partial + others[0]) + (others[1] + others[2])
     else:
         coefficients = jnp.sum(lax.all_gather(partial, "gx", axis=0, tiled=False), axis=0)
+    filter_out = pl.pallas_call(
+        gather_nodes,
+        out_shape=jax.ShapeDtypeStruct((1, nodes), F32),
+        in_specs=[smem] * 2 + [whole()] * 3 + [whole(pl.ANY)],
+        out_specs=whole(),
+        scratch_shapes=[pltpu.VMEM((nodes, LANES), F32)],
+        compiler_params=params(16),
+        name="gather_nodes",
+    )(cells, loss, states, cells, material, partial)
     return pressure, before, filter_out.reshape(filter_state.shape), coefficients
 
 

time: 58.5 us -> 51.2 us (0.88)
  local copies, waits for them, and re-layouts: 5.13 us -> 1.71 us
  waiting for transfers between devices: 5.5 us -> 2.13 us
    pallas_call x1, Pallas kernels: 13.4 us -> 7.36 us  [shards(): pl.pallas_call(finish, grid=(1,), out_shape=(block, jax.ShapeDtypeStruct(...]
    pallas_call x1 -> x2, Pallas kernels: 0.37 us -> 5.85 us  [the longest x1 5.68 us: shards(): pl.pallas_call(gather_nodes, out_shape=jax.ShapeDtypeStruct((1, nodes), F...]
    unnamed x28, local copies, waits for them, and re-layouts: 5.13 us -> 1.71 us
    ppermute x3, waiting for transfers between devices: 3.37 us -> 0.01 us  [shards(): lax.ppermute(partial, 'gx', [(i, i ^ move) for i in range(8)])]
  transfers between devices with their start and end apart: 12 -> 12, of which waited for: 5 -> 2; matrix products, arithmetic and copies ran while one was open for 0% -> 0% of each run, Pallas kernels for 30% -> 46%
where the time goes in v4:
time: 51.2 us; the launch traced here: 51 us
  Pallas kernels  31.6 us (62%)
  starting transfers between devices  14 us (27%)
  waiting for transfers between devices  2.13 us (4%)
  local copies, waits for them, and re-layouts  1.71 us (3%)
  between operations  0.87 us (2%)
  other arithmetic  0.63 us (1%)
    pallas_call x3, Pallas kernels, step(): pl.pallas_call(functools.partial(stencil, start, slab - 1), grid=(stop -...  12.9 us
    ppermute x9, starting transfers between devices, swap(): lax.ppermute(value, axis, [(i, (i + moves[i]) % count) for i in range(cou...  10.6 us
    pallas_call x1, Pallas kernels, shards(): pl.pallas_call(finish, grid=(1,), out_shape=(block, jax.ShapeDtypeStruct(...  7.36 us
    pallas_call x1, Pallas kernels, shards(): pl.pallas_call(gather_nodes, out_shape=jax.ShapeDtypeStruct((1, nodes), F...  5.68 us
    pallas_call x1, Pallas kernels, shards(): pl.pallas_call(node_maps, out_shape=(dense, dense), in_specs=[smem] * 2 +...  4.71 us
    ppermute x3, starting transfers between devices, shards(): lax.ppermute(partial, 'gx', [(i, i ^ move) for i in range(8)])  3.49 us
    ppermute x9, waiting for transfers between devices, swap(): lax.ppermute(value, axis, [(i, (i + moves[i]) % count) for i in range(cou...  2.12 us
    unnamed x28, local copies, waits for them, and re-layouts  1.71 us
  transfers between devices with their start and end apart: 12, of which 2 were waited for; matrix products, arithmetic and copies ran while one was open for 0% of the time, Pallas kernels for 46%

profile of v4, /device:TPU:0, one launch (start us, length us, event | category | flops | bytes accessed | tf_op | source)
XLA Modules:
  0.0 51.0 jit_solution(17563456939960983640)
XLA Ops:
  0.6 1.7 %copy-done = f32[8,96,768]{2,1,0:T(8,128)S(1)} copy-done((f32[8,96,768]{2,1,0:T(8,128)S(1)}, f32[8,96,768]{2,1,0:T(8,128)}, u32[]{:S(2)}) %copy-start) | copy-done | bytes 2359320
  2.4 0.2 edges.1
  2.5 0.5 %collective-permute-start = (bf16[96,768]{1,0:T(8,128)(2,1)S(1)}, bf16[96,768]{1,0:T(8,128)(2,1)S(1)}, u32[]{:S(2)}, u32[]{:S(2)}) collective-permute-start(bf16[96,768]{1,0:T(8,128)(2,1)S(1)} %get-tuple-element.33), channel_id=1, source_target_pairs={{0,4},{4,0},{8,12},{12,8},{16,20},{20,16},{24,28},{28,24},{1,5},{5... | collective-permute-start | bytes 442376 | tf_op jit(solution)/shard_map/ppermute | solution.py:463
  3.0 3.6 %collective-permute-start.1 = (bf16[96,768]{1,0:T(8,128)(2,1)S(1)}, bf16[96,768]{1,0:T(8,128)(2,1)S(1)}, u32[]{:S(2)}, u32[]{:S(2)}) collective-permute-start(bf16[96,768]{1,0:T(8,128)(2,1)S(1)} %get-tuple-element.34), channel_id=1, source_target_pairs={{0,28},{4,8},{8,4},{12,16},{16,12},{20,24},{24,20},{28,0},{1,29},{... | collective-permute-start | bytes 442376 | tf_op jit(solution)/shard_map/ppermute | solution.py:463
  6.6 1.6 %collective-permute-start.2 = (bf16[8,768]{1,0:T(8,128)(2,1)S(1)}, bf16[8,768]{1,0:T(8,128)(2,1)S(1)}, u32[]{:S(2)}, u32[]{:S(2)}) collective-permute-start(bf16[8,768]{1,0:T(8,128)(2,1)S(1)} %get-tuple-element.35), channel_id=1, source_target_pairs={{0,1},{1,0},{2,3},{3,2},{4,5},{5,4},{6,7},{7,6},{8,9},{9,8},{10,11... | collective-permute-start | bytes 36872 | tf_op jit(solution)/shard_map/ppermute | solution.py:463
  8.2 2.5 %collective-permute-start.3 = (bf16[8,768]{1,0:T(8,128)(2,1)S(1)}, bf16[8,768]{1,0:T(8,128)(2,1)S(1)}, u32[]{:S(2)}, u32[]{:S(2)}) collective-permute-start(bf16[8,768]{1,0:T(8,128)(2,1)S(1)} %get-tuple-element.36), channel_id=1, source_target_pairs={{0,3},{1,2},{2,1},{3,0},{4,7},{5,6},{6,5},{7,4},{8,11},{9,10},{10,... | collective-permute-start | bytes 36872 | tf_op jit(solution)/shard_map/ppermute | solution.py:463
  10.7 4.7 %node_maps.1 = (f32[4608,128]{1,0:T(8,128)S(1)}, f32[4608,128]{1,0:T(8,128)S(1)}) custom-call(s32[1,2048]{1,0:T(1,128)S(1)} %bitcast.7, f32[8]{0:T(128)S(1)} %copy-done.8, s32[1,2048]{1,0:T(1,128)S(1)} %bitcast.8, s32[1,2048]{1,0:T(1,128)S(1)} %bitcast.11, f32[1,2048]{1,0:T(1,128)S(1)} %bitcast.13), custom_call_target="tpu_custom_call" | custom-call | tf_op jit(solution)/shard_map/node_maps/pallas_call | solution.py:508
  15.4 5.5 %stencil.3 = (f32[8,96,768]{2,1,0:T(8,128)S(1)}, f32[4608,128]{1,0:T(8,128)S(1)}) custom-call(f32[8]{0:T(128)S(1)} %copy-done.10, f32[8]{0:T(128)S(1)} %copy-done.8, f32[8,96,768]{2,1,0:T(8,128)S(1)} %copy-done.1, f32[8,96,768]{2,1,0:T(8,128)S(1)} %copy-done.1, f32[8,96,768]{2,1,0:T(8,128)S(1)} %copy-done.1, f32[8,96,768]{2,1,0:T(8,128)S(1)} %copy-done.3, ...), custom_call_target="tpu_custom_call" | custom-call | tf_op jit(solution)/shard_map/stencil/pallas_call | solution.py:483
  21.0 0.9 %fix_and_send.1 = (f32[8,96,768]{2,1,0:T(8,128)S(1)}, bf16[96,768]{1,0:T(8,128)(2,1)S(1)}, bf16[96,768]{1,0:T(8,128)(2,1)S(1)}, bf16[8,768]{1,0:T(8,128)(2,1)S(1)}, bf16[8,768]{1,0:T(8,128)(2,1)S(1)}) custom-call(f32[8,96,768]{2,1,0:T(8,128)S(1)} %get-tuple-element.32.field_in, bf16[8,96,768]{2,1,0:T(8,128)(2,1)S(1)} %copy-done.2, ...), custom_call_target="tpu_custom_call", output_to_operand_aliasing={{0}: (0, {})} | custom-call | tf_op jit(solution)/shard_map/fix_and_send/pallas_call | solution.py:519
  21.9 0.1 collective-permute-start.4
  21.9 0.6 %collective-permute-start.5 = (bf16[96,768]{1,0:T(8,128)(2,1)S(1)}, bf16[96,768]{1,0:T(8,128)(2,1)S(1)}, u32[]{:S(2)}, u32[]{:S(2)}) collective-permute-start(bf16[96,768]{1,0:T(8,128)(2,1)S(1)} %get-tuple-element.49), channel_id=1, source_target_pairs={{0,28},{4,8},{8,4},{12,16},{16,12},{20,24},{24,20},{28,0},{1,29},{... | collective-permute-start | bytes 442376 | tf_op jit(solution)/shard_map/ppermute | solution.py:463
  22.6 3.7 %stencil.4 = (f32[8,96,768]{2,1,0:T(8,128)S(1)}, f32[4608,128]{1,0:T(8,128)S(1)}, f32[8,96,768]{2,1,0:T(8,128)}) custom-call(f32[8]{0:T(128)S(1)} %copy-done.10, f32[8]{0:T(128)S(1)} %copy-done.8, f32[8,96,768]{2,1,0:T(8,128)S(1)} %get-tuple-element.37.below.here_ref.above, f32[8,96,768]{2,1,0:T(8,128)S(1)} %get-tuple-element.37.below.here_ref.above, ...), custom_call_target="tpu_custom_call" | custom-call | tf_op jit(solution)/shard_map/stencil/pallas_call | solution.py:483
  26.3 0.7 %collective-permute-start.6 = (bf16[8,768]{1,0:T(8,128)(2,1)S(1)}, bf16[8,768]{1,0:T(8,128)(2,1)S(1)}, u32[]{:S(2)}, u32[]{:S(2)}) collective-permute-start(bf16[8,768]{1,0:T(8,128)(2,1)S(1)} %get-tuple-element.50), channel_id=1, source_target_pairs={{0,1},{1,0},{2,3},{3,2},{4,5},{5,4},{6,7},{7,6},{8,9},{9,8},{10,11... | collective-permute-start | bytes 36872 | tf_op jit(solution)/shard_map/ppermute | solution.py:463
  27.0 0.9 %collective-permute-start.7 = (bf16[8,768]{1,0:T(8,128)(2,1)S(1)}, bf16[8,768]{1,0:T(8,128)(2,1)S(1)}, u32[]{:S(2)}, u32[]{:S(2)}) collective-permute-start(bf16[8,768]{1,0:T(8,128)(2,1)S(1)} %get-tuple-element.51), channel_id=1, source_target_pairs={{0,3},{1,2},{2,1},{3,0},{4,7},{5,6},{6,5},{7,4},{8,11},{9,10},{10,... | collective-permute-start | bytes 36872 | tf_op jit(solution)/shard_map/ppermute | solution.py:463
  27.9 3.7 %stencil.5 = (f32[8,96,768]{2,1,0:T(8,128)S(1)}, f32[4608,128]{1,0:T(8,128)S(1)}, f32[8,96,768]{2,1,0:T(8,128)}) custom-call(f32[8]{0:T(128)S(1)} %copy-done.10, f32[8]{0:T(128)S(1)} %copy-done.8, f32[8,96,768]{2,1,0:T(8,128)S(1)} %get-tuple-element.37.below.here_ref.above, ...), custom_call_target="tpu_custom_call", output_to_operand_aliasing={{0}: (9, {}), {1}: (10, {}), {2}: (11, {})} | custom-call | tf_op jit(solution)/shard_map/stencil/pallas_call | solution.py:483
  31.6 0.9 %collective-permute-done.7.y_two = bf16[8,768]{1,0:T(8,128)(2,1)S(1)} collective-permute-done((bf16[8,768]{1,0:T(8,128)(2,1)S(1)}, bf16[8,768]{1,0:T(8,128)(2,1)S(1)}, u32[]{:S(2)}, u32[]{:S(2)}) %collective-permute-start.7) | collective-permute-done | bytes 12320 | tf_op jit(solution)/shard_map/ppermute | solution.py:463
  32.6 7.4 %finish.1 = (f32[8,96,768]{2,1,0:T(8,128)}, f32[32,256]{1,0:T(8,128)S(1)}) custom-call(s32[3,128]{1,0:T(4,128)S(1)} %bitcast.14, f32[8,96,768]{2,1,0:T(8,128)S(1)} %get-tuple-element.47.pressure_in, bf16[8,96,768]{2,1,0:T(8,128)(2,1)S(1)} %copy-done.2, bf16[8,96,768]{2,1,0:T(8,128)(2,1)S(1)} %copy-done.2, bf16[8,96,768]{2,1,0:T(8,128)(2,1)S(1)} %copy-done.2, ...), custom_call_target="tpu_custom_call" | custom-call | tf_op jit(solution)/shard_map/finish/pallas_call | solution.py:538
  39.9 0.1 collective-permute-start.8
  40.0 1.2 %collective-permute-done.8 = f32[32,256]{1,0:T(8,128)S(1)} collective-permute-done((f32[32,256]{1,0:T(8,128)S(1)}, f32[32,256]{1,0:T(8,128)S(1)}, u32[]{:S(2)}, u32[]{:S(2)}) %collective-permute-start.8) | collective-permute-done | bytes 32800 | tf_op jit(solution)/shard_map/ppermute | solution.py:463
  41.2 1.4 %collective-permute-start.11 = (f32[32,256]{1,0:T(8,128)S(1)}, f32[32,256]{1,0:T(8,128)S(1)}, u32[]{:S(2)}, u32[]{:S(2)}) collective-permute-start(f32[32,256]{1,0:T(8,128)S(1)} %add.12.order), channel_id=1, source_target_pairs={{0,24},{4,28},{8,16},{12,20},{16,8},{20,12},{24,0},{28,4},{1,25},{... | collective-permute-start | bytes 98312 | tf_op jit(solution)/shard_map/ppermute | solution.py:562
  42.6 1.5 %collective-permute-start.10 = (f32[32,256]{1,0:T(8,128)S(1)}, f32[32,256]{1,0:T(8,128)S(1)}, u32[]{:S(2)}, u32[]{:S(2)}) collective-permute-start(f32[32,256]{1,0:T(8,128)S(1)} %add.12.order), channel_id=1, source_target_pairs={{0,16},{4,20},{8,24},{12,28},{16,0},{20,4},{24,8},{28,12},{1,17},{... | collective-permute-start | bytes 98312 | tf_op jit(solution)/shard_map/ppermute | solution.py:562
  44.2 0.5 %collective-permute-start.9 = (f32[32,256]{1,0:T(8,128)S(1)}, f32[32,256]{1,0:T(8,128)S(1)}, u32[]{:S(2)}, u32[]{:S(2)}) collective-permute-start(f32[32,256]{1,0:T(8,128)S(1)} %add.12.order), channel_id=1, source_target_pairs={{0,8},{4,12},{8,0},{12,4},{16,24},{20,28},{24,16},{28,20},{1,9},{5... | collective-permute-start | bytes 98312 | tf_op jit(solution)/shard_map/ppermute | solution.py:562
  44.7 5.7 %gather_nodes.1 = f32[1,2048]{1,0:T(1,128)} custom-call(s32[1,2048]{1,0:T(1,128)S(1)} %bitcast.9, f32[8]{0:T(128)S(1)} %copy-done.8, f32[4608,128]{1,0:T(8,128)S(1)} %get-tuple-element.54.states, s32[1,2048]{1,0:T(1,128)S(1)} %bitcast.10, s32[1,2048]{1,0:T(1,128)S(1)} %bitcast.12, f32[32,256]{1,0:T(8,128)S(1)} %add.12.order), custom_call_target="tpu_custom_call" | custom-call | tf_op jit(solution)/shard_map/gather_nodes/pallas_call | solution.py:567
  50.4 0.6 %add_add_fusion = f32[32,256]{1,0:T(8,128)} fusion(f32[32,256]{1,0:T(8,128)S(1)} %collective-permute-done.10, f32[32,256]{1,0:T(8,128)S(1)} %collective-permute-done.11, f32[32,256]{1,0:T(8,128)S(1)} %add.12.order, f32[32,256]{1,0:T(8,128)S(1)} %collective-permute-done.9), kind=kLoop, calls=%fused_computation | loop fusion | flops 24576 | bytes 163840 | tf_op jit(solution)/shard_map/add | solution.py:564
  (39 shorter events, 0.1 us)
Async XLA Ops:
  2.3 8.3 %copy-start.6 = (s32[1,1,2048]{2,1,0:T(1,128)S(1)}, s32[1,1,2048]{2,1,0:T(1,128)}, u32[]{:S(2)}) copy-start(s32[1,1,2048]{2,1,0:T(1,128)} %param.15) | copy-start | bytes 24580
  2.3 8.3 %copy-start.7 = (s32[1,1,2048]{2,1,0:T(1,128)S(1)}, s32[1,1,2048]{2,1,0:T(1,128)}, u32[]{:S(2)}) copy-start(s32[1,1,2048]{2,1,0:T(1,128)} %param.16) | copy-start | bytes 24580
  2.3 8.3 %copy-start.8 = (f32[8]{0:T(128)S(1)}, f32[8]{0:T(128)}, u32[]{:S(2)}) copy-start(f32[8]{0:T(128)} %loss_ref.9) | copy-start | bytes 100
  2.3 8.4 %copy-start.9 = (f32[1,1,2048]{2,1,0:T(1,128)S(1)}, f32[1,1,2048]{2,1,0:T(1,128)}, u32[]{:S(2)}) copy-start(f32[1,1,2048]{2,1,0:T(1,128)} %param.17) | copy-start | bytes 24580
  2.3 13.1 %copy-start.1 = (f32[8,96,768]{2,1,0:T(8,128)S(1)}, f32[8,96,768]{2,1,0:T(8,128)}, u32[]{:S(2)}) copy-start(f32[8,96,768]{2,1,0:T(8,128)} %previous.5) | copy-start | bytes 7077892
  2.3 13.1 %copy-start.2 = (bf16[8,96,768]{2,1,0:T(8,128)(2,1)S(1)}, bf16[8,96,768]{2,1,0:T(8,128)(2,1)}, u32[]{:S(2)}) copy-start(bf16[8,96,768]{2,1,0:T(8,128)(2,1)} %c_bottom.3) | copy-start | bytes 3538948
  2.3 13.1 %copy-start.3 = (f32[8,96,768]{2,1,0:T(8,128)S(1)}, f32[8,96,768]{2,1,0:T(8,128)}, u32[]{:S(2)}) copy-start(f32[8,96,768]{2,1,0:T(8,128)} %previous.3) | copy-start | bytes 7077892
  2.3 13.1 %copy-start.10 = (f32[8]{0:T(128)S(1)}, f32[8]{0:T(128)}, u32[]{:S(2)}) copy-start(f32[8]{0:T(128)} %pole_ref.5) | copy-start | bytes 100
  2.5 18.5 %collective-permute-start = (bf16[96,768]{1,0:T(8,128)(2,1)S(1)}, bf16[96,768]{1,0:T(8,128)(2,1)S(1)}, u32[]{:S(2)}, u32[]{:S(2)}) collective-permute-start(bf16[96,768]{1,0:T(8,128)(2,1)S(1)} %get-tuple-element.33), channel_id=1, source_target_pairs={{0,4},{4,0},{8,12},{12,8},{16,20},{20,16},{24,28},{28,24},{1,5},{5... | collective-permute-start | bytes 442376 | tf_op jit(solution)/shard_map/ppermute | solution.py:463
  3.0 17.9 %collective-permute-start.1 = (bf16[96,768]{1,0:T(8,128)(2,1)S(1)}, bf16[96,768]{1,0:T(8,128)(2,1)S(1)}, u32[]{:S(2)}, u32[]{:S(2)}) collective-permute-start(bf16[96,768]{1,0:T(8,128)(2,1)S(1)} %get-tuple-element.34), channel_id=1, source_target_pairs={{0,28},{4,8},{8,4},{12,16},{16,12},{20,24},{24,20},{28,0},{1,29},{... | collective-permute-start | bytes 442376 | tf_op jit(solution)/shard_map/ppermute | solution.py:463
  6.6 14.4 %collective-permute-start.2 = (bf16[8,768]{1,0:T(8,128)(2,1)S(1)}, bf16[8,768]{1,0:T(8,128)(2,1)S(1)}, u32[]{:S(2)}, u32[]{:S(2)}) collective-permute-start(bf16[8,768]{1,0:T(8,128)(2,1)S(1)} %get-tuple-element.35), channel_id=1, source_target_pairs={{0,1},{1,0},{2,3},{3,2},{4,5},{5,4},{6,7},{7,6},{8,9},{9,8},{10,11... | collective-permute-start | bytes 36872 | tf_op jit(solution)/shard_map/ppermute | solution.py:463
  8.2 12.8 %collective-permute-start.3 = (bf16[8,768]{1,0:T(8,128)(2,1)S(1)}, bf16[8,768]{1,0:T(8,128)(2,1)S(1)}, u32[]{:S(2)}, u32[]{:S(2)}) collective-permute-start(bf16[8,768]{1,0:T(8,128)(2,1)S(1)} %get-tuple-element.36), channel_id=1, source_target_pairs={{0,3},{1,2},{2,1},{3,0},{4,7},{5,6},{6,5},{7,4},{8,11},{9,10},{10,... | collective-permute-start | bytes 36872 | tf_op jit(solution)/shard_map/ppermute | solution.py:463
  21.9 10.7 %collective-permute-start.4 = (bf16[96,768]{1,0:T(8,128)(2,1)S(1)}, bf16[96,768]{1,0:T(8,128)(2,1)S(1)}, u32[]{:S(2)}, u32[]{:S(2)}) collective-permute-start(bf16[96,768]{1,0:T(8,128)(2,1)S(1)} %get-tuple-element.48), channel_id=1, source_target_pairs={{0,4},{4,0},{8,12},{12,8},{16,20},{20,16},{24,28},{28,24},{1,5},{5... | collective-permute-start | bytes 442376 | tf_op jit(solution)/shard_map/ppermute | solution.py:463
  21.9 10.6 %collective-permute-start.5 = (bf16[96,768]{1,0:T(8,128)(2,1)S(1)}, bf16[96,768]{1,0:T(8,128)(2,1)S(1)}, u32[]{:S(2)}, u32[]{:S(2)}) collective-permute-start(bf16[96,768]{1,0:T(8,128)(2,1)S(1)} %get-tuple-element.49), channel_id=1, source_target_pairs={{0,28},{4,8},{8,4},{12,16},{16,12},{20,24},{24,20},{28,0},{1,29},{... | collective-permute-start | bytes 442376 | tf_op jit(solution)/shard_map/ppermute | solution.py:463
  26.2 6.3 %slice-start.1 = ((s8[4456448]{0:T(1024)(128)(4,1)}), s8[262144]{0:T(1024)(128)(4,1)S(1)}, s32[]{:S(2)}) async-start(s8[4456448]{0:T(1024)(128)(4,1)} %bitcast.5), calls=%async_computation.1 | async-start | bytes 524288
  26.2 6.3 %copy-start.4 = (bf16[2,944,256]{2,1,0:T(8,128)(2,1)S(1)}, bf16[2,944,256]{2,1,0:T(8,128)(2,1)}, u32[]{:S(2)}) copy-start(bf16[2,944,256]{2,1,0:T(8,128)(2,1)} %constant.8.clone.mix_in) | copy-start | bytes 2899972
  26.2 6.3 %copy-start.5 = (bf16[16,32,256]{2,1,0:T(8,128)(2,1)S(1)}, bf16[16,32,256]{2,1,0:T(8,128)(2,1)}, u32[]{:S(2)}) copy-start(bf16[16,32,256]{2,1,0:T(8,128)(2,1)} %constant.7.clone.axial_in) | copy-start | bytes 786436
  26.3 6.3 %copy-start.11 = (s32[128,3]{0,1:T(4,128)S(1)}, s32[128,3]{0,1:T(4,128)}, u32[]{:S(2)}) copy-start(s32[128,3]{0,1:T(4,128)} %param.20) | copy-start | bytes 4612
  26.3 5.3 %collective-permute-start.6 = (bf16[8,768]{1,0:T(8,128)(2,1)S(1)}, bf16[8,768]{1,0:T(8,128)(2,1)S(1)}, u32[]{:S(2)}, u32[]{:S(2)}) collective-permute-start(bf16[8,768]{1,0:T(8,128)(2,1)S(1)} %get-tuple-element.50), channel_id=1, source_target_pairs={{0,1},{1,0},{2,3},{3,2},{4,5},{5,4},{6,7},{7,6},{8,9},{9,8},{10,11... | collective-permute-start | bytes 36872 | tf_op jit(solution)/shard_map/ppermute | solution.py:463
  27.0 5.5 %collective-permute-start.7 = (bf16[8,768]{1,0:T(8,128)(2,1)S(1)}, bf16[8,768]{1,0:T(8,128)(2,1)S(1)}, u32[]{:S(2)}, u32[]{:S(2)}) collective-permute-start(bf16[8,768]{1,0:T(8,128)(2,1)S(1)} %get-tuple-element.51), channel_id=1, source_target_pairs={{0,3},{1,2},{2,1},{3,0},{4,7},{5,6},{6,5},{7,4},{8,11},{9,10},{10,... | collective-permute-start | bytes 36872 | tf_op jit(solution)/shard_map/ppermute | solution.py:463
  39.9 1.3 %collective-permute-start.8 = (f32[32,256]{1,0:T(8,128)S(1)}, f32[32,256]{1,0:T(8,128)S(1)}, u32[]{:S(2)}, u32[]{:S(2)}) collective-permute-start(f32[32,256]{1,0:T(8,128)S(1)} %get-tuple-element.55), channel_id=1, source_target_pairs={{0,4},{4,0},{8,12},{12,8},{16,20},{20,16},{24,28},{28,24},{1,5},{5... | collective-permute-start | bytes 98312 | tf_op jit(solution)/shard_map/ppermute | solution.py:463
  41.2 9.2 %collective-permute-start.11 = (f32[32,256]{1,0:T(8,128)S(1)}, f32[32,256]{1,0:T(8,128)S(1)}, u32[]{:S(2)}, u32[]{:S(2)}) collective-permute-start(f32[32,256]{1,0:T(8,128)S(1)} %add.12.order), channel_id=1, source_target_pairs={{0,24},{4,28},{8,16},{12,20},{16,8},{20,12},{24,0},{28,4},{1,25},{... | collective-permute-start | bytes 98312 | tf_op jit(solution)/shard_map/ppermute | solution.py:562
  42.6 7.7 %collective-permute-start.10 = (f32[32,256]{1,0:T(8,128)S(1)}, f32[32,256]{1,0:T(8,128)S(1)}, u32[]{:S(2)}, u32[]{:S(2)}) collective-permute-start(f32[32,256]{1,0:T(8,128)S(1)} %add.12.order), channel_id=1, source_target_pairs={{0,16},{4,20},{8,24},{12,28},{16,0},{20,4},{24,8},{28,12},{1,17},{... | collective-permute-start | bytes 98312 | tf_op jit(solution)/shard_map/ppermute | solution.py:562
  44.2 6.2 %collective-permute-start.9 = (f32[32,256]{1,0:T(8,128)S(1)}, f32[32,256]{1,0:T(8,128)S(1)}, u32[]{:S(2)}, u32[]{:S(2)}) collective-permute-start(f32[32,256]{1,0:T(8,128)S(1)} %add.12.order), channel_id=1, source_target_pairs={{0,8},{4,12},{8,0},{12,4},{16,24},{20,28},{24,16},{28,20},{1,9},{5... | collective-permute-start | bytes 98312 | tf_op jit(solution)/shard_map/ppermute | solution.py:562
  (2 other events, 7.9 us)

commit v5 on v4

--- a/solution.py
+++ b/solution.py
@@ -145,7 +145,7 @@
     ones = jnp.ones((GROUP, GROUP), BF16)
     spread = jnp.where(eye, row, 0.0)
     out, rest = None, spread
-    for _ in range(3):
+    for _ in range(2):
         part = rest.astype(BF16)
         rest = rest - part.astype(F32)
         term = dot(part, ones)
@@ -336,7 +336,7 @@
         part = slice(at * GROUP, (at + 1) * GROUP)
         rest = jnp.where(columns_small(lane_row[:, part]) == lane, picked[part, :], 0.0)
         line = jnp.zeros((8, GROUP), F32)
-        for _ in range(3):
+        for _ in range(2):
             piece = rest.astype(BF16)
             rest = rest - piece.astype(F32)
             line = line + lax.dot_general(

time: 51.2 us -> 50.8 us (level)
  transfers between devices with their start and end apart: 12 -> 12, of which waited for: 2 -> 2; matrix products, arithmetic and copies ran while one was open for 0% -> 0% of each run, Pallas kernels for 46% -> 45%
where the time goes in v5:
time: 50.8 us; the launch traced here: 50.6 us
  Pallas kernels  31.2 us (61%)
  starting transfers between devices  14 us (28%)
  waiting for transfers between devices  2.13 us (4%)
  local copies, waits for them, and re-layouts  1.71 us (3%)
  between operations  0.87 us (2%)
  other arithmetic  0.63 us (1%)
    pallas_call x3, Pallas kernels, step(): pl.pallas_call(functools.partial(stencil, start, slab - 1), grid=(stop -...  12.9 us
    ppermute x9, starting transfers between devices, swap(): lax.ppermute(value, axis, [(i, (i + moves[i]) % count) for i in range(cou...  10.6 us
    pallas_call x1, Pallas kernels, shards(): pl.pallas_call(finish, grid=(1,), out_shape=(block, jax.ShapeDtypeStruct(...  7.35 us
    pallas_call x1, Pallas kernels, shards(): pl.pallas_call(gather_nodes, out_shape=jax.ShapeDtypeStruct((1, nodes), F...  5.43 us
    pallas_call x1, Pallas kernels, shards(): pl.pallas_call(node_maps, out_shape=(dense, dense), in_specs=[smem] * 2 +...  4.58 us
    ppermute x3, starting transfers between devices, shards(): lax.ppermute(partial, 'gx', [(i, i ^ move) for i in range(8)])  3.49 us
    ppermute x9, waiting for transfers between devices, swap(): lax.ppermute(value, axis, [(i, (i + moves[i]) % count) for i in range(cou...  2.12 us
    unnamed x28, local copies, waits for them, and re-layouts  1.71 us
  transfers between devices with their start and end apart: 12, of which 2 were waited for; matrix products, arithmetic and copies ran while one was open for 0% of the time, Pallas kernels for 45%

profile of v5, /device:TPU:0, one launch (start us, length us, event | category | flops | bytes accessed | tf_op | source)
XLA Modules:
  0.0 50.6 jit_solution(11802807379505099577)
XLA Ops:
  0.6 1.7 %copy-done = f32[8,96,768]{2,1,0:T(8,128)S(1)} copy-done((f32[8,96,768]{2,1,0:T(8,128)S(1)}, f32[8,96,768]{2,1,0:T(8,128)}, u32[]{:S(2)}) %copy-start) | copy-done | bytes 2359320
  2.4 0.2 edges.1
  2.5 0.5 %collective-permute-start = (bf16[96,768]{1,0:T(8,128)(2,1)S(1)}, bf16[96,768]{1,0:T(8,128)(2,1)S(1)}, u32[]{:S(2)}, u32[]{:S(2)}) collective-permute-start(bf16[96,768]{1,0:T(8,128)(2,1)S(1)} %get-tuple-element.33), channel_id=1, source_target_pairs={{0,4},{4,0},{8,12},{12,8},{16,20},{20,16},{24,28},{28,24},{1,5},{5... | collective-permute-start | bytes 442376 | tf_op jit(solution)/shard_map/ppermute | solution.py:463
  3.0 3.6 %collective-permute-start.1 = (bf16[96,768]{1,0:T(8,128)(2,1)S(1)}, bf16[96,768]{1,0:T(8,128)(2,1)S(1)}, u32[]{:S(2)}, u32[]{:S(2)}) collective-permute-start(bf16[96,768]{1,0:T(8,128)(2,1)S(1)} %get-tuple-element.34), channel_id=1, source_target_pairs={{0,28},{4,8},{8,4},{12,16},{16,12},{20,24},{24,20},{28,0},{1,29},{... | collective-permute-start | bytes 442376 | tf_op jit(solution)/shard_map/ppermute | solution.py:463
  6.6 1.6 %collective-permute-start.2 = (bf16[8,768]{1,0:T(8,128)(2,1)S(1)}, bf16[8,768]{1,0:T(8,128)(2,1)S(1)}, u32[]{:S(2)}, u32[]{:S(2)}) collective-permute-start(bf16[8,768]{1,0:T(8,128)(2,1)S(1)} %get-tuple-element.35), channel_id=1, source_target_pairs={{0,1},{1,0},{2,3},{3,2},{4,5},{5,4},{6,7},{7,6},{8,9},{9,8},{10,11... | collective-permute-start | bytes 36872 | tf_op jit(solution)/shard_map/ppermute | solution.py:463
  8.2 2.5 %collective-permute-start.3 = (bf16[8,768]{1,0:T(8,128)(2,1)S(1)}, bf16[8,768]{1,0:T(8,128)(2,1)S(1)}, u32[]{:S(2)}, u32[]{:S(2)}) collective-permute-start(bf16[8,768]{1,0:T(8,128)(2,1)S(1)} %get-tuple-element.36), channel_id=1, source_target_pairs={{0,3},{1,2},{2,1},{3,0},{4,7},{5,6},{6,5},{7,4},{8,11},{9,10},{10,... | collective-permute-start | bytes 36872 | tf_op jit(solution)/shard_map/ppermute | solution.py:463
  10.7 4.6 %node_maps.1 = (f32[4608,128]{1,0:T(8,128)S(1)}, f32[4608,128]{1,0:T(8,128)S(1)}) custom-call(s32[1,2048]{1,0:T(1,128)S(1)} %bitcast.7, f32[8]{0:T(128)S(1)} %copy-done.8, s32[1,2048]{1,0:T(1,128)S(1)} %bitcast.8, s32[1,2048]{1,0:T(1,128)S(1)} %bitcast.11, f32[1,2048]{1,0:T(1,128)S(1)} %bitcast.13), custom_call_target="tpu_custom_call" | custom-call | tf_op jit(solution)/shard_map/node_maps/pallas_call | solution.py:508
  15.3 5.5 %stencil.3 = (f32[8,96,768]{2,1,0:T(8,128)S(1)}, f32[4608,128]{1,0:T(8,128)S(1)}) custom-call(f32[8]{0:T(128)S(1)} %copy-done.10, f32[8]{0:T(128)S(1)} %copy-done.8, f32[8,96,768]{2,1,0:T(8,128)S(1)} %copy-done.1, f32[8,96,768]{2,1,0:T(8,128)S(1)} %copy-done.1, f32[8,96,768]{2,1,0:T(8,128)S(1)} %copy-done.1, f32[8,96,768]{2,1,0:T(8,128)S(1)} %copy-done.3, ...), custom_call_target="tpu_custom_call" | custom-call | tf_op jit(solution)/shard_map/stencil/pallas_call | solution.py:483
  20.9 0.9 %fix_and_send.1 = (f32[8,96,768]{2,1,0:T(8,128)S(1)}, bf16[96,768]{1,0:T(8,128)(2,1)S(1)}, bf16[96,768]{1,0:T(8,128)(2,1)S(1)}, bf16[8,768]{1,0:T(8,128)(2,1)S(1)}, bf16[8,768]{1,0:T(8,128)(2,1)S(1)}) custom-call(f32[8,96,768]{2,1,0:T(8,128)S(1)} %get-tuple-element.32.field_in, bf16[8,96,768]{2,1,0:T(8,128)(2,1)S(1)} %copy-done.2, ...), custom_call_target="tpu_custom_call", output_to_operand_aliasing={{0}: (0, {})} | custom-call | tf_op jit(solution)/shard_map/fix_and_send/pallas_call | solution.py:519
  21.7 0.1 collective-permute-start.4
  21.8 0.6 %collective-permute-start.5 = (bf16[96,768]{1,0:T(8,128)(2,1)S(1)}, bf16[96,768]{1,0:T(8,128)(2,1)S(1)}, u32[]{:S(2)}, u32[]{:S(2)}) collective-permute-start(bf16[96,768]{1,0:T(8,128)(2,1)S(1)} %get-tuple-element.49), channel_id=1, source_target_pairs={{0,28},{4,8},{8,4},{12,16},{16,12},{20,24},{24,20},{28,0},{1,29},{... | collective-permute-start | bytes 442376 | tf_op jit(solution)/shard_map/ppermute | solution.py:463
  22.4 3.7 %stencil.4 = (f32[8,96,768]{2,1,0:T(8,128)S(1)}, f32[4608,128]{1,0:T(8,128)S(1)}, f32[8,96,768]{2,1,0:T(8,128)}) custom-call(f32[8]{0:T(128)S(1)} %copy-done.10, f32[8]{0:T(128)S(1)} %copy-done.8, f32[8,96,768]{2,1,0:T(8,128)S(1)} %get-tuple-element.37.below.here_ref.above, f32[8,96,768]{2,1,0:T(8,128)S(1)} %get-tuple-element.37.below.here_ref.above, ...), custom_call_target="tpu_custom_call" | custom-call | tf_op jit(solution)/shard_map/stencil/pallas_call | solution.py:483
  26.1 0.7 %collective-permute-start.6 = (bf16[8,768]{1,0:T(8,128)(2,1)S(1)}, bf16[8,768]{1,0:T(8,128)(2,1)S(1)}, u32[]{:S(2)}, u32[]{:S(2)}) collective-permute-start(bf16[8,768]{1,0:T(8,128)(2,1)S(1)} %get-tuple-element.50), channel_id=1, source_target_pairs={{0,1},{1,0},{2,3},{3,2},{4,5},{5,4},{6,7},{7,6},{8,9},{9,8},{10,11... | collective-permute-start | bytes 36872 | tf_op jit(solution)/shard_map/ppermute | solution.py:463
  26.9 0.9 %collective-permute-start.7 = (bf16[8,768]{1,0:T(8,128)(2,1)S(1)}, bf16[8,768]{1,0:T(8,128)(2,1)S(1)}, u32[]{:S(2)}, u32[]{:S(2)}) collective-permute-start(bf16[8,768]{1,0:T(8,128)(2,1)S(1)} %get-tuple-element.51), channel_id=1, source_target_pairs={{0,3},{1,2},{2,1},{3,0},{4,7},{5,6},{6,5},{7,4},{8,11},{9,10},{10,... | collective-permute-start | bytes 36872 | tf_op jit(solution)/shard_map/ppermute | solution.py:463
  27.8 3.7 %stencil.5 = (f32[8,96,768]{2,1,0:T(8,128)S(1)}, f32[4608,128]{1,0:T(8,128)S(1)}, f32[8,96,768]{2,1,0:T(8,128)}) custom-call(f32[8]{0:T(128)S(1)} %copy-done.10, f32[8]{0:T(128)S(1)} %copy-done.8, f32[8,96,768]{2,1,0:T(8,128)S(1)} %get-tuple-element.37.below.here_ref.above, ...), custom_call_target="tpu_custom_call", output_to_operand_aliasing={{0}: (9, {}), {1}: (10, {}), {2}: (11, {})} | custom-call | tf_op jit(solution)/shard_map/stencil/pallas_call | solution.py:483
  31.5 0.9 %collective-permute-done.7.y_two = bf16[8,768]{1,0:T(8,128)(2,1)S(1)} collective-permute-done((bf16[8,768]{1,0:T(8,128)(2,1)S(1)}, bf16[8,768]{1,0:T(8,128)(2,1)S(1)}, u32[]{:S(2)}, u32[]{:S(2)}) %collective-permute-start.7) | collective-permute-done | bytes 12320 | tf_op jit(solution)/shard_map/ppermute | solution.py:463
  32.4 7.4 %finish.1 = (f32[8,96,768]{2,1,0:T(8,128)}, f32[32,256]{1,0:T(8,128)S(1)}) custom-call(s32[3,128]{1,0:T(4,128)S(1)} %bitcast.14, f32[8,96,768]{2,1,0:T(8,128)S(1)} %get-tuple-element.47.pressure_in, bf16[8,96,768]{2,1,0:T(8,128)(2,1)S(1)} %copy-done.2, bf16[8,96,768]{2,1,0:T(8,128)(2,1)S(1)} %copy-done.2, bf16[8,96,768]{2,1,0:T(8,128)(2,1)S(1)} %copy-done.2, ...), custom_call_target="tpu_custom_call" | custom-call | tf_op jit(solution)/shard_map/finish/pallas_call | solution.py:538
  39.8 0.1 collective-permute-start.8
  39.9 1.2 %collective-permute-done.8 = f32[32,256]{1,0:T(8,128)S(1)} collective-permute-done((f32[32,256]{1,0:T(8,128)S(1)}, f32[32,256]{1,0:T(8,128)S(1)}, u32[]{:S(2)}, u32[]{:S(2)}) %collective-permute-start.8) | collective-permute-done | bytes 32800 | tf_op jit(solution)/shard_map/ppermute | solution.py:463
  41.1 1.4 %collective-permute-start.11 = (f32[32,256]{1,0:T(8,128)S(1)}, f32[32,256]{1,0:T(8,128)S(1)}, u32[]{:S(2)}, u32[]{:S(2)}) collective-permute-start(f32[32,256]{1,0:T(8,128)S(1)} %add.12.order), channel_id=1, source_target_pairs={{0,24},{4,28},{8,16},{12,20},{16,8},{20,12},{24,0},{28,4},{1,25},{... | collective-permute-start | bytes 98312 | tf_op jit(solution)/shard_map/ppermute | solution.py:562
  42.5 1.5 %collective-permute-start.10 = (f32[32,256]{1,0:T(8,128)S(1)}, f32[32,256]{1,0:T(8,128)S(1)}, u32[]{:S(2)}, u32[]{:S(2)}) collective-permute-start(f32[32,256]{1,0:T(8,128)S(1)} %add.12.order), channel_id=1, source_target_pairs={{0,16},{4,20},{8,24},{12,28},{16,0},{20,4},{24,8},{28,12},{1,17},{... | collective-permute-start | bytes 98312 | tf_op jit(solution)/shard_map/ppermute | solution.py:562
  44.0 0.5 %collective-permute-start.9 = (f32[32,256]{1,0:T(8,128)S(1)}, f32[32,256]{1,0:T(8,128)S(1)}, u32[]{:S(2)}, u32[]{:S(2)}) collective-permute-start(f32[32,256]{1,0:T(8,128)S(1)} %add.12.order), channel_id=1, source_target_pairs={{0,8},{4,12},{8,0},{12,4},{16,24},{20,28},{24,16},{28,20},{1,9},{5... | collective-permute-start | bytes 98312 | tf_op jit(solution)/shard_map/ppermute | solution.py:562
  44.6 5.4 %gather_nodes.1 = f32[1,2048]{1,0:T(1,128)} custom-call(s32[1,2048]{1,0:T(1,128)S(1)} %bitcast.9, f32[8]{0:T(128)S(1)} %copy-done.8, f32[4608,128]{1,0:T(8,128)S(1)} %get-tuple-element.54.states, s32[1,2048]{1,0:T(1,128)S(1)} %bitcast.10, s32[1,2048]{1,0:T(1,128)S(1)} %bitcast.12, f32[32,256]{1,0:T(8,128)S(1)} %add.12.order), custom_call_target="tpu_custom_call" | custom-call | tf_op jit(solution)/shard_map/gather_nodes/pallas_call | solution.py:567
  50.0 0.6 %add_add_fusion = f32[32,256]{1,0:T(8,128)} fusion(f32[32,256]{1,0:T(8,128)S(1)} %collective-permute-done.10, f32[32,256]{1,0:T(8,128)S(1)} %collective-permute-done.11, f32[32,256]{1,0:T(8,128)S(1)} %add.12.order, f32[32,256]{1,0:T(8,128)S(1)} %collective-permute-done.9), kind=kLoop, calls=%fused_computation | loop fusion | flops 24576 | bytes 163840 | tf_op jit(solution)/shard_map/add | solution.py:564
  (39 shorter events, 0.1 us)
Async XLA Ops:
  2.3 8.3 %copy-start.6 = (s32[1,1,2048]{2,1,0:T(1,128)S(1)}, s32[1,1,2048]{2,1,0:T(1,128)}, u32[]{:S(2)}) copy-start(s32[1,1,2048]{2,1,0:T(1,128)} %param.15) | copy-start | bytes 24580
  2.3 8.3 %copy-start.7 = (s32[1,1,2048]{2,1,0:T(1,128)S(1)}, s32[1,1,2048]{2,1,0:T(1,128)}, u32[]{:S(2)}) copy-start(s32[1,1,2048]{2,1,0:T(1,128)} %param.16) | copy-start | bytes 24580
  2.3 8.3 %copy-start.8 = (f32[8]{0:T(128)S(1)}, f32[8]{0:T(128)}, u32[]{:S(2)}) copy-start(f32[8]{0:T(128)} %loss_ref.9) | copy-start | bytes 100
  2.3 8.4 %copy-start.9 = (f32[1,1,2048]{2,1,0:T(1,128)S(1)}, f32[1,1,2048]{2,1,0:T(1,128)}, u32[]{:S(2)}) copy-start(f32[1,1,2048]{2,1,0:T(1,128)} %param.17) | copy-start | bytes 24580
  2.3 12.9 %copy-start.1 = (f32[8,96,768]{2,1,0:T(8,128)S(1)}, f32[8,96,768]{2,1,0:T(8,128)}, u32[]{:S(2)}) copy-start(f32[8,96,768]{2,1,0:T(8,128)} %previous.5) | copy-start | bytes 7077892
  2.3 12.9 %copy-start.2 = (bf16[8,96,768]{2,1,0:T(8,128)(2,1)S(1)}, bf16[8,96,768]{2,1,0:T(8,128)(2,1)}, u32[]{:S(2)}) copy-start(bf16[8,96,768]{2,1,0:T(8,128)(2,1)} %c_bottom.3) | copy-start | bytes 3538948
  2.3 12.9 %copy-start.3 = (f32[8,96,768]{2,1,0:T(8,128)S(1)}, f32[8,96,768]{2,1,0:T(8,128)}, u32[]{:S(2)}) copy-start(f32[8,96,768]{2,1,0:T(8,128)} %previous.3) | copy-start | bytes 7077892
  2.3 12.9 %copy-start.10 = (f32[8]{0:T(128)S(1)}, f32[8]{0:T(128)}, u32[]{:S(2)}) copy-start(f32[8]{0:T(128)} %pole_ref.5) | copy-start | bytes 100
  2.5 18.3 %collective-permute-start = (bf16[96,768]{1,0:T(8,128)(2,1)S(1)}, bf16[96,768]{1,0:T(8,128)(2,1)S(1)}, u32[]{:S(2)}, u32[]{:S(2)}) collective-permute-start(bf16[96,768]{1,0:T(8,128)(2,1)S(1)} %get-tuple-element.33), channel_id=1, source_target_pairs={{0,4},{4,0},{8,12},{12,8},{16,20},{20,16},{24,28},{28,24},{1,5},{5... | collective-permute-start | bytes 442376 | tf_op jit(solution)/shard_map/ppermute | solution.py:463
  3.0 17.8 %collective-permute-start.1 = (bf16[96,768]{1,0:T(8,128)(2,1)S(1)}, bf16[96,768]{1,0:T(8,128)(2,1)S(1)}, u32[]{:S(2)}, u32[]{:S(2)}) collective-permute-start(bf16[96,768]{1,0:T(8,128)(2,1)S(1)} %get-tuple-element.34), channel_id=1, source_target_pairs={{0,28},{4,8},{8,4},{12,16},{16,12},{20,24},{24,20},{28,0},{1,29},{... | collective-permute-start | bytes 442376 | tf_op jit(solution)/shard_map/ppermute | solution.py:463
  6.6 14.2 %collective-permute-start.2 = (bf16[8,768]{1,0:T(8,128)(2,1)S(1)}, bf16[8,768]{1,0:T(8,128)(2,1)S(1)}, u32[]{:S(2)}, u32[]{:S(2)}) collective-permute-start(bf16[8,768]{1,0:T(8,128)(2,1)S(1)} %get-tuple-element.35), channel_id=1, source_target_pairs={{0,1},{1,0},{2,3},{3,2},{4,5},{5,4},{6,7},{7,6},{8,9},{9,8},{10,11... | collective-permute-start | bytes 36872 | tf_op jit(solution)/shard_map/ppermute | solution.py:463
  8.2 12.7 %collective-permute-start.3 = (bf16[8,768]{1,0:T(8,128)(2,1)S(1)}, bf16[8,768]{1,0:T(8,128)(2,1)S(1)}, u32[]{:S(2)}, u32[]{:S(2)}) collective-permute-start(bf16[8,768]{1,0:T(8,128)(2,1)S(1)} %get-tuple-element.36), channel_id=1, source_target_pairs={{0,3},{1,2},{2,1},{3,0},{4,7},{5,6},{6,5},{7,4},{8,11},{9,10},{10,... | collective-permute-start | bytes 36872 | tf_op jit(solution)/shard_map/ppermute | solution.py:463
  21.7 10.6 %collective-permute-start.4 = (bf16[96,768]{1,0:T(8,128)(2,1)S(1)}, bf16[96,768]{1,0:T(8,128)(2,1)S(1)}, u32[]{:S(2)}, u32[]{:S(2)}) collective-permute-start(bf16[96,768]{1,0:T(8,128)(2,1)S(1)} %get-tuple-element.48), channel_id=1, source_target_pairs={{0,4},{4,0},{8,12},{12,8},{16,20},{20,16},{24,28},{28,24},{1,5},{5... | collective-permute-start | bytes 442376 | tf_op jit(solution)/shard_map/ppermute | solution.py:463
  21.8 10.6 %collective-permute-start.5 = (bf16[96,768]{1,0:T(8,128)(2,1)S(1)}, bf16[96,768]{1,0:T(8,128)(2,1)S(1)}, u32[]{:S(2)}, u32[]{:S(2)}) collective-permute-start(bf16[96,768]{1,0:T(8,128)(2,1)S(1)} %get-tuple-element.49), channel_id=1, source_target_pairs={{0,28},{4,8},{8,4},{12,16},{16,12},{20,24},{24,20},{28,0},{1,29},{... | collective-permute-start | bytes 442376 | tf_op jit(solution)/shard_map/ppermute | solution.py:463
  26.1 6.3 %slice-start.1 = ((s8[4456448]{0:T(1024)(128)(4,1)}), s8[262144]{0:T(1024)(128)(4,1)S(1)}, s32[]{:S(2)}) async-start(s8[4456448]{0:T(1024)(128)(4,1)} %bitcast.5), calls=%async_computation.1 | async-start | bytes 524288
  26.1 6.3 %copy-start.4 = (bf16[2,944,256]{2,1,0:T(8,128)(2,1)S(1)}, bf16[2,944,256]{2,1,0:T(8,128)(2,1)}, u32[]{:S(2)}) copy-start(bf16[2,944,256]{2,1,0:T(8,128)(2,1)} %constant.8.clone.mix_in) | copy-start | bytes 2899972
  26.1 6.3 %copy-start.5 = (bf16[16,32,256]{2,1,0:T(8,128)(2,1)S(1)}, bf16[16,32,256]{2,1,0:T(8,128)(2,1)}, u32[]{:S(2)}) copy-start(bf16[16,32,256]{2,1,0:T(8,128)(2,1)} %constant.7.clone.axial_in) | copy-start | bytes 786436
  26.1 6.3 %copy-start.11 = (s32[128,3]{0,1:T(4,128)S(1)}, s32[128,3]{0,1:T(4,128)}, u32[]{:S(2)}) copy-start(s32[128,3]{0,1:T(4,128)} %param.20) | copy-start | bytes 4612
  26.1 5.3 %collective-permute-start.6 = (bf16[8,768]{1,0:T(8,128)(2,1)S(1)}, bf16[8,768]{1,0:T(8,128)(2,1)S(1)}, u32[]{:S(2)}, u32[]{:S(2)}) collective-permute-start(bf16[8,768]{1,0:T(8,128)(2,1)S(1)} %get-tuple-element.50), channel_id=1, source_target_pairs={{0,1},{1,0},{2,3},{3,2},{4,5},{5,4},{6,7},{7,6},{8,9},{9,8},{10,11... | collective-permute-start | bytes 36872 | tf_op jit(solution)/shard_map/ppermute | solution.py:463
  26.9 5.5 %collective-permute-start.7 = (bf16[8,768]{1,0:T(8,128)(2,1)S(1)}, bf16[8,768]{1,0:T(8,128)(2,1)S(1)}, u32[]{:S(2)}, u32[]{:S(2)}) collective-permute-start(bf16[8,768]{1,0:T(8,128)(2,1)S(1)} %get-tuple-element.51), channel_id=1, source_target_pairs={{0,3},{1,2},{2,1},{3,0},{4,7},{5,6},{6,5},{7,4},{8,11},{9,10},{10,... | collective-permute-start | bytes 36872 | tf_op jit(solution)/shard_map/ppermute | solution.py:463
  39.8 1.3 %collective-permute-start.8 = (f32[32,256]{1,0:T(8,128)S(1)}, f32[32,256]{1,0:T(8,128)S(1)}, u32[]{:S(2)}, u32[]{:S(2)}) collective-permute-start(f32[32,256]{1,0:T(8,128)S(1)} %get-tuple-element.55), channel_id=1, source_target_pairs={{0,4},{4,0},{8,12},{12,8},{16,20},{20,16},{24,28},{28,24},{1,5},{5... | collective-permute-start | bytes 98312 | tf_op jit(solution)/shard_map/ppermute | solution.py:463
  41.1 8.9 %collective-permute-start.11 = (f32[32,256]{1,0:T(8,128)S(1)}, f32[32,256]{1,0:T(8,128)S(1)}, u32[]{:S(2)}, u32[]{:S(2)}) collective-permute-start(f32[32,256]{1,0:T(8,128)S(1)} %add.12.order), channel_id=1, source_target_pairs={{0,24},{4,28},{8,16},{12,20},{16,8},{20,12},{24,0},{28,4},{1,25},{... | collective-permute-start | bytes 98312 | tf_op jit(solution)/shard_map/ppermute | solution.py:562
  42.5 7.5 %collective-permute-start.10 = (f32[32,256]{1,0:T(8,128)S(1)}, f32[32,256]{1,0:T(8,128)S(1)}, u32[]{:S(2)}, u32[]{:S(2)}) collective-permute-start(f32[32,256]{1,0:T(8,128)S(1)} %add.12.order), channel_id=1, source_target_pairs={{0,16},{4,20},{8,24},{12,28},{16,0},{20,4},{24,8},{28,12},{1,17},{... | collective-permute-start | bytes 98312 | tf_op jit(solution)/shard_map/ppermute | solution.py:562
  44.0 6.0 %collective-permute-start.9 = (f32[32,256]{1,0:T(8,128)S(1)}, f32[32,256]{1,0:T(8,128)S(1)}, u32[]{:S(2)}, u32[]{:S(2)}) collective-permute-start(f32[32,256]{1,0:T(8,128)S(1)} %add.12.order), channel_id=1, source_target_pairs={{0,8},{4,12},{8,0},{12,4},{16,24},{20,28},{24,16},{28,20},{1,9},{5... | collective-permute-start | bytes 98312 | tf_op jit(solution)/shard_map/ppermute | solution.py:562
  (2 other events, 7.9 us)

commit v6 on v5

--- a/solution.py
+++ b/solution.py
@@ -418,8 +418,8 @@
         products[1][at, 0 : count - LANES] = moment[:, LANES:]
         return carry
 
-    lax.fori_loop(0, spheres, across, 0, unroll=8)
-    lax.fori_loop(0, spheres, along, 0, unroll=16)
+    lax.fori_loop(0, spheres, across, 0, unroll=16)
+    lax.fori_loop(0, spheres, along, 0, unroll=32)
     result = jnp.zeros((spheres, COEFS), F32)
     for q in range(DEGREES):
         at = pl.ds(q, spheres, stride=DEGREES)

time: 50.8 us -> 50.9 us (level)
  no operation moved by 1% of the time
where the time goes in v6:
time: 50.9 us; the launch traced here: 50.7 us
  Pallas kernels  31.3 us (61%)
  starting transfers between devices  14 us (28%)
  waiting for transfers between devices  2.13 us (4%)
  local copies, waits for them, and re-layouts  1.71 us (3%)
  between operations  0.87 us (2%)
  other arithmetic  0.63 us (1%)
    pallas_call x3, Pallas kernels, step(): pl.pallas_call(functools.partial(stencil, start, slab - 1), grid=(stop -...  12.9 us
    ppermute x9, starting transfers between devices, swap(): lax.ppermute(value, axis, [(i, (i + moves[i]) % count) for i in range(cou...  10.6 us
    pallas_call x1, Pallas kernels, shards(): pl.pallas_call(finish, grid=(1,), out_shape=(block, jax.ShapeDtypeStruct(...  7.45 us
    pallas_call x1, Pallas kernels, shards(): pl.pallas_call(gather_nodes, out_shape=jax.ShapeDtypeStruct((1, nodes), F...  5.43 us
    pallas_call x1, Pallas kernels, shards(): pl.pallas_call(node_maps, out_shape=(dense, dense), in_specs=[smem] * 2 +...  4.58 us
    ppermute x3, starting transfers between devices, shards(): lax.ppermute(partial, 'gx', [(i, i ^ move) for i in range(8)])  3.49 us
    ppermute x9, waiting for transfers between devices, swap(): lax.ppermute(value, axis, [(i, (i + moves[i]) % count) for i in range(cou...  2.12 us
    unnamed x28, local copies, waits for them, and re-layouts  1.71 us
  transfers between devices with their start and end apart: 12, of which 2 were waited for; matrix products, arithmetic and copies ran while one was open for 0% of the time, Pallas kernels for 45%

profile of v6, /device:TPU:0, one launch (start us, length us, event | category | flops | bytes accessed | tf_op | source)
XLA Modules:
  0.0 50.7 jit_solution(4285994487594152710)
XLA Ops:
  0.6 1.7 %copy-done = f32[8,96,768]{2,1,0:T(8,128)S(1)} copy-done((f32[8,96,768]{2,1,0:T(8,128)S(1)}, f32[8,96,768]{2,1,0:T(8,128)}, u32[]{:S(2)}) %copy-start) | copy-done | bytes 2359320
  2.4 0.2 edges.1
  2.5 0.5 %collective-permute-start = (bf16[96,768]{1,0:T(8,128)(2,1)S(1)}, bf16[96,768]{1,0:T(8,128)(2,1)S(1)}, u32[]{:S(2)}, u32[]{:S(2)}) collective-permute-start(bf16[96,768]{1,0:T(8,128)(2,1)S(1)} %get-tuple-element.33), channel_id=1, source_target_pairs={{0,4},{4,0},{8,12},{12,8},{16,20},{20,16},{24,28},{28,24},{1,5},{5... | collective-permute-start | bytes 442376 | tf_op jit(solution)/shard_map/ppermute | solution.py:463
  3.0 3.6 %collective-permute-start.1 = (bf16[96,768]{1,0:T(8,128)(2,1)S(1)}, bf16[96,768]{1,0:T(8,128)(2,1)S(1)}, u32[]{:S(2)}, u32[]{:S(2)}) collective-permute-start(bf16[96,768]{1,0:T(8,128)(2,1)S(1)} %get-tuple-element.34), channel_id=1, source_target_pairs={{0,28},{4,8},{8,4},{12,16},{16,12},{20,24},{24,20},{28,0},{1,29},{... | collective-permute-start | bytes 442376 | tf_op jit(solution)/shard_map/ppermute | solution.py:463
  6.6 1.6 %collective-permute-start.2 = (bf16[8,768]{1,0:T(8,128)(2,1)S(1)}, bf16[8,768]{1,0:T(8,128)(2,1)S(1)}, u32[]{:S(2)}, u32[]{:S(2)}) collective-permute-start(bf16[8,768]{1,0:T(8,128)(2,1)S(1)} %get-tuple-element.35), channel_id=1, source_target_pairs={{0,1},{1,0},{2,3},{3,2},{4,5},{5,4},{6,7},{7,6},{8,9},{9,8},{10,11... | collective-permute-start | bytes 36872 | tf_op jit(solution)/shard_map/ppermute | solution.py:463
  8.2 2.5 %collective-permute-start.3 = (bf16[8,768]{1,0:T(8,128)(2,1)S(1)}, bf16[8,768]{1,0:T(8,128)(2,1)S(1)}, u32[]{:S(2)}, u32[]{:S(2)}) collective-permute-start(bf16[8,768]{1,0:T(8,128)(2,1)S(1)} %get-tuple-element.36), channel_id=1, source_target_pairs={{0,3},{1,2},{2,1},{3,0},{4,7},{5,6},{6,5},{7,4},{8,11},{9,10},{10,... | collective-permute-start | bytes 36872 | tf_op jit(solution)/shard_map/ppermute | solution.py:463
  10.7 4.6 %node_maps.1 = (f32[4608,128]{1,0:T(8,128)S(1)}, f32[4608,128]{1,0:T(8,128)S(1)}) custom-call(s32[1,2048]{1,0:T(1,128)S(1)} %bitcast.7, f32[8]{0:T(128)S(1)} %copy-done.8, s32[1,2048]{1,0:T(1,128)S(1)} %bitcast.8, s32[1,2048]{1,0:T(1,128)S(1)} %bitcast.11, f32[1,2048]{1,0:T(1,128)S(1)} %bitcast.13), custom_call_target="tpu_custom_call" | custom-call | tf_op jit(solution)/shard_map/node_maps/pallas_call | solution.py:508
  15.3 5.5 %stencil.3 = (f32[8,96,768]{2,1,0:T(8,128)S(1)}, f32[4608,128]{1,0:T(8,128)S(1)}) custom-call(f32[8]{0:T(128)S(1)} %copy-done.10, f32[8]{0:T(128)S(1)} %copy-done.8, f32[8,96,768]{2,1,0:T(8,128)S(1)} %copy-done.1, f32[8,96,768]{2,1,0:T(8,128)S(1)} %copy-done.1, f32[8,96,768]{2,1,0:T(8,128)S(1)} %copy-done.1, f32[8,96,768]{2,1,0:T(8,128)S(1)} %copy-done.3, ...), custom_call_target="tpu_custom_call" | custom-call | tf_op jit(solution)/shard_map/stencil/pallas_call | solution.py:483
  20.9 0.9 %fix_and_send.1 = (f32[8,96,768]{2,1,0:T(8,128)S(1)}, bf16[96,768]{1,0:T(8,128)(2,1)S(1)}, bf16[96,768]{1,0:T(8,128)(2,1)S(1)}, bf16[8,768]{1,0:T(8,128)(2,1)S(1)}, bf16[8,768]{1,0:T(8,128)(2,1)S(1)}) custom-call(f32[8,96,768]{2,1,0:T(8,128)S(1)} %get-tuple-element.32.field_in, bf16[8,96,768]{2,1,0:T(8,128)(2,1)S(1)} %copy-done.2, ...), custom_call_target="tpu_custom_call", output_to_operand_aliasing={{0}: (0, {})} | custom-call | tf_op jit(solution)/shard_map/fix_and_send/pallas_call | solution.py:519
  21.7 0.1 collective-permute-start.4
  21.8 0.6 %collective-permute-start.5 = (bf16[96,768]{1,0:T(8,128)(2,1)S(1)}, bf16[96,768]{1,0:T(8,128)(2,1)S(1)}, u32[]{:S(2)}, u32[]{:S(2)}) collective-permute-start(bf16[96,768]{1,0:T(8,128)(2,1)S(1)} %get-tuple-element.49), channel_id=1, source_target_pairs={{0,28},{4,8},{8,4},{12,16},{16,12},{20,24},{24,20},{28,0},{1,29},{... | collective-permute-start | bytes 442376 | tf_op jit(solution)/shard_map/ppermute | solution.py:463
  22.4 3.7 %stencil.4 = (f32[8,96,768]{2,1,0:T(8,128)S(1)}, f32[4608,128]{1,0:T(8,128)S(1)}, f32[8,96,768]{2,1,0:T(8,128)}) custom-call(f32[8]{0:T(128)S(1)} %copy-done.10, f32[8]{0:T(128)S(1)} %copy-done.8, f32[8,96,768]{2,1,0:T(8,128)S(1)} %get-tuple-element.37.below.here_ref.above, f32[8,96,768]{2,1,0:T(8,128)S(1)} %get-tuple-element.37.below.here_ref.above, ...), custom_call_target="tpu_custom_call" | custom-call | tf_op jit(solution)/shard_map/stencil/pallas_call | solution.py:483
  26.1 0.7 %collective-permute-start.6 = (bf16[8,768]{1,0:T(8,128)(2,1)S(1)}, bf16[8,768]{1,0:T(8,128)(2,1)S(1)}, u32[]{:S(2)}, u32[]{:S(2)}) collective-permute-start(bf16[8,768]{1,0:T(8,128)(2,1)S(1)} %get-tuple-element.50), channel_id=1, source_target_pairs={{0,1},{1,0},{2,3},{3,2},{4,5},{5,4},{6,7},{7,6},{8,9},{9,8},{10,11... | collective-permute-start | bytes 36872 | tf_op jit(solution)/shard_map/ppermute | solution.py:463
  26.9 0.9 %collective-permute-start.7 = (bf16[8,768]{1,0:T(8,128)(2,1)S(1)}, bf16[8,768]{1,0:T(8,128)(2,1)S(1)}, u32[]{:S(2)}, u32[]{:S(2)}) collective-permute-start(bf16[8,768]{1,0:T(8,128)(2,1)S(1)} %get-tuple-element.51), channel_id=1, source_target_pairs={{0,3},{1,2},{2,1},{3,0},{4,7},{5,6},{6,5},{7,4},{8,11},{9,10},{10,... | collective-permute-start | bytes 36872 | tf_op jit(solution)/shard_map/ppermute | solution.py:463
  27.8 3.7 %stencil.5 = (f32[8,96,768]{2,1,0:T(8,128)S(1)}, f32[4608,128]{1,0:T(8,128)S(1)}, f32[8,96,768]{2,1,0:T(8,128)}) custom-call(f32[8]{0:T(128)S(1)} %copy-done.10, f32[8]{0:T(128)S(1)} %copy-done.8, f32[8,96,768]{2,1,0:T(8,128)S(1)} %get-tuple-element.37.below.here_ref.above, ...), custom_call_target="tpu_custom_call", output_to_operand_aliasing={{0}: (9, {}), {1}: (10, {}), {2}: (11, {})} | custom-call | tf_op jit(solution)/shard_map/stencil/pallas_call | solution.py:483
  31.5 0.9 %collective-permute-done.7.y_two = bf16[8,768]{1,0:T(8,128)(2,1)S(1)} collective-permute-done((bf16[8,768]{1,0:T(8,128)(2,1)S(1)}, bf16[8,768]{1,0:T(8,128)(2,1)S(1)}, u32[]{:S(2)}, u32[]{:S(2)}) %collective-permute-start.7) | collective-permute-done | bytes 12320 | tf_op jit(solution)/shard_map/ppermute | solution.py:463
  32.4 7.5 %finish.1 = (f32[8,96,768]{2,1,0:T(8,128)}, f32[32,256]{1,0:T(8,128)S(1)}) custom-call(s32[3,128]{1,0:T(4,128)S(1)} %bitcast.14, f32[8,96,768]{2,1,0:T(8,128)S(1)} %get-tuple-element.47.pressure_in, bf16[8,96,768]{2,1,0:T(8,128)(2,1)S(1)} %copy-done.2, bf16[8,96,768]{2,1,0:T(8,128)(2,1)S(1)} %copy-done.2, bf16[8,96,768]{2,1,0:T(8,128)(2,1)S(1)} %copy-done.2, ...), custom_call_target="tpu_custom_call" | custom-call | tf_op jit(solution)/shard_map/finish/pallas_call | solution.py:538
  39.9 0.1 collective-permute-start.8
  40.0 1.2 %collective-permute-done.8 = f32[32,256]{1,0:T(8,128)S(1)} collective-permute-done((f32[32,256]{1,0:T(8,128)S(1)}, f32[32,256]{1,0:T(8,128)S(1)}, u32[]{:S(2)}, u32[]{:S(2)}) %collective-permute-start.8) | collective-permute-done | bytes 32800 | tf_op jit(solution)/shard_map/ppermute | solution.py:463
  41.2 1.4 %collective-permute-start.11 = (f32[32,256]{1,0:T(8,128)S(1)}, f32[32,256]{1,0:T(8,128)S(1)}, u32[]{:S(2)}, u32[]{:S(2)}) collective-permute-start(f32[32,256]{1,0:T(8,128)S(1)} %add.12.order), channel_id=1, source_target_pairs={{0,24},{4,28},{8,16},{12,20},{16,8},{20,12},{24,0},{28,4},{1,25},{... | collective-permute-start | bytes 98312 | tf_op jit(solution)/shard_map/ppermute | solution.py:562
  42.6 1.5 %collective-permute-start.10 = (f32[32,256]{1,0:T(8,128)S(1)}, f32[32,256]{1,0:T(8,128)S(1)}, u32[]{:S(2)}, u32[]{:S(2)}) collective-permute-start(f32[32,256]{1,0:T(8,128)S(1)} %add.12.order), channel_id=1, source_target_pairs={{0,16},{4,20},{8,24},{12,28},{16,0},{20,4},{24,8},{28,12},{1,17},{... | collective-permute-start | bytes 98312 | tf_op jit(solution)/shard_map/ppermute | solution.py:562
  44.1 0.5 %collective-permute-start.9 = (f32[32,256]{1,0:T(8,128)S(1)}, f32[32,256]{1,0:T(8,128)S(1)}, u32[]{:S(2)}, u32[]{:S(2)}) collective-permute-start(f32[32,256]{1,0:T(8,128)S(1)} %add.12.order), channel_id=1, source_target_pairs={{0,8},{4,12},{8,0},{12,4},{16,24},{20,28},{24,16},{28,20},{1,9},{5... | collective-permute-start | bytes 98312 | tf_op jit(solution)/shard_map/ppermute | solution.py:562
  44.7 5.4 %gather_nodes.1 = f32[1,2048]{1,0:T(1,128)} custom-call(s32[1,2048]{1,0:T(1,128)S(1)} %bitcast.9, f32[8]{0:T(128)S(1)} %copy-done.8, f32[4608,128]{1,0:T(8,128)S(1)} %get-tuple-element.54.states, s32[1,2048]{1,0:T(1,128)S(1)} %bitcast.10, s32[1,2048]{1,0:T(1,128)S(1)} %bitcast.12, f32[32,256]{1,0:T(8,128)S(1)} %add.12.order), custom_call_target="tpu_custom_call" | custom-call | tf_op jit(solution)/shard_map/gather_nodes/pallas_call | solution.py:567
  50.1 0.6 %add_add_fusion = f32[32,256]{1,0:T(8,128)} fusion(f32[32,256]{1,0:T(8,128)S(1)} %collective-permute-done.10, f32[32,256]{1,0:T(8,128)S(1)} %collective-permute-done.11, f32[32,256]{1,0:T(8,128)S(1)} %add.12.order, f32[32,256]{1,0:T(8,128)S(1)} %collective-permute-done.9), kind=kLoop, calls=%fused_computation | loop fusion | flops 24576 | bytes 163840 | tf_op jit(solution)/shard_map/add | solution.py:564
  (39 shorter events, 0.1 us)
Async XLA Ops:
  2.3 8.3 %copy-start.6 = (s32[1,1,2048]{2,1,0:T(1,128)S(1)}, s32[1,1,2048]{2,1,0:T(1,128)}, u32[]{:S(2)}) copy-start(s32[1,1,2048]{2,1,0:T(1,128)} %param.15) | copy-start | bytes 24580
  2.3 8.3 %copy-start.7 = (s32[1,1,2048]{2,1,0:T(1,128)S(1)}, s32[1,1,2048]{2,1,0:T(1,128)}, u32[]{:S(2)}) copy-start(s32[1,1,2048]{2,1,0:T(1,128)} %param.16) | copy-start | bytes 24580
  2.3 8.3 %copy-start.8 = (f32[8]{0:T(128)S(1)}, f32[8]{0:T(128)}, u32[]{:S(2)}) copy-start(f32[8]{0:T(128)} %loss_ref.9) | copy-start | bytes 100
  2.3 8.4 %copy-start.9 = (f32[1,1,2048]{2,1,0:T(1,128)S(1)}, f32[1,1,2048]{2,1,0:T(1,128)}, u32[]{:S(2)}) copy-start(f32[1,1,2048]{2,1,0:T(1,128)} %param.17) | copy-start | bytes 24580
  2.3 12.9 %copy-start.1 = (f32[8,96,768]{2,1,0:T(8,128)S(1)}, f32[8,96,768]{2,1,0:T(8,128)}, u32[]{:S(2)}) copy-start(f32[8,96,768]{2,1,0:T(8,128)} %previous.5) | copy-start | bytes 7077892
  2.3 12.9 %copy-start.2 = (bf16[8,96,768]{2,1,0:T(8,128)(2,1)S(1)}, bf16[8,96,768]{2,1,0:T(8,128)(2,1)}, u32[]{:S(2)}) copy-start(bf16[8,96,768]{2,1,0:T(8,128)(2,1)} %c_bottom.3) | copy-start | bytes 3538948
  2.3 12.9 %copy-start.3 = (f32[8,96,768]{2,1,0:T(8,128)S(1)}, f32[8,96,768]{2,1,0:T(8,128)}, u32[]{:S(2)}) copy-start(f32[8,96,768]{2,1,0:T(8,128)} %previous.3) | copy-start | bytes 7077892
  2.3 12.9 %copy-start.10 = (f32[8]{0:T(128)S(1)}, f32[8]{0:T(128)}, u32[]{:S(2)}) copy-start(f32[8]{0:T(128)} %pole_ref.5) | copy-start | bytes 100
  2.5 18.3 %collective-permute-start = (bf16[96,768]{1,0:T(8,128)(2,1)S(1)}, bf16[96,768]{1,0:T(8,128)(2,1)S(1)}, u32[]{:S(2)}, u32[]{:S(2)}) collective-permute-start(bf16[96,768]{1,0:T(8,128)(2,1)S(1)} %get-tuple-element.33), channel_id=1, source_target_pairs={{0,4},{4,0},{8,12},{12,8},{16,20},{20,16},{24,28},{28,24},{1,5},{5... | collective-permute-start | bytes 442376 | tf_op jit(solution)/shard_map/ppermute | solution.py:463
  3.0 17.8 %collective-permute-start.1 = (bf16[96,768]{1,0:T(8,128)(2,1)S(1)}, bf16[96,768]{1,0:T(8,128)(2,1)S(1)}, u32[]{:S(2)}, u32[]{:S(2)}) collective-permute-start(bf16[96,768]{1,0:T(8,128)(2,1)S(1)} %get-tuple-element.34), channel_id=1, source_target_pairs={{0,28},{4,8},{8,4},{12,16},{16,12},{20,24},{24,20},{28,0},{1,29},{... | collective-permute-start | bytes 442376 | tf_op jit(solution)/shard_map/ppermute | solution.py:463
  6.6 14.2 %collective-permute-start.2 = (bf16[8,768]{1,0:T(8,128)(2,1)S(1)}, bf16[8,768]{1,0:T(8,128)(2,1)S(1)}, u32[]{:S(2)}, u32[]{:S(2)}) collective-permute-start(bf16[8,768]{1,0:T(8,128)(2,1)S(1)} %get-tuple-element.35), channel_id=1, source_target_pairs={{0,1},{1,0},{2,3},{3,2},{4,5},{5,4},{6,7},{7,6},{8,9},{9,8},{10,11... | collective-permute-start | bytes 36872 | tf_op jit(solution)/shard_map/ppermute | solution.py:463
  8.2 12.7 %collective-permute-start.3 = (bf16[8,768]{1,0:T(8,128)(2,1)S(1)}, bf16[8,768]{1,0:T(8,128)(2,1)S(1)}, u32[]{:S(2)}, u32[]{:S(2)}) collective-permute-start(bf16[8,768]{1,0:T(8,128)(2,1)S(1)} %get-tuple-element.36), channel_id=1, source_target_pairs={{0,3},{1,2},{2,1},{3,0},{4,7},{5,6},{6,5},{7,4},{8,11},{9,10},{10,... | collective-permute-start | bytes 36872 | tf_op jit(solution)/shard_map/ppermute | solution.py:463
  21.7 10.6 %collective-permute-start.4 = (bf16[96,768]{1,0:T(8,128)(2,1)S(1)}, bf16[96,768]{1,0:T(8,128)(2,1)S(1)}, u32[]{:S(2)}, u32[]{:S(2)}) collective-permute-start(bf16[96,768]{1,0:T(8,128)(2,1)S(1)} %get-tuple-element.48), channel_id=1, source_target_pairs={{0,4},{4,0},{8,12},{12,8},{16,20},{20,16},{24,28},{28,24},{1,5},{5... | collective-permute-start | bytes 442376 | tf_op jit(solution)/shard_map/ppermute | solution.py:463
  21.8 10.6 %collective-permute-start.5 = (bf16[96,768]{1,0:T(8,128)(2,1)S(1)}, bf16[96,768]{1,0:T(8,128)(2,1)S(1)}, u32[]{:S(2)}, u32[]{:S(2)}) collective-permute-start(bf16[96,768]{1,0:T(8,128)(2,1)S(1)} %get-tuple-element.49), channel_id=1, source_target_pairs={{0,28},{4,8},{8,4},{12,16},{16,12},{20,24},{24,20},{28,0},{1,29},{... | collective-permute-start | bytes 442376 | tf_op jit(solution)/shard_map/ppermute | solution.py:463
  26.1 6.3 %slice-start.1 = ((s8[4456448]{0:T(1024)(128)(4,1)}), s8[262144]{0:T(1024)(128)(4,1)S(1)}, s32[]{:S(2)}) async-start(s8[4456448]{0:T(1024)(128)(4,1)} %bitcast.5), calls=%async_computation.1 | async-start | bytes 524288
  26.1 6.3 %copy-start.4 = (bf16[2,944,256]{2,1,0:T(8,128)(2,1)S(1)}, bf16[2,944,256]{2,1,0:T(8,128)(2,1)}, u32[]{:S(2)}) copy-start(bf16[2,944,256]{2,1,0:T(8,128)(2,1)} %constant.8.clone.mix_in) | copy-start | bytes 2899972
  26.1 6.3 %copy-start.5 = (bf16[16,32,256]{2,1,0:T(8,128)(2,1)S(1)}, bf16[16,32,256]{2,1,0:T(8,128)(2,1)}, u32[]{:S(2)}) copy-start(bf16[16,32,256]{2,1,0:T(8,128)(2,1)} %constant.7.clone.axial_in) | copy-start | bytes 786436
  26.1 6.3 %copy-start.11 = (s32[128,3]{0,1:T(4,128)S(1)}, s32[128,3]{0,1:T(4,128)}, u32[]{:S(2)}) copy-start(s32[128,3]{0,1:T(4,128)} %param.20) | copy-start | bytes 4612
  26.1 5.3 %collective-permute-start.6 = (bf16[8,768]{1,0:T(8,128)(2,1)S(1)}, bf16[8,768]{1,0:T(8,128)(2,1)S(1)}, u32[]{:S(2)}, u32[]{:S(2)}) collective-permute-start(bf16[8,768]{1,0:T(8,128)(2,1)S(1)} %get-tuple-element.50), channel_id=1, source_target_pairs={{0,1},{1,0},{2,3},{3,2},{4,5},{5,4},{6,7},{7,6},{8,9},{9,8},{10,11... | collective-permute-start | bytes 36872 | tf_op jit(solution)/shard_map/ppermute | solution.py:463
  26.9 5.5 %collective-permute-start.7 = (bf16[8,768]{1,0:T(8,128)(2,1)S(1)}, bf16[8,768]{1,0:T(8,128)(2,1)S(1)}, u32[]{:S(2)}, u32[]{:S(2)}) collective-permute-start(bf16[8,768]{1,0:T(8,128)(2,1)S(1)} %get-tuple-element.51), channel_id=1, source_target_pairs={{0,3},{1,2},{2,1},{3,0},{4,7},{5,6},{6,5},{7,4},{8,11},{9,10},{10,... | collective-permute-start | bytes 36872 | tf_op jit(solution)/shard_map/ppermute | solution.py:463
  39.9 1.3 %collective-permute-start.8 = (f32[32,256]{1,0:T(8,128)S(1)}, f32[32,256]{1,0:T(8,128)S(1)}, u32[]{:S(2)}, u32[]{:S(2)}) collective-permute-start(f32[32,256]{1,0:T(8,128)S(1)} %get-tuple-element.55), channel_id=1, source_target_pairs={{0,4},{4,0},{8,12},{12,8},{16,20},{20,16},{24,28},{28,24},{1,5},{5... | collective-permute-start | bytes 98312 | tf_op jit(solution)/shard_map/ppermute | solution.py:463
  41.2 8.9 %collective-permute-start.11 = (f32[32,256]{1,0:T(8,128)S(1)}, f32[32,256]{1,0:T(8,128)S(1)}, u32[]{:S(2)}, u32[]{:S(2)}) collective-permute-start(f32[32,256]{1,0:T(8,128)S(1)} %add.12.order), channel_id=1, source_target_pairs={{0,24},{4,28},{8,16},{12,20},{16,8},{20,12},{24,0},{28,4},{1,25},{... | collective-permute-start | bytes 98312 | tf_op jit(solution)/shard_map/ppermute | solution.py:562
  42.6 7.5 %collective-permute-start.10 = (f32[32,256]{1,0:T(8,128)S(1)}, f32[32,256]{1,0:T(8,128)S(1)}, u32[]{:S(2)}, u32[]{:S(2)}) collective-permute-start(f32[32,256]{1,0:T(8,128)S(1)} %add.12.order), channel_id=1, source_target_pairs={{0,16},{4,20},{8,24},{12,28},{16,0},{20,4},{24,8},{28,12},{1,17},{... | collective-permute-start | bytes 98312 | tf_op jit(solution)/shard_map/ppermute | solution.py:562
  44.1 6.0 %collective-permute-start.9 = (f32[32,256]{1,0:T(8,128)S(1)}, f32[32,256]{1,0:T(8,128)S(1)}, u32[]{:S(2)}, u32[]{:S(2)}) collective-permute-start(f32[32,256]{1,0:T(8,128)S(1)} %add.12.order), channel_id=1, source_target_pairs={{0,8},{4,12},{8,0},{12,4},{16,24},{20,28},{24,16},{28,20},{1,9},{5... | collective-permute-start | bytes 98312 | tf_op jit(solution)/shard_map/ppermute | solution.py:562
  (2 other events, 7.9 us)
